TPU v7x, 128 devices: a whole 4x4x4 slice. The times are simulated.
128 devices in a mesh: pair: 2 (over core), batch: 4 (over y), vocab: 16 (over x, z).
Axes of the slice: x: 4, y: 4, z: 4, core: 2. Of those that a mesh axis runs over, the one named last changes fastest.
Arguments:
- hidden: bfloat16 [2, 512, 8192], P('pair', 'batch', 'vocab'), may hold values from -120 to 120
- norm_gain: bfloat16 [8192], P('vocab'), may hold values from 0.099609375 to 1.8984375
- head_weight: bfloat16 [8192, 65536], P(('pair', 'batch'), 'vocab'), may hold values from -1 to 1
Outputs:
- guided_logprobs: float32 [512, 65536], P(('pair', 'batch'), 'vocab')
- cond_logprobs: float32 [512, 65536], P(('pair', 'batch'), 'vocab')
All inputs are finite; a program needn't handle non-finite values.
Results may differ from a plain program's by a relative error of at most 0.007.
Values may be sent and summed in bfloat16 or wider, within the bound.
A program may use at most 128 MiB of HBM per device.

v0:
```python
import jax
import jax.numpy as jnp
from jax import lax
from jax.sharding import PartitionSpec as P

D = 8192


EPS = 1e-05
GUIDE = 1.5


def on_device(hidden, norm_gain, head_weight):
    rows = hidden[0]
    wide = rows.astype(jnp.float32)
    partial_sq = jnp.sum(wide * wide, axis=1)
    total_sq = lax.psum(partial_sq, "vocab")
    scaled = wide * lax.rsqrt(total_sq / D + EPS)[:, None] * norm_gain.astype(jnp.float32)[None, :]
    features = lax.all_gather(scaled.astype(jnp.bfloat16), "vocab", axis=1, tiled=True)
    blocks = lax.all_to_all(features, ("pair", "batch"), split_axis=1, concat_axis=0, tiled=True)
    groups = lax.axis_size("pair") * lax.axis_size("batch")
    width = blocks.shape[1]
    out_rows = blocks.shape[0] // (2 * groups)
    ordered = blocks.reshape(2, groups, out_rows, width).transpose(1, 0, 2, 3).reshape(-1, width)
    logits = lax.psum_scatter(
        jnp.dot(ordered, head_weight, preferred_element_type=jnp.float32),
        ("pair", "batch"),
        scatter_dimension=0,
        tiled=True,
    )
    cond = logits[:out_rows]
    uncond = logits[out_rows:]
    guided = GUIDE * cond + (1.0 - GUIDE) * uncond
    peak_c, peak_g = lax.pmax((jnp.max(cond, axis=1), jnp.max(guided, axis=1)), "vocab")
    local_c = jnp.sum(jnp.exp(cond - peak_c[:, None]), axis=1)
    local_g = jnp.sum(jnp.exp(guided - peak_g[:, None]), axis=1)
    total_c, total_g = lax.psum((local_c, local_g), "vocab")
    cond_out = cond - (peak_c + jnp.log(total_c))[:, None]
    guided_out = guided - (peak_g + jnp.log(total_g))[:, None]
    return (guided_out, cond_out)


def solution(mesh):
    in_specs = (P("pair", "batch", "vocab"), P("vocab"), P(("pair", "batch"), "vocab"))
    out_specs = (P(("pair", "batch"), "vocab"), P(("pair", "batch"), "vocab"))
    return jax.shard_map(
        on_device, mesh=mesh, in_specs=in_specs, out_specs=out_specs, check_vma=False
    )
```

profile of v0, /device:TPU:0, one launch (start us, length us, event | category | flops | bytes accessed | tf_op | source)
XLA Modules:
  0.0 398.5 jit_solution(13088770015210042575)
XLA Ops:
  7.2 0.0 all-gather.2.cloned.1.call-start
  7.2 0.7 convert_element_type.14
  7.9 1.0 copy.6
  8.9 0.1 fusion.1
  9.0 41.8 %psum.21 = f32[128]{0:T(128)S(1)} all-reduce(f32[128]{0:T(128)S(1)} %fusion.1), channel_id=1, replica_groups=mesh['pair'=2,'batch'=4,'vocab'=16] {'vocab'}, use_global_device_ids=true, to_apply=%region_1.0 | all-reduce | flops 128 | bytes 1024 | tf_op jit(solution)/shard_map/psum | solution.py:17
  50.8 0.8 fusion.3
  51.6 0.0 all-gather.2.cloned.1.call-update
  51.6 0.0 reduce-scatter.2.cloned.1.call-start
  51.7 41.8 %all-gather.2.cloned.1.call-done = bf16[128,8192]{0,1:T(8,128)(2,1)} async-done(((bf16[128,512]{0,1:T(8,128)(2,1)}), bf16[128,8192]{0,1:T(8,128)(2,1)}) %all-gather.2.cloned.1.call-update) | async-done | bytes 2097168 | tf_op jit(solution)/shard_map/all_gather | solution.py:19
  93.5 30.9 %all_to_all.16 = bf16[128,8,1024]{0,2,1:T(8,128)(2,1)S(1)} all-to-all(bf16[128,8,1024]{0,2,1:T(8,128)(2,1)} %bitcast.14), channel_id=1, replica_groups=mesh['pair'=2,'batch'=4,'vocab'=16] {'pair','batch'}, dimensions={1} | all-to-all | bytes 4194304 | tf_op jit(solution)/shard_map/all_to_all | solution.py:20
  124.4 2.6 copy.7
  127.0 1.8 copy.8
  128.8 14.4 %fusion.5 = f32[1024,4096]{1,0:T(8,128)} fusion(bf16[1024,1024]{1,0:T(8,128)(2,1)S(1)} %bitcast.15, bf16[1024,4096]{1,0:T(8,128)(2,1)} %param.5), kind=kOutput, calls=%fused_computation.16 | convolution fusion | flops 8589934592 | bytes 27262976 | tf_op jit(solution)/shard_map/dot_general | solution.py:26
  143.2 0.0 reduce-scatter.2.cloned.1.call-update
  143.2 168.4 %reduce-scatter.2.cloned.1.call-done = f32[128,4096]{1,0:T(8,128)} async-done(((f32[1024,4096]{1,0:T(8,128)}), f32[128,4096]{1,0:T(8,128)}) %reduce-scatter.2.cloned.1.call-update) | async-done | bytes 2097168 | tf_op jit(solution)/shard_map/reduce_scatter | solution.py:25
  311.6 0.0 copy-start
  311.6 2.0 slice_reduce_fusion
  313.5 40.5 %all-reduce.1 = (f32[64]{0:T(128)S(1)}, f32[64]{0:T(128)S(1)}) all-reduce(f32[64]{0:T(128)S(1)} %get-tuple-element.5, f32[64]{0:T(128)S(1)} %get-tuple-element.4), channel_id=1, replica_groups=mesh['pair'=2,'batch'=4,'vocab'=16] {'vocab'}, use_global_device_ids=true, to_apply=%region_4.0 | all-reduce | flops 128 | bytes 1024 | tf_op jit(solution)/shard_map/pmax | solution.py:34
  354.1 0.0 copy-done
  354.1 0.5 exponential_reduce_fusion
  354.6 35.5 %all-reduce = (f32[64]{0:T(128)S(1)}, f32[64]{0:T(128)S(1)}) all-reduce(f32[64]{0:T(128)S(1)} %get-tuple-element.3, f32[64]{0:T(128)S(1)} %get-tuple-element.2), channel_id=1, replica_groups=mesh['pair'=2,'batch'=4,'vocab'=16] {'vocab'}, use_global_device_ids=true, to_apply=%region_6.0 | all-reduce | flops 128 | bytes 1024 | tf_op jit(solution)/shard_map/psum | solution.py:37
  390.1 1.6 slice_subtract_fusion
  (2 shorter events, 0.0 us)
Async XLA Ops:
  7.2 86.3 %all-gather.2.cloned.1.call-start = ((), (), s32[]{:S(2)}) async-start(), calls=%async_computation.2 | async-start | bytes 2228224 | tf_op jit(solution)/shard_map/all_gather | solution.py:19
  51.6 260.0 %reduce-scatter.2.cloned.1.call-start = ((), (), s32[]{:S(2)}) async-start(), calls=%async_computation.3 | async-start | bytes 18874368 | tf_op jit(solution)/shard_map/reduce_scatter | solution.py:25
  311.6 42.5 %copy-start = (f32[128,4096]{1,0:T(8,128)S(1)}, f32[128,4096]{1,0:T(8,128)}, u32[]{:S(2)}) copy-start(f32[128,4096]{1,0:T(8,128)} %reduce-scatter.2.cloned.1.call-done) | copy-start | bytes 6291460
Sparse Core Ops, SparseCore 0:
  51.7 41.6 all-gather.1
  143.3 168.2 reduce-scatter.1
where the time goes:
time: 399 us
  waiting for transfers between devices  210 us (53%)
  blocking collectives  149 us (37%)
  matrix products  14.4 us (4%)
  between operations  14.1 us (4%)
  other arithmetic  5.68 us (1%)
  local copies, waits for them, and re-layouts  5.44 us (1%)
    reduce_scatter x1, waiting for transfers between devices, on_device(): lax.psum_scatter(jnp.dot(ordered, head_weight, preferred_element_type=jnp...  168 us
    all_gather x1, waiting for transfers between devices, on_device(): lax.all_gather(scaled.astype(jnp.bfloat16), 'vocab', axis=1, tiled=True)  41.8 us
    psum x1, blocking collectives, on_device(): total_sq = lax.psum(partial_sq, 'vocab')  41.8 us
    pmax x1, blocking collectives, on_device(): lax.pmax((jnp.max(cond, axis=1), jnp.max(guided, axis=1)), 'vocab')  40.5 us
    psum x1, blocking collectives, on_device(): total_c, total_g = lax.psum((local_c, local_g), 'vocab')  35.5 us
    all_to_all x1, blocking collectives, on_device(): lax.all_to_all(features, ('pair', 'batch'), split_axis=1, concat_axis=0,...  30.9 us
    dot_general x1, matrix products, on_device(): jnp.dot(ordered, head_weight, preferred_element_type=jnp.float32)  14.4 us
  transfers between devices with their start and end apart: 2, of which 2 were waited for; matrix products, arithmetic and copies ran while one was open for 0% of the time, Pallas kernels for 0%

commit v1 on v0

--- a/solution.py
+++ b/solution.py
@@ -11,12 +11,12 @@
 
 
 def on_device(hidden, norm_gain, head_weight):
-    rows = hidden[0]
+    rows = lax.all_gather(hidden[0], "vocab", axis=1, tiled=True)
+    gain = lax.all_gather(norm_gain, "vocab", axis=0, tiled=True)
     wide = rows.astype(jnp.float32)
-    partial_sq = jnp.sum(wide * wide, axis=1)
-    total_sq = lax.psum(partial_sq, "vocab")
-    scaled = wide * lax.rsqrt(total_sq / D + EPS)[:, None] * norm_gain.astype(jnp.float32)[None, :]
-    features = lax.all_gather(scaled.astype(jnp.bfloat16), "vocab", axis=1, tiled=True)
+    total_sq = jnp.sum(wide * wide, axis=1)
+    scaled = wide * lax.rsqrt(total_sq / D + EPS)[:, None] * gain.astype(jnp.float32)[None, :]
+    features = scaled.astype(jnp.bfloat16)
     blocks = lax.all_to_all(features, ("pair", "batch"), split_axis=1, concat_axis=0, tiled=True)
     groups = lax.axis_size("pair") * lax.axis_size("batch")
     width = blocks.shape[1]
@@ -31,12 +31,18 @@
     cond = logits[:out_rows]
     uncond = logits[out_rows:]
     guided = GUIDE * cond + (1.0 - GUIDE) * uncond
-    peak_c, peak_g = lax.pmax((jnp.max(cond, axis=1), jnp.max(guided, axis=1)), "vocab")
+    peak_c = jnp.max(cond, axis=1)
+    peak_g = jnp.max(guided, axis=1)
     local_c = jnp.sum(jnp.exp(cond - peak_c[:, None]), axis=1)
     local_g = jnp.sum(jnp.exp(guided - peak_g[:, None]), axis=1)
-    total_c, total_g = lax.psum((local_c, local_g), "vocab")
-    cond_out = cond - (peak_c + jnp.log(total_c))[:, None]
-    guided_out = guided - (peak_g + jnp.log(total_g))[:, None]
+    stats = jnp.stack([peak_c, local_c, peak_g, local_g])
+    every = lax.all_gather(stats, "vocab", axis=0)
+    top_c = jnp.max(every[:, 0], axis=0)
+    top_g = jnp.max(every[:, 2], axis=0)
+    total_c = jnp.sum(every[:, 1] * jnp.exp(every[:, 0] - top_c[None, :]), axis=0)
+    total_g = jnp.sum(every[:, 3] * jnp.exp(every[:, 2] - top_g[None, :]), axis=0)
+    cond_out = cond - (top_c + jnp.log(total_c))[:, None]
+    guided_out = guided - (top_g + jnp.log(total_g))[:, None]
     return (guided_out, cond_out)
 
 

time: 399 us -> 318 us (0.80)
  blocking collectives: 149 us -> 78.9 us
  waiting for transfers between devices: 210 us -> 193 us
  other arithmetic: 5.68 us -> 10.6 us
    psum x2 -> x0, blocking collectives: 77.2 us -> none  [the longest x1 41.8 us: on_device(): total_sq = lax.psum(partial_sq, 'vocab')]
    all_gather x0 -> x2, blocking collectives: none -> 48.2 us  [the longest x1 24.7 us: on_device(): gain = lax.all_gather(norm_gain, 'vocab', axis=0, tiled=True)]
    pmax x1 -> x0, blocking collectives: 40.5 us -> none  [on_device(): lax.pmax((jnp.max(cond, axis=1), jnp.max(guided, axis=1)), 'vocab')]
    all_gather x1, waiting for transfers between devices: 41.8 us -> 24.1 us  [on_device(): rows = lax.all_gather(hidden[0], 'vocab', axis=1, tiled=True)]
where the time goes in v1:
time: 318 us
  waiting for transfers between devices  193 us (61%)
  blocking collectives  78.9 us (25%)
  matrix products  14.4 us (5%)
  between operations  14.1 us (4%)
  other arithmetic  10.6 us (3%)
  local copies, waits for them, and re-layouts  7.03 us (2%)
    reduce_scatter x1, waiting for transfers between devices, on_device(): lax.psum_scatter(jnp.dot(ordered, head_weight, preferred_element_type=jnp...  168 us
    all_to_all x1, blocking collectives, on_device(): lax.all_to_all(features, ('pair', 'batch'), split_axis=1, concat_axis=0,...  30.7 us
    all_gather x1, blocking collectives, on_device(): gain = lax.all_gather(norm_gain, 'vocab', axis=0, tiled=True)  24.7 us
    all_gather x1, waiting for transfers between devices, on_device(): rows = lax.all_gather(hidden[0], 'vocab', axis=1, tiled=True)  24.1 us
    all_gather x1, blocking collectives, on_device(): every = lax.all_gather(stats, 'vocab', axis=0)  23.5 us
    dot_general x1, matrix products, on_device(): jnp.dot(ordered, head_weight, preferred_element_type=jnp.float32)  14.4 us
  transfers between devices with their start and end apart: 2, of which 2 were waited for; matrix products, arithmetic and copies ran while one was open for 0% of the time, Pallas kernels for 0%

profile of v1, /device:TPU:0, one launch (start us, length us, event | category | flops | bytes accessed | tf_op | source)
XLA Modules:
  0.0 317.6 jit_solution(5014193301131208361)
XLA Ops:
  7.2 0.0 all-gather.6.cloned.1.call-start
  7.2 1.7 copy.15
  8.9 0.0 all-gather.6.cloned.1.call-update
  8.9 0.0 reduce-scatter.2.cloned.1.call-start
  8.9 0.7 reshape.41
  9.6 24.7 %all-gather.2 = bf16[16,1,512]{2,1,0:T(2,128)(2,1)S(1)} all-gather(bf16[1,1,512]{2,1,0:T(2,128)(2,1)S(1)} %reshape.41), channel_id=1, replica_groups=mesh['pair'=2,'batch'=4,'vocab'=16] {'vocab'}, dimensions={0}, use_global_device_ids=true | all-gather | bytes 17408 | tf_op jit(solution)/shard_map/all_gather | solution.py:15
  34.4 24.1 %all-gather.6.cloned.1.call-done = bf16[1,128,8192]{1,2,0:T(8,128)(2,1)} async-done(((bf16[1,128,512]{1,2,0:T(8,128)(2,1)}), bf16[1,128,8192]{1,2,0:T(8,128)(2,1)}) %all-gather.6.cloned.1.call-update) | async-done | bytes 2097168 | tf_op jit(solution)/shard_map/all_gather | solution.py:14
  58.5 0.0 copy-start.1
  58.5 2.8 fusion
  61.3 0.0 copy-done.1
  61.3 3.5 %fusion.2 = bf16[128,8192]{0,1:T(8,128)(2,1)S(1)} fusion(bf16[1,128,8192]{1,2,0:T(8,128)(2,1)S(1)} %copy-done.1, f32[8192]{0:T(1024)S(1)} %bitcast.31, f32[128]{0:T(128)S(1)} %add_rsqrt_fusion), kind=kLoop, calls=%fused_computation.4 | loop fusion | flops 4194304 | bytes 4227584 | tf_op jit(solution)/shard_map/convert_element_type | solution.py:19
  64.8 30.7 %all_to_all.16 = bf16[128,8,1024]{0,2,1:T(8,128)(2,1)S(1)} all-to-all(bf16[128,8,1024]{0,2,1:T(8,128)(2,1)S(1)} %bitcast.27), channel_id=1, replica_groups=mesh['pair'=2,'batch'=4,'vocab'=16] {'pair','batch'}, dimensions={1} | all-to-all | bytes 4194304 | tf_op jit(solution)/shard_map/all_to_all | solution.py:20
  95.5 2.6 copy.16
  98.1 1.8 copy.17
  99.9 14.4 %fusion.6 = f32[1024,4096]{1,0:T(8,128)} fusion(bf16[1024,1024]{1,0:T(8,128)(2,1)S(1)} %bitcast.30, bf16[1024,4096]{1,0:T(8,128)(2,1)} %param.5), kind=kOutput, calls=%fused_computation.21 | convolution fusion | flops 8589934592 | bytes 27262976 | tf_op jit(solution)/shard_map/dot_general | solution.py:26
  114.3 0.0 reduce-scatter.2.cloned.1.call-update
  114.3 168.4 %reduce-scatter.2.cloned.1.call-done = f32[128,4096]{1,0:T(8,128)} async-done(((f32[1024,4096]{1,0:T(8,128)}), f32[128,4096]{1,0:T(8,128)}) %reduce-scatter.2.cloned.1.call-update) | async-done | bytes 2097168 | tf_op jit(solution)/shard_map/reduce_scatter | solution.py:25
  282.7 0.0 copy-start
  282.7 2.0 slice_reduce_fusion
  284.7 0.3 copy-done
  284.9 0.5 exponential_reduce_fusion.1
  285.5 23.5 %all-gather.3 = f32[16,4,64]{2,1,0:T(4,128)S(1)} all-gather(f32[1,4,64]{2,1,0:T(4,128)S(1)} %maximum_bitcast_fusion), channel_id=3, replica_groups=mesh['pair'=2,'batch'=4,'vocab'=16] {'vocab'}, dimensions={0}, use_global_device_ids=true | all-gather | bytes 17408 | tf_op jit(solution)/shard_map/all_gather | solution.py:39
  309.1 1.6 slice_subtract_fusion
  (8 shorter events, 0.2 us)
Async XLA Ops:
  7.2 51.3 %all-gather.6.cloned.1.call-start = ((), (), s32[]{:S(2)}) async-start(), calls=%async_computation.3 | async-start | bytes 2228224 | tf_op jit(solution)/shard_map/all_gather | solution.py:14
  8.9 273.8 %reduce-scatter.2.cloned.1.call-start = ((), (), s32[]{:S(2)}) async-start(), calls=%async_computation.2 | async-start | bytes 18874368 | tf_op jit(solution)/shard_map/reduce_scatter | solution.py:25
  58.5 2.8 copy-start.1
  282.7 2.2 copy-start
Sparse Core Ops, SparseCore 0:
  10.7 47.7 all-gather.5
  114.5 168.2 reduce-scatter.1

commit v2 on v1

--- a/solution.py
+++ b/solution.py
@@ -11,9 +11,11 @@
 
 
 def on_device(hidden, norm_gain, head_weight):
-    rows = lax.all_gather(hidden[0], "vocab", axis=1, tiled=True)
-    gain = lax.all_gather(norm_gain, "vocab", axis=0, tiled=True)
-    wide = rows.astype(jnp.float32)
+    local_rows = hidden.shape[1]
+    packed = jnp.concatenate([hidden[0], norm_gain[None, :]], axis=0)
+    gathered = lax.all_gather(packed, "vocab", axis=1, tiled=True)
+    wide = gathered[:local_rows].astype(jnp.float32)
+    gain = gathered[local_rows]
     total_sq = jnp.sum(wide * wide, axis=1)
     scaled = wide * lax.rsqrt(total_sq / D + EPS)[:, None] * gain.astype(jnp.float32)[None, :]
     features = scaled.astype(jnp.bfloat16)
@@ -22,12 +24,9 @@
     width = blocks.shape[1]
     out_rows = blocks.shape[0] // (2 * groups)
     ordered = blocks.reshape(2, groups, out_rows, width).transpose(1, 0, 2, 3).reshape(-1, width)
-    logits = lax.psum_scatter(
-        jnp.dot(ordered, head_weight, preferred_element_type=jnp.float32),
-        ("pair", "batch"),
-        scatter_dimension=0,
-        tiled=True,
-    )
+    partial = jnp.dot(ordered, head_weight, preferred_element_type=jnp.float32)
+    half = lax.psum_scatter(partial, "pair", scatter_dimension=0, tiled=True)
+    logits = lax.psum_scatter(half, "batch", scatter_dimension=0, tiled=True)
     cond = logits[:out_rows]
     uncond = logits[out_rows:]
     guided = GUIDE * cond + (1.0 - GUIDE) * uncond

time: 318 us -> 271 us (0.85)
  waiting for transfers between devices: 193 us -> 167 us
  blocking collectives: 78.9 us -> 54.2 us
  other arithmetic: 10.6 us -> 15.1 us
    reduce_scatter x1 -> x2, waiting for transfers between devices: 168 us -> 112 us  [the longest x1 84.5 us: on_device(): logits = lax.psum_scatter(half, 'batch', scatter_dimension=0, tiled=True)]
    all_gather x1, waiting for transfers between devices: 24.1 us -> 55 us  [on_device(): gathered = lax.all_gather(packed, 'vocab', axis=1, tiled=True)]
    all_gather x1 -> x0, blocking collectives: 24.7 us -> none  [on_device(): gain = lax.all_gather(norm_gain, 'vocab', axis=0, tiled=True)]
  transfers between devices with their start and end apart: 2 -> 3, of which waited for: 2 -> 3; matrix products, arithmetic and copies ran while one was open for 0% -> 0% of each run, Pallas kernels for 0% -> 0%
where the time goes in v2:
time: 271 us
  waiting for transfers between devices  167 us (62%)
  blocking collectives  54.2 us (20%)
  other arithmetic  15.1 us (6%)
  matrix products  14.4 us (5%)
  between operations  13.8 us (5%)
  local copies, waits for them, and re-layouts  6.25 us (2%)
    reduce_scatter x1, waiting for transfers between devices, on_device(): logits = lax.psum_scatter(half, 'batch', scatter_dimension=0, tiled=True)  84.5 us
    all_gather x1, waiting for transfers between devices, on_device(): gathered = lax.all_gather(packed, 'vocab', axis=1, tiled=True)  55 us
    all_to_all x1, blocking collectives, on_device(): lax.all_to_all(features, ('pair', 'batch'), split_axis=1, concat_axis=0,...  30.7 us
    reduce_scatter x1, waiting for transfers between devices, on_device(): half = lax.psum_scatter(partial, 'pair', scatter_dimension=0, tiled=True)  27.5 us
    all_gather x1, blocking collectives, on_device(): every = lax.all_gather(stats, 'vocab', axis=0)  23.5 us
    dot_general x1, matrix products, on_device(): partial = jnp.dot(ordered, head_weight, preferred_element_type=jnp.float32)  14.4 us
  transfers between devices with their start and end apart: 3, of which 3 were waited for; matrix products, arithmetic and copies ran while one was open for 0% of the time, Pallas kernels for 0%

profile of v2, /device:TPU:0, one launch (start us, length us, event | category | flops | bytes accessed | tf_op | source)
XLA Modules:
  0.0 270.9 jit_solution(1549752590738809804)
XLA Ops:
  7.2 0.0 all-gather.4.cloned.1.call-start
  7.2 1.0 copy.21
  8.2 0.8 broadcast_in_dim.3
  9.1 0.8 pad_maximum_fusion
  9.8 0.0 all-gather.4.cloned.1.call-update
  9.8 0.0 reduce-scatter.3.cloned.1.call-start
  9.9 55.0 %all-gather.4.cloned.1.call-done = bf16[129,8192]{0,1:T(8,128)(2,1)} async-done(((bf16[129,512]{0,1:T(8,128)(2,1)}), bf16[129,8192]{0,1:T(8,128)(2,1)}) %all-gather.4.cloned.1.call-update) | async-done | bytes 2113552 | tf_op jit(solution)/shard_map/all_gather | solution.py:16
  64.9 2.8 %fusion = f32[128]{0:T(128)S(1)} fusion(bf16[129,8192]{0,1:T(8,128)(2,1)} %all-gather.4.cloned.1.call-done), kind=kLoop, calls=%fused_computation.2 | loop fusion | flops 3145600 | bytes 2097664 | tf_op jit(solution)/shard_map/reduce_sum | solution.py:19
  67.7 2.2 convert_reduce_fusion
  70.0 0.0 copy-done.1
  70.0 3.5 %fusion.2 = bf16[128,8192]{0,1:T(8,128)(2,1)S(1)} fusion(f32[8192]{0:T(1024)S(1)} %convert_reduce_fusion, f32[128]{0:T(128)S(1)} %add_rsqrt_fusion, bf16[129,8192]{0,1:T(8,128)(2,1)S(1)} %copy-done.1), kind=kLoop, calls=%fused_computation.4 | loop fusion | flops 4194304 | bytes 4227584 | tf_op jit(solution)/shard_map/convert_element_type | solution.py:21
  73.5 30.7 %all_to_all.16 = bf16[128,8,1024]{0,2,1:T(8,128)(2,1)S(1)} all-to-all(bf16[128,8,1024]{0,2,1:T(8,128)(2,1)S(1)} %bitcast.23), channel_id=1, replica_groups=mesh['pair'=2,'batch'=4,'vocab'=16] {'pair','batch'}, dimensions={1} | all-to-all | bytes 4194304 | tf_op jit(solution)/shard_map/all_to_all | solution.py:22
  104.1 2.6 copy.23
  106.7 1.8 copy.24
  108.5 14.4 %fusion.6 = f32[1024,4096]{1,0:T(8,128)} fusion(bf16[1024,1024]{1,0:T(8,128)(2,1)S(1)} %bitcast.26, bf16[1024,4096]{1,0:T(8,128)(2,1)} %param.5), kind=kOutput, calls=%fused_computation.23 | convolution fusion | flops 8589934592 | bytes 27262976 | tf_op jit(solution)/shard_map/dot_general | solution.py:27
  123.0 0.0 reduce-scatter.3.cloned.1.call-update
  123.0 0.0 reduce-scatter.5.cloned.1.call-start
  123.0 27.5 %reduce-scatter.3.cloned.1.call-done = f32[512,4096]{1,0:T(8,128)} async-done(((f32[1024,4096]{1,0:T(8,128)}), f32[512,4096]{1,0:T(8,128)}) %reduce-scatter.3.cloned.1.call-update) | async-done | bytes 8388624 | tf_op jit(solution)/shard_map/reduce_scatter | solution.py:28
  150.5 0.0 reduce-scatter.5.cloned.1.call-update
  150.5 84.5 %reduce-scatter.5.cloned.1.call-done = f32[128,4096]{1,0:T(8,128)} async-done(((f32[512,4096]{1,0:T(8,128)}), f32[128,4096]{1,0:T(8,128)}) %reduce-scatter.5.cloned.1.call-update) | async-done | bytes 2097168 | tf_op jit(solution)/shard_map/reduce_scatter | solution.py:29
  235.0 2.0 slice_reduce_fusion
  237.0 2.1 exponential_reduce_fusion.1
  239.1 23.5 %all-gather.1 = f32[16,4,64]{2,1,0:T(4,128)S(1)} all-gather(f32[1,4,64]{2,1,0:T(4,128)S(1)} %maximum_bitcast_fusion), channel_id=2, replica_groups=mesh['pair'=2,'batch'=4,'vocab'=16] {'vocab'}, dimensions={0}, use_global_device_ids=true | all-gather | bytes 17408 | tf_op jit(solution)/shard_map/all_gather | solution.py:38
  262.7 1.6 slice_subtract_fusion
  (10 shorter events, 0.1 us)
Async XLA Ops:
  7.2 57.7 %all-gather.4.cloned.1.call-start = ((), (), s32[]{:S(2)}) async-start(), calls=%async_computation.3 | async-start | bytes 4456448 | tf_op jit(solution)/shard_map/all_gather | solution.py:16
  9.8 140.7 %reduce-scatter.3.cloned.1.call-start = ((), (), s32[]{:S(2)}) async-start(), calls=%async_computation.4 | async-start | bytes 25165824 | tf_op jit(solution)/shard_map/reduce_scatter | solution.py:28
  64.9 5.1 %copy-start.1 = (bf16[129,8192]{0,1:T(8,128)(2,1)S(1)}, bf16[129,8192]{0,1:T(8,128)(2,1)}, u32[]{:S(2)}) copy-start(bf16[129,8192]{0,1:T(8,128)(2,1)} %all-gather.4.cloned.1.call-done) | copy-start | bytes 6340612
  123.0 112.1 %reduce-scatter.5.cloned.1.call-start = ((), (), s32[]{:S(2)}) async-start(), calls=%async_computation.5 | async-start | bytes 10485760 | tf_op jit(solution)/shard_map/reduce_scatter | solution.py:29
  235.0 27.7 %copy-start = (f32[128,4096]{1,0:T(8,128)S(1)}, f32[128,4096]{1,0:T(8,128)}, u32[]{:S(2)}) copy-start(f32[128,4096]{1,0:T(8,128)} %reduce-scatter.5.cloned.1.call-done) | copy-start | bytes 6291460
Sparse Core Ops, SparseCore 0:
  10.7 54.1 all-gather.3
  123.1 27.3 reduce-scatter.2
  153.1 81.8 reduce-scatter.4

commit v3 on v2

--- a/solution.py
+++ b/solution.py
@@ -8,11 +8,13 @@
 
 EPS = 1e-05
 GUIDE = 1.5
+CHUNKS = 2
 
 
 def on_device(hidden, norm_gain, head_weight):
     local_rows = hidden.shape[1]
-    packed = jnp.concatenate([hidden[0], norm_gain[None, :]], axis=0)
+    pad = jnp.zeros((15, norm_gain.shape[0]), hidden.dtype)
+    packed = jnp.concatenate([hidden[0], norm_gain[None, :], pad], axis=0)
     gathered = lax.all_gather(packed, "vocab", axis=1, tiled=True)
     wide = gathered[:local_rows].astype(jnp.float32)
     gain = gathered[local_rows]
@@ -24,9 +26,20 @@
     width = blocks.shape[1]
     out_rows = blocks.shape[0] // (2 * groups)
     ordered = blocks.reshape(2, groups, out_rows, width).transpose(1, 0, 2, 3).reshape(-1, width)
-    partial = jnp.dot(ordered, head_weight, preferred_element_type=jnp.float32)
-    half = lax.psum_scatter(partial, "pair", scatter_dimension=0, tiled=True)
-    logits = lax.psum_scatter(half, "batch", scatter_dimension=0, tiled=True)
+    half_rows = ordered.shape[0] // 2
+    me = lax.axis_index("pair")
+    mine = lax.dynamic_slice_in_dim(ordered, me * half_rows, half_rows, axis=0)
+    theirs = lax.dynamic_slice_in_dim(ordered, (1 - me) * half_rows, half_rows, axis=0)
+    cols = head_weight.shape[1]
+    step = cols // CHUNKS
+    pieces = []
+    for j in range(CHUNKS):
+        w = head_weight[:, j * step:(j + 1) * step]
+        sent = jnp.dot(theirs, w, preferred_element_type=jnp.float32)
+        got = lax.ppermute(sent, "pair", [(0, 1), (1, 0)])
+        kept = jnp.dot(mine, w, preferred_element_type=jnp.float32)
+        pieces.append(lax.psum_scatter(kept + got, "batch", scatter_dimension=0, tiled=True))
+    logits = jnp.concatenate(pieces, axis=1)
     cond = logits[:out_rows]
     uncond = logits[out_rows:]
     guided = GUIDE * cond + (1.0 - GUIDE) * uncond

time: 271 us -> 260 us (0.959)
  blocking collectives: 54.2 us -> 23.5 us
  matrix products: 14.4 us -> 25.2 us
  starting transfers between devices: 0.12 us -> 4.96 us
  waiting for transfers between devices: 167 us -> 170 us
    reduce_scatter x2, waiting for transfers between devices: 112 us -> 74.6 us  [on_device(): lax.psum_scatter(kept + got, 'batch', scatter_dimension=0, tiled=True)]
    all_to_all x1 -> x0, blocking collectives: 30.7 us -> none  [on_device(): lax.all_to_all(features, ('pair', 'batch'), split_axis=1, concat_axis=0,...]
    all_to_all x0 -> x1, waiting for transfers between devices: none -> 26.5 us  [on_device(): lax.all_to_all(features, ('pair', 'batch'), split_axis=1, concat_axis=0,...]
    ppermute x0 -> x2, waiting for transfers between devices: none -> 14.4 us  [on_device(): got = lax.ppermute(sent, 'pair', [(0, 1), (1, 0)])]
    dot_general x1 -> x4, matrix products: 14.4 us -> 25.2 us  [the longest x2 14.2 us: on_device(): kept = jnp.dot(mine, w, preferred_element_type=jnp.float32)]
    all_to_all x0 -> x1, starting transfers between devices: none -> 4.29 us  [on_device(): lax.all_to_all(features, ('pair', 'batch'), split_axis=1, concat_axis=0,...]
  transfers between devices with their start and end apart: 3 -> 6, of which waited for: 3 -> 6; matrix products, arithmetic and copies ran while one was open for 0% -> 5% of each run, Pallas kernels for 0% -> 0%
where the time goes in v3:
time: 260 us
  waiting for transfers between devices  170 us (65%)
  matrix products  25.2 us (10%)
  blocking collectives  23.5 us (9%)
  between operations  13.8 us (5%)
  other arithmetic  12.8 us (5%)
  local copies, waits for them, and re-layouts  8.95 us (3%)
  starting transfers between devices  4.96 us (2%)
    reduce_scatter x2, waiting for transfers between devices, on_device(): lax.psum_scatter(kept + got, 'batch', scatter_dimension=0, tiled=True)  74.6 us
    all_gather x1, waiting for transfers between devices, on_device(): gathered = lax.all_gather(packed, 'vocab', axis=1, tiled=True)  54.9 us
    all_to_all x1, waiting for transfers between devices, on_device(): lax.all_to_all(features, ('pair', 'batch'), split_axis=1, concat_axis=0,...  26.5 us
    all_gather x1, blocking collectives, on_device(): every = lax.all_gather(stats, 'vocab', axis=0)  23.5 us
    ppermute x2, waiting for transfers between devices, on_device(): got = lax.ppermute(sent, 'pair', [(0, 1), (1, 0)])  14.4 us
    dot_general x2, matrix products, on_device(): kept = jnp.dot(mine, w, preferred_element_type=jnp.float32)  14.2 us
    dot_general x2, matrix products, on_device(): sent = jnp.dot(theirs, w, preferred_element_type=jnp.float32)  11 us
  transfers between devices with their start and end apart: 6, of which 6 were waited for; matrix products, arithmetic and copies ran while one was open for 5% of the time, Pallas kernels for 0%

profile of v3, /device:TPU:0, one launch (start us, length us, event | category | flops | bytes accessed | tf_op | source)
XLA Modules:
  0.0 259.7 jit_solution(1291108250158917924)
XLA Ops:
  7.2 1.0 copy.21
  8.2 0.8 broadcast_in_dim.6
  9.1 0.8 maximum_maximum_fusion
  9.9 54.9 %all-gather.4.cloned.1.call-done = bf16[144,8192]{0,1:T(8,128)(2,1)} async-done(((bf16[144,512]{0,1:T(8,128)(2,1)}), bf16[144,8192]{0,1:T(8,128)(2,1)}) %all-gather.4.cloned.1.call-update) | async-done | bytes 2359312 | tf_op jit(solution)/shard_map/all_gather | solution.py:18
  64.9 2.8 %fusion = f32[128]{0:T(128)S(1)} fusion(bf16[144,8192]{0,1:T(8,128)(2,1)} %all-gather.4.cloned.1.call-done), kind=kLoop, calls=%fused_computation.2 | loop fusion | flops 3145600 | bytes 2097664 | tf_op jit(solution)/shard_map/reduce_sum | solution.py:21
  67.7 2.2 convert_reduce_fusion
  70.0 4.4 %fusion.2 = bf16[128,8192]{0,1:T(8,128)(2,1)} fusion(f32[8192]{0:T(1024)S(1)} %convert_reduce_fusion, f32[128]{0:T(128)S(1)} %add_rsqrt_fusion, bf16[144,8192]{0,1:T(8,128)(2,1)S(1)} %copy-done), kind=kLoop, calls=%fused_computation.4 | loop fusion | flops 4194304 | bytes 4227584 | tf_op jit(solution)/shard_map/convert_element_type | solution.py:23
  74.4 4.3 %all-to-all-start = ((bf16[128,8,1024]{0,2,1:T(8,128)(2,1)}), bf16[128,8,1024]{0,2,1:T(8,128)(2,1)S(1)}, u32[]{:S(2)}, u32[]{:S(2)}) async-start(bf16[128,8,1024]{0,2,1:T(8,128)(2,1)} %bitcast.22), calls=%async_computation | async-start | bytes 4194304 | tf_op jit(solution)/shard_map/all_to_all | solution.py:24
  78.7 26.5 %all-to-all-done = bf16[128,8,1024]{0,2,1:T(8,128)(2,1)S(1)} async-done(((bf16[128,8,1024]{0,2,1:T(8,128)(2,1)}), bf16[128,8,1024]{0,2,1:T(8,128)(2,1)S(1)}, u32[]{:S(2)}, u32[]{:S(2)}) %all-to-all-start) | async-done | bytes 2097184 | tf_op jit(solution)/shard_map/all_to_all | solution.py:24
  105.2 2.6 %copy.23 = bf16[8,128,1024]{2,1,0:T(8,128)(2,1)} copy(bf16[8,128,1024]{1,2,0:T(8,128)(2,1)S(1)} %bitcast.21) | data formatting | bytes 4194304 | tf_op jit(solution)/shard_map/all_to_all | solution.py:24
  107.8 1.8 copy.24
  109.7 6.5 %fusion.7 = f32[512,2048]{1,0:T(8,128)} fusion(bf16[1024,4096]{1,0:T(8,128)(2,1)} %param.5, bf16[1024,1024]{1,0:T(8,128)(2,1)S(1)} %bitcast.24, s32[]{:T(128)S(6)} %select_n.7), kind=kOutput, calls=%fused_computation.10 | convolution fusion | flops 2147483648 | bytes 9437188 | tf_op jit(solution)/shard_map/dot_general | solution.py:38
  116.3 7.4 %collective-permute-done = f32[512,2048]{1,0:T(8,128)} collective-permute-done((f32[512,2048]{1,0:T(8,128)}, f32[512,2048]{1,0:T(8,128)}, u32[]{:S(2)}, u32[]{:S(2)}) %collective-permute-start) | collective-permute-done | bytes 4194336 | tf_op jit(solution)/shard_map/ppermute | solution.py:39
  123.6 7.7 %fusion.11 = f32[512,2048]{1,0:T(8,128)} fusion(f32[512,2048]{1,0:T(8,128)} %collective-permute-done, bf16[1024,4096]{1,0:T(8,128)(2,1)} %param.5, bf16[1024,1024]{1,0:T(8,128)(2,1)S(1)} %bitcast.25, s32[]{:T(128)S(6)} %select_n.6), kind=kOutput, calls=%fused_computation.14 | convolution fusion | flops 2148532224 | bytes 13631492 | tf_op jit(solution)/shard_map/dot_general | solution.py:40
  131.4 4.5 %fusion.3 = f32[512,2048]{1,0:T(8,128)S(1)} fusion(bf16[1024,4096]{1,0:T(8,128)(2,1)} %param.5, bf16[1024,1024]{1,0:T(8,128)(2,1)S(1)} %bitcast.26, s32[]{:T(128)S(6)} %select_n.7), kind=kOutput, calls=%fused_computation.6 | convolution fusion | flops 2147483648 | bytes 9437188 | tf_op jit(solution)/shard_map/dot_general | solution.py:38
  136.4 7.0 %collective-permute-done.1 = f32[512,2048]{1,0:T(8,128)S(1)} collective-permute-done((f32[512,2048]{1,0:T(8,128)S(1)}, f32[512,2048]{1,0:T(8,128)S(1)}, u32[]{:S(2)}, u32[]{:S(2)}) %collective-permute-start.1) | collective-permute-done | bytes 4194336 | tf_op jit(solution)/shard_map/ppermute | solution.py:39
  143.4 6.5 %fusion.14 = f32[512,2048]{1,0:T(8,128)} fusion(f32[512,2048]{1,0:T(8,128)S(1)} %collective-permute-done.1, bf16[1024,4096]{1,0:T(8,128)(2,1)} %param.5, bf16[1024,1024]{1,0:T(8,128)(2,1)S(1)} %bitcast.27, s32[]{:T(128)S(6)} %select_n.6), kind=kOutput, calls=%fused_computation.15 | convolution fusion | flops 2148532224 | bytes 13631492 | tf_op jit(solution)/shard_map/dot_general | solution.py:40
  149.9 26.8 %reduce-scatter.3.cloned.1.call-done = f32[128,2048]{1,0:T(8,128)} async-done(((f32[512,2048]{1,0:T(8,128)}), f32[128,2048]{1,0:T(8,128)}) %reduce-scatter.3.cloned.1.call-update) | async-done | bytes 1048592 | tf_op jit(solution)/shard_map/reduce_scatter | solution.py:41
  176.7 1.3 constant_dynamic-update-slice_fusion.1
  178.0 47.8 %reduce-scatter.5.cloned.1.call-done = f32[128,2048]{1,0:T(8,128)} async-done(((f32[512,2048]{1,0:T(8,128)}), f32[128,2048]{1,0:T(8,128)}) %reduce-scatter.5.cloned.1.call-update) | async-done | bytes 1048592 | tf_op jit(solution)/shard_map/reduce_scatter | solution.py:41
  225.8 1.3 constant_dynamic-update-slice_fusion
  227.4 0.5 exponential_reduce_fusion.1
  228.0 23.5 %all-gather.1 = f32[16,4,64]{2,1,0:T(4,128)S(1)} all-gather(f32[1,4,64]{2,1,0:T(4,128)S(1)} %maximum_bitcast_fusion), channel_id=2, replica_groups=mesh['pair'=2,'batch'=4,'vocab'=16] {'vocab'}, dimensions={0}, use_global_device_ids=true | all-gather | bytes 17408 | tf_op jit(solution)/shard_map/all_gather | solution.py:51
  251.6 1.6 slice_subtract_fusion
  (20 shorter events, 1.2 us)
Async XLA Ops:
  7.2 57.7 %all-gather.4.cloned.1.call-start = ((), (), s32[]{:S(2)}) async-start(), calls=%async_computation.3 | async-start | bytes 4456448 | tf_op jit(solution)/shard_map/all_gather | solution.py:18
  64.9 5.1 %copy-start = (bf16[144,8192]{0,1:T(8,128)(2,1)S(1)}, bf16[144,8192]{0,1:T(8,128)(2,1)}, u32[]{:S(2)}) copy-start(bf16[144,8192]{0,1:T(8,128)(2,1)} %all-gather.4.cloned.1.call-done) | copy-start | bytes 7077892
  74.4 30.9 %all-to-all-start = ((bf16[128,8,1024]{0,2,1:T(8,128)(2,1)}), bf16[128,8,1024]{0,2,1:T(8,128)(2,1)S(1)}, u32[]{:S(2)}, u32[]{:S(2)}) async-start(bf16[128,8,1024]{0,2,1:T(8,128)(2,1)} %bitcast.22), calls=%async_computation | async-start | bytes 4194304 | tf_op jit(solution)/shard_map/all_to_all | solution.py:24
  78.6 98.1 %reduce-scatter.3.cloned.1.call-start = ((), (), s32[]{:S(2)}) async-start(), calls=%async_computation.4 | async-start | bytes 5242880 | tf_op jit(solution)/shard_map/reduce_scatter | solution.py:41
  116.1 7.5 %collective-permute-start = (f32[512,2048]{1,0:T(8,128)}, f32[512,2048]{1,0:T(8,128)}, u32[]{:S(2)}, u32[]{:S(2)}) collective-permute-start(f32[512,2048]{1,0:T(8,128)} %fusion.7), channel_id=1, source_target_pairs={{0,64},{64,0},{1,65},{65,1},{2,66},{66,2},{3,67},{67,3},{4,68},{68... | collective-permute-start | bytes 12582920 | tf_op jit(solution)/shard_map/ppermute | solution.py:39
  131.4 94.4 %reduce-scatter.5.cloned.1.call-start = ((), (), s32[]{:S(2)}) async-start(), calls=%async_computation.5 | async-start | bytes 5242880 | tf_op jit(solution)/shard_map/reduce_scatter | solution.py:41
  136.0 7.4 %collective-permute-start.1 = (f32[512,2048]{1,0:T(8,128)S(1)}, f32[512,2048]{1,0:T(8,128)S(1)}, u32[]{:S(2)}, u32[]{:S(2)}) collective-permute-start(f32[512,2048]{1,0:T(8,128)S(1)} %fusion.3), channel_id=1, source_target_pairs={{0,64},{64,0},{1,65},{65,1},{2,66},{66,2},{3,67},{67,3},{4,68},{68... | collective-permute-start | bytes 12582920 | tf_op jit(solution)/shard_map/ppermute | solution.py:39
Sparse Core Ops, SparseCore 0:
  10.7 54.1 all-gather.3
  131.5 45.1 reduce-scatter.2
  179.3 46.5 reduce-scatter.4

commit v4 on v3

v4 whole, which is shorter than its diff:
```python
import functools

import jax
import jax.numpy as jnp
from jax import lax
from jax.experimental import pallas as pl
from jax.experimental.pallas import tpu as pltpu
from jax.sharding import PartitionSpec as P

MESH = pl.DeviceIdType.MESH

EPS = 1e-05
GUIDE = 1.5
CHUNKS = 2
SPARE = 16


def dispatch_kernel(npair, nb, nv, span, src_ref, out_ref, send_sems, recv_sems):
    beta = lax.axis_index("pair")
    b = lax.axis_index("batch")
    v = lax.axis_index("vocab")
    groups = npair * nb
    mine = beta * nb + b
    q = v // span
    tp = q // nb
    tb = q % nb
    slot = mine * span + v % span
    d = q - mine
    own = 1 - (d * d + groups * groups - 1) // (groups * groups)

    def sources(s):
        bs = s // (nb * span)
        bbs = (s // span) % nb
        sv = mine * span + s % span
        return bs, bbs, sv

    barrier = pltpu.get_barrier_semaphore()
    for w in range(nv):
        @pl.when(jnp.logical_not((tp == beta) & (tb == b) & (v == w)))
        def _():
            pl.semaphore_signal(barrier, inc=1, device_id=(tp, tb, w), device_id_type=MESH)
    for s in range(nv):
        bs, bbs, sv = sources(s)

        @pl.when(jnp.logical_not((bs == beta) & (bbs == b) & (sv == v)))
        def _():
            pl.semaphore_signal(barrier, inc=1, device_id=(bs, bbs, sv), device_id_type=MESH)
    pl.semaphore_wait(barrier, 2 * (nv - own))

    def remote(w):
        return pltpu.make_async_remote_copy(
            src_ref=src_ref,
            dst_ref=out_ref.at[slot],
            send_sem=send_sems.at[w],
            recv_sem=recv_sems.at[slot],
            device_id=(tp, tb, w),
            device_id_type=MESH,
        )

    for w in range(nv):
        here = (tp == beta) & (tb == b) & (v == w)

        @pl.when(jnp.logical_not(here))
        def _():
            remote(w).start()

        @pl.when(here)
        def _():
            pltpu.make_async_copy(src_ref, out_ref.at[slot], recv_sems.at[slot]).start()

    for w in range(nv):
        here = (tp == beta) & (tb == b) & (v == w)

        @pl.when(jnp.logical_not(here))
        def _():
            remote(w).wait_send()

    for s in range(nv):
        bs, bbs, sv = sources(s)
        here = (bs == beta) & (bbs == b) & (sv == v)

        @pl.when(jnp.logical_not(here))
        def _():
            pltpu.make_async_remote_copy(
                src_ref=src_ref,
                dst_ref=out_ref.at[s],
                send_sem=send_sems.at[0],
                recv_sem=recv_sems.at[s],
                device_id=(bs, bbs, sv),
                device_id_type=MESH,
            ).wait_recv()

        @pl.when(here)
        def _():
            pltpu.make_async_copy(src_ref, out_ref.at[s], recv_sems.at[s]).wait()


def dispatch(block, npair, nb, nv):
    span = nv // (npair * nb)
    size = block.size * block.dtype.itemsize
    return pl.pallas_call(
        functools.partial(dispatch_kernel, npair, nb, nv, span),
        out_shape=jax.ShapeDtypeStruct((nv,) + block.shape, block.dtype),
        in_specs=[pl.BlockSpec(memory_space=pltpu.VMEM)],
        out_specs=pl.BlockSpec(memory_space=pltpu.VMEM),
        scratch_shapes=[pltpu.SemaphoreType.DMA((nv,)), pltpu.SemaphoreType.DMA((nv,))],
        compiler_params=pltpu.CompilerParams(collective_id=0, has_side_effects=True),
        cost_estimate=pl.CostEstimate(flops=0, transcendentals=0, bytes_accessed=2 * nv * size),
    )(block)


def on_device(npair, nb, nv, hidden, norm_gain, head_weight):
    groups = npair * nb
    span = nv // groups
    local_rows, width = hidden.shape[1], hidden.shape[2]
    total_d = width * nv
    pad = jnp.zeros((SPARE - 1, width), hidden.dtype)
    block = jnp.concatenate([hidden[0], norm_gain[None, :], pad], axis=0)
    got = dispatch(block, npair, nb, nv)
    raw = got[:, :local_rows, :].reshape(npair, nb, span, local_rows, width)
    raw = raw.transpose(0, 1, 3, 2, 4).reshape(npair * nb * local_rows, span * width)
    gain = got[:span, local_rows, :].reshape(span * width)
    wide = raw.astype(jnp.float32)
    sq = jnp.sum(wide * wide, axis=1)
    feats = (wide * gain.astype(jnp.float32)[None, :]).astype(jnp.bfloat16)
    rows_all = feats.shape[0] // npair
    out_rows = rows_all // groups
    ordered = feats.reshape(npair, groups, out_rows, -1).transpose(1, 0, 2, 3).reshape(npair * rows_all, -1)
    sq_ordered = sq.reshape(npair, groups, out_rows).transpose(1, 0, 2).reshape(npair * rows_all)
    half_rows = ordered.shape[0] // 2
    me = lax.axis_index("pair")
    mine = lax.dynamic_slice_in_dim(ordered, me * half_rows, half_rows, axis=0)
    theirs = lax.dynamic_slice_in_dim(ordered, (1 - me) * half_rows, half_rows, axis=0)
    sq_mine = lax.dynamic_slice_in_dim(sq_ordered, me * half_rows, half_rows, axis=0)
    sq_theirs = lax.dynamic_slice_in_dim(sq_ordered, (1 - me) * half_rows, half_rows, axis=0)
    lanes = 128
    extra_mine = jnp.zeros((half_rows, lanes), jnp.float32).at[:, 0].set(sq_mine)
    extra_theirs = jnp.zeros((half_rows, lanes), jnp.float32).at[:, 0].set(sq_theirs)
    cols = head_weight.shape[1]
    step = cols // CHUNKS
    pieces = []
    for j in range(CHUNKS):
        w = head_weight[:, j * step:(j + 1) * step]
        sent = jnp.dot(theirs, w, preferred_element_type=jnp.float32)
        kept = jnp.dot(mine, w, preferred_element_type=jnp.float32)
        if j == 0:
            sent = jnp.concatenate([sent, extra_theirs], axis=1)
            kept = jnp.concatenate([kept, extra_mine], axis=1)
        got_half = lax.ppermute(sent, "pair", [(0, 1), (1, 0)])
        pieces.append(lax.psum_scatter(kept + got_half, "batch", scatter_dimension=0, tiled=True))
    total_sq = pieces[0][:, step]
    pieces[0] = pieces[0][:, :step]
    scale = lax.rsqrt(total_sq / total_d + EPS)
    logits = jnp.concatenate(pieces, axis=1) * scale[:, None]
    cond = logits[:out_rows]
    uncond = logits[out_rows:]
    guided = GUIDE * cond + (1.0 - GUIDE) * uncond
    peak_c = jnp.max(cond, axis=1)
    peak_g = jnp.max(guided, axis=1)
    local_c = jnp.sum(jnp.exp(cond - peak_c[:, None]), axis=1)
    local_g = jnp.sum(jnp.exp(guided - peak_g[:, None]), axis=1)
    stats = jnp.stack([peak_c, local_c, peak_g, local_g])
    every = lax.all_gather(stats, "vocab", axis=0)
    top_c = jnp.max(every[:, 0], axis=0)
    top_g = jnp.max(every[:, 2], axis=0)
    total_c = jnp.sum(every[:, 1] * jnp.exp(every[:, 0] - top_c[None, :]), axis=0)
    total_g = jnp.sum(every[:, 3] * jnp.exp(every[:, 2] - top_g[None, :]), axis=0)
    cond_out = cond - (top_c + jnp.log(total_c))[:, None]
    guided_out = guided - (top_g + jnp.log(total_g))[:, None]
    return (guided_out, cond_out)


def solution(mesh):
    npair, nb, nv = mesh.shape["pair"], mesh.shape["batch"], mesh.shape["vocab"]
    in_specs = (P("pair", "batch", "vocab"), P("vocab"), P(("pair", "batch"), "vocab"))
    out_specs = (P(("pair", "batch"), "vocab"), P(("pair", "batch"), "vocab"))
    return jax.shard_map(
        functools.partial(on_device, npair, nb, nv),
        mesh=mesh, in_specs=in_specs, out_specs=out_specs, check_vma=False,
    )
```

time: 260 us -> 313 us (1.20)
  Pallas kernels: 0 us -> 67.9 us
  waiting for transfers between devices: 170 us -> 147 us
  other arithmetic: 12.8 us -> 22.9 us
  local copies, waits for them, and re-layouts: 8.95 us -> 16.8 us
  matrix products: 25.2 us -> 20.1 us
  starting transfers between devices: 4.96 us -> 0.48 us
    pallas_call x0 -> x1, Pallas kernels: none -> 67.9 us  [dispatch(): pl.pallas_call(functools.partial(dispatch_kernel, npair, nb, nv, span), o...]
    reduce_scatter x2, waiting for transfers between devices: 74.6 us -> 136 us  [on_device(): lax.psum_scatter(kept + got_half, 'batch', scatter_dimension=0, tiled=True)]
    all_gather x1 -> x0, waiting for transfers between devices: 54.9 us -> none  [on_device(): gathered = lax.all_gather(packed, 'vocab', axis=1, tiled=True)]
    all_to_all x1 -> x0, waiting for transfers between devices: 26.5 us -> none  [on_device(): lax.all_to_all(features, ('pair', 'batch'), split_axis=1, concat_axis=0,...]
    convert_element_type x0 -> x2, local copies, waits for them, and re-layouts: none -> 14 us  [on_device(): wide = raw.astype(jnp.float32)]
    add x0 -> x1, other arithmetic: none -> 4.94 us  [on_device(): kept + got_half]
    all_to_all x1 -> x0, starting transfers between devices: 4.29 us -> none  [on_device(): lax.all_to_all(features, ('pair', 'batch'), split_axis=1, concat_axis=0,...]
    ppermute x2, waiting for transfers between devices: 14.4 us -> 10.2 us  [on_device(): got_half = lax.ppermute(sent, 'pair', [(0, 1), (1, 0)])]
  transfers between devices with their start and end apart: 6 -> 4, of which waited for: 6 -> 4; matrix products, arithmetic and copies ran while one was open for 5% -> 6% of each run, Pallas kernels for 0% -> 0%
where the time goes in v4:
time: 313 us; the launch traced here: 312 us
  waiting for transfers between devices  147 us (47%)
  Pallas kernels  67.9 us (22%)
  blocking collectives  23.5 us (8%)
  other arithmetic  22.9 us (7%)
  matrix products  20.1 us (6%)
  local copies, waits for them, and re-layouts  16.8 us (5%)
  between operations  14.2 us (5%)
    reduce_scatter x2, waiting for transfers between devices, on_device(): lax.psum_scatter(kept + got_half, 'batch', scatter_dimension=0, tiled=True)  136 us
    pallas_call x1, Pallas kernels, dispatch(): pl.pallas_call(functools.partial(dispatch_kernel, npair, nb, nv, span), o...  67.9 us
    all_gather x1, blocking collectives, on_device(): every = lax.all_gather(stats, 'vocab', axis=0)  23.5 us
    convert_element_type x2, local copies, waits for them, and re-layouts, on_device(): wide = raw.astype(jnp.float32)  14 us
    dot_general x2, matrix products, on_device(): kept = jnp.dot(mine, w, preferred_element_type=jnp.float32)  11 us
    ppermute x2, waiting for transfers between devices, on_device(): got_half = lax.ppermute(sent, 'pair', [(0, 1), (1, 0)])  10.2 us
    dot_general x2, matrix products, on_device(): sent = jnp.dot(theirs, w, preferred_element_type=jnp.float32)  9.05 us
  transfers between devices with their start and end apart: 4, of which 4 were waited for; matrix products, arithmetic and copies ran while one was open for 6% of the time, Pallas kernels for 0%

profile of v4, /device:TPU:0, one launch (start us, length us, event | category | flops | bytes accessed | tf_op | source)
XLA Modules:
  0.0 312.4 jit_solution(8863615909916689781)
XLA Ops:
  7.2 0.7 broadcast_in_dim.4
  8.0 1.7 maximum_maximum_fusion.src_ref
  9.6 67.9 %shard_map.50 = bf16[16,144,512]{2,1,0:T(8,128)(2,1)} custom-call(bf16[144,512]{1,0:T(8,128)(2,1)} %maximum_maximum_fusion.src_ref), custom_call_target="tpu_custom_call" | custom-call | bytes 4718592 | tf_op jit(solution)/shard_map/pallas_call | solution.py:101
  77.5 4.2 %slice_convert_fusion = f32[16,128,512]{2,1,0:T(8,128)} fusion(bf16[16,144,512]{2,1,0:T(8,128)(2,1)} %shard_map.50), kind=kLoop, calls=%fused_computation.18 | loop fusion | flops 1048576 | bytes 6291456 | tf_op jit(solution)/shard_map/convert_element_type | solution.py:123
  82.3 0.6 compare_reduce_fusion
  82.9 7.4 %copy.46 = f32[2,4,2,128,512]{4,2,3,1,0:T(2,128)} copy(f32[2,4,2,128,512]{4,3,2,1,0:T(8,128)} %bitcast.27) | data formatting | bytes 8388608 | tf_op jit(solution)/shard_map/convert_element_type | solution.py:123
  90.3 6.6 %reshape.112 = f32[2,8,64,1024]{3,2,1,0:T(8,128)} reshape(f32[2,4,128,2,512]{4,3,2,1,0:T(2,128)} %bitcast.28) | data formatting | bytes 8388608 | tf_op jit(solution)/shard_map/convert_element_type | solution.py:123
  96.9 2.8 fusion.12
  100.1 0.7 dynamic-slice_select_fusion.1
  101.0 4.5 %fusion.5 = f32[512,2048]{1,0:T(8,128)S(1)} fusion(bf16[1024,4096]{1,0:T(8,128)(2,1)} %param.9, bf16[1024,1024]{1,0:T(8,128)(2,1)S(1)} %bitcast.29, s32[]{:T(128)S(6)} %select_n.9), kind=kOutput, calls=%fused_computation.11 | convolution fusion | flops 2147483648 | bytes 9437188 | tf_op jit(solution)/shard_map/dot_general | solution.py:144
  105.5 2.4 select_maximum_fusion
  108.1 4.5 %fusion.7 = f32[512,2048]{1,0:T(8,128)S(1)} fusion(bf16[1024,4096]{1,0:T(8,128)(2,1)} %param.9, bf16[1024,1024]{1,0:T(8,128)(2,1)S(1)} %bitcast.30, s32[]{:T(128)S(6)} %select_n.8), kind=kOutput, calls=%fused_computation.13 | convolution fusion | flops 2147483648 | bytes 9437188 | tf_op jit(solution)/shard_map/dot_general | solution.py:145
  112.6 3.2 %collective-permute-done = f32[512,2176]{1,0:T(8,128)} collective-permute-done((f32[512,2176]{1,0:T(8,128)}, f32[512,2176]{1,0:T(8,128)}, u32[]{:S(2)}, u32[]{:S(2)}) %collective-permute-start) | collective-permute-done | bytes 4456480 | tf_op jit(solution)/shard_map/ppermute | solution.py:149
  115.8 4.9 %fusion = f32[512,2176]{1,0:T(8,128)} fusion(f32[512,2176]{1,0:T(8,128)} %collective-permute-done, f32[512,1]{1,0:T(8,128)S(1)} %copy.38, f32[512,2048]{1,0:T(8,128)S(1)} %fusion.7), kind=kLoop, calls=%fused_computation.2 | loop fusion | flops 4456448 | bytes 13109248 | tf_op jit(solution)/shard_map/add | solution.py:150
  121.0 4.5 %fusion.1 = f32[512,2048]{1,0:T(8,128)S(1)} fusion(bf16[1024,4096]{1,0:T(8,128)(2,1)} %param.9, bf16[1024,1024]{1,0:T(8,128)(2,1)S(1)} %bitcast.31, s32[]{:T(128)S(6)} %select_n.9), kind=kOutput, calls=%fused_computation.7 | convolution fusion | flops 2147483648 | bytes 9437188 | tf_op jit(solution)/shard_map/dot_general | solution.py:144
  125.7 7.0 %collective-permute-done.1 = f32[512,2048]{1,0:T(8,128)S(1)} collective-permute-done((f32[512,2048]{1,0:T(8,128)S(1)}, f32[512,2048]{1,0:T(8,128)S(1)}, u32[]{:S(2)}, u32[]{:S(2)}) %collective-permute-start.1) | collective-permute-done | bytes 4194336 | tf_op jit(solution)/shard_map/ppermute | solution.py:149
  132.8 6.5 %fusion.9 = f32[512,2048]{1,0:T(8,128)} fusion(f32[512,2048]{1,0:T(8,128)S(1)} %collective-permute-done.1, bf16[1024,4096]{1,0:T(8,128)(2,1)} %param.9, bf16[1024,1024]{1,0:T(8,128)(2,1)S(1)} %bitcast.32, s32[]{:T(128)S(6)} %select_n.8), kind=kOutput, calls=%fused_computation.15 | convolution fusion | flops 2148532224 | bytes 13631492 | tf_op jit(solution)/shard_map/dot_general | solution.py:145
  139.3 89.8 %reduce-scatter.3.cloned.1.call-done = f32[128,2176]{1,0:T(8,128)} async-done(((f32[512,2176]{1,0:T(8,128)}), f32[128,2176]{1,0:T(8,128)}) %reduce-scatter.3.cloned.1.call-update) | async-done | bytes 1114128 | tf_op jit(solution)/shard_map/reduce_scatter | solution.py:150
  229.0 1.3 slice.78
  230.3 0.9 fusion.20
  231.3 46.7 %reduce-scatter.5.cloned.1.call-done = f32[128,2048]{1,0:T(8,128)} async-done(((f32[512,2048]{1,0:T(8,128)}), f32[128,2048]{1,0:T(8,128)}) %reduce-scatter.5.cloned.1.call-update) | async-done | bytes 1048592 | tf_op jit(solution)/shard_map/reduce_scatter | solution.py:150
  278.0 1.5 maximum_multiply_fusion
  280.3 23.5 %all-gather.1 = f32[16,4,64]{2,1,0:T(4,128)S(1)} all-gather(f32[1,4,64]{2,1,0:T(4,128)S(1)} %maximum_bitcast_fusion), channel_id=2, replica_groups=mesh['pair'=2,'batch'=4,'vocab'=16] {'vocab'}, dimensions={0}, use_global_device_ids=true | all-gather | bytes 17408 | tf_op jit(solution)/shard_map/all_gather | solution.py:163
  303.9 1.6 slice_subtract_fusion
  (27 shorter events, 2.7 us)
Async XLA Ops:
  7.2 221.9 %reduce-scatter.3.cloned.1.call-start = ((), (), s32[]{:S(2)}) async-start(), calls=%async_computation.2 | async-start | bytes 5570560 | tf_op jit(solution)/shard_map/reduce_scatter | solution.py:150
  77.5 4.3 %copy-start = (bf16[16,144,512]{2,1,0:T(8,128)(2,1)S(1)}, bf16[16,144,512]{2,1,0:T(8,128)(2,1)}, u32[]{:S(2)}) copy-start(bf16[16,144,512]{2,1,0:T(8,128)(2,1)} %shard_map.50) | copy-start | bytes 7077892
  107.9 7.9 %collective-permute-start = (f32[512,2176]{1,0:T(8,128)}, f32[512,2176]{1,0:T(8,128)}, u32[]{:S(2)}, u32[]{:S(2)}) collective-permute-start(f32[512,2176]{1,0:T(8,128)} %select_maximum_fusion), channel_id=1, source_target_pairs={{0,64},{64,0},{1,65},{65,1},{2,66},{66,2},{3,67},{67,3},{4,68},{68... | collective-permute-start | bytes 13369352 | tf_op jit(solution)/shard_map/ppermute | solution.py:149
  120.8 157.2 %reduce-scatter.5.cloned.1.call-start = ((), (), s32[]{:S(2)}) async-start(), calls=%async_computation.3 | async-start | bytes 5242880 | tf_op jit(solution)/shard_map/reduce_scatter | solution.py:150
  125.5 7.2 %collective-permute-start.1 = (f32[512,2048]{1,0:T(8,128)S(1)}, f32[512,2048]{1,0:T(8,128)S(1)}, u32[]{:S(2)}, u32[]{:S(2)}) collective-permute-start(f32[512,2048]{1,0:T(8,128)S(1)} %fusion.1), channel_id=1, source_target_pairs={{0,64},{64,0},{1,65},{65,1},{2,66},{66,2},{3,67},{67,3},{4,68},{68... | collective-permute-start | bytes 12582920 | tf_op jit(solution)/shard_map/ppermute | solution.py:149
Sparse Core Ops, SparseCore 0:
  120.9 108.0 reduce-scatter.2
  231.4 46.5 reduce-scatter.4

commit v5 on v4

--- a/solution.py
+++ b/solution.py
@@ -117,25 +117,23 @@
     pad = jnp.zeros((SPARE - 1, width), hidden.dtype)
     block = jnp.concatenate([hidden[0], norm_gain[None, :], pad], axis=0)
     got = dispatch(block, npair, nb, nv)
-    raw = got[:, :local_rows, :].reshape(npair, nb, span, local_rows, width)
-    raw = raw.transpose(0, 1, 3, 2, 4).reshape(npair * nb * local_rows, span * width)
-    gain = got[:span, local_rows, :].reshape(span * width)
+    half = local_rows // 2
+    raw = got[:, :local_rows, :].reshape(npair, nb, span, 2, half, width)
+    raw = raw.transpose(1, 3, 0, 4, 2, 5)
+    gain = got[:span, local_rows, :].reshape(span, width)
     wide = raw.astype(jnp.float32)
-    sq = jnp.sum(wide * wide, axis=1)
-    feats = (wide * gain.astype(jnp.float32)[None, :]).astype(jnp.bfloat16)
-    rows_all = feats.shape[0] // npair
-    out_rows = rows_all // groups
-    ordered = feats.reshape(npair, groups, out_rows, -1).transpose(1, 0, 2, 3).reshape(npair * rows_all, -1)
-    sq_ordered = sq.reshape(npair, groups, out_rows).transpose(1, 0, 2).reshape(npair * rows_all)
+    sq = jnp.sum(wide * wide, axis=(4, 5)).reshape(groups, npair * half)
+    feats = (wide * gain.astype(jnp.float32)).astype(jnp.bfloat16)
+    ordered = feats.reshape(groups * npair * half, span * width)
+    out_rows = half
+    me = lax.axis_index("pair")
+    sq_mine = lax.dynamic_slice_in_dim(sq, me * nb, nb, axis=0)
+    sq_theirs = lax.dynamic_slice_in_dim(sq, (1 - me) * nb, nb, axis=0)
+    sq_half = sq_mine + lax.ppermute(sq_theirs, "pair", [(0, 1), (1, 0)])
+    total_sq = lax.psum_scatter(sq_half, "batch", scatter_dimension=0, tiled=True).reshape(npair * half)
     half_rows = ordered.shape[0] // 2
-    me = lax.axis_index("pair")
     mine = lax.dynamic_slice_in_dim(ordered, me * half_rows, half_rows, axis=0)
     theirs = lax.dynamic_slice_in_dim(ordered, (1 - me) * half_rows, half_rows, axis=0)
-    sq_mine = lax.dynamic_slice_in_dim(sq_ordered, me * half_rows, half_rows, axis=0)
-    sq_theirs = lax.dynamic_slice_in_dim(sq_ordered, (1 - me) * half_rows, half_rows, axis=0)
-    lanes = 128
-    extra_mine = jnp.zeros((half_rows, lanes), jnp.float32).at[:, 0].set(sq_mine)
-    extra_theirs = jnp.zeros((half_rows, lanes), jnp.float32).at[:, 0].set(sq_theirs)
     cols = head_weight.shape[1]
     step = cols // CHUNKS
     pieces = []
@@ -143,13 +141,8 @@
         w = head_weight[:, j * step:(j + 1) * step]
         sent = jnp.dot(theirs, w, preferred_element_type=jnp.float32)
         kept = jnp.dot(mine, w, preferred_element_type=jnp.float32)
-        if j == 0:
-            sent = jnp.concatenate([sent, extra_theirs], axis=1)
-            kept = jnp.concatenate([kept, extra_mine], axis=1)
         got_half = lax.ppermute(sent, "pair", [(0, 1), (1, 0)])
         pieces.append(lax.psum_scatter(kept + got_half, "batch", scatter_dimension=0, tiled=True))
-    total_sq = pieces[0][:, step]
-    pieces[0] = pieces[0][:, :step]
     scale = lax.rsqrt(total_sq / total_d + EPS)
     logits = jnp.concatenate(pieces, axis=1) * scale[:, None]
     cond = logits[:out_rows]

time: 313 us -> 296 us (0.946)
  blocking collectives: 23.5 us -> 54.4 us
  waiting for transfers between devices: 147 us -> 118 us
  other arithmetic: 22.9 us -> 8.1 us
  local copies, waits for them, and re-layouts: 16.8 us -> 6.33 us
  matrix products: 20.1 us -> 25.2 us
    reduce_scatter x2, waiting for transfers between devices: 136 us -> 104 us  [on_device(): lax.psum_scatter(kept + got_half, 'batch', scatter_dimension=0, tiled=True)]
    unnamed x0 -> x1, blocking collectives: none -> 30.9 us
    convert_element_type x2 -> x1, local copies, waits for them, and re-layouts: 14 us -> 2.16 us  [on_device(): feats = (wide * gain.astype(jnp.float32)).astype(jnp.bfloat16)]
    add x1, other arithmetic: 4.94 us -> 0.01 us  [on_device(): sq_half = sq_mine + lax.ppermute(sq_theirs, 'pair', [(0, 1), (1, 0)])]
    ppermute x2, waiting for transfers between devices: 10.2 us -> 14.5 us  [on_device(): got_half = lax.ppermute(sent, 'pair', [(0, 1), (1, 0)])]
    convert_element_type x2 -> x1, other arithmetic: 4.25 us -> 0.72 us  [on_device(): feats = (wide * gain.astype(jnp.float32)).astype(jnp.bfloat16)]
    dot_general x2, matrix products: 11 us -> 14.2 us  [on_device(): kept = jnp.dot(mine, w, preferred_element_type=jnp.float32)]
  transfers between devices with their start and end apart: 4 -> 5, of which waited for: 4 -> 5; matrix products, arithmetic and copies ran while one was open for 6% -> 4% of each run, Pallas kernels for 0% -> 0%
where the time goes in v5:
time: 296 us; the launch traced here: 295 us
  waiting for transfers between devices  118 us (40%)
  Pallas kernels  67.9 us (23%)
  blocking collectives  54.4 us (18%)
  matrix products  25.2 us (9%)
  between operations  14.1 us (5%)
  other arithmetic  8.1 us (3%)
  local copies, waits for them, and re-layouts  6.33 us (2%)
    reduce_scatter x2, waiting for transfers between devices, on_device(): lax.psum_scatter(kept + got_half, 'batch', scatter_dimension=0, tiled=True)  104 us
    pallas_call x1, Pallas kernels, dispatch(): pl.pallas_call(functools.partial(dispatch_kernel, npair, nb, nv, span), o...  67.9 us
    unnamed x1, blocking collectives  30.9 us
    all_gather x1, blocking collectives, on_device(): every = lax.all_gather(stats, 'vocab', axis=0)  23.5 us
    ppermute x2, waiting for transfers between devices, on_device(): got_half = lax.ppermute(sent, 'pair', [(0, 1), (1, 0)])  14.5 us
    dot_general x2, matrix products, on_device(): kept = jnp.dot(mine, w, preferred_element_type=jnp.float32)  14.2 us
    dot_general x2, matrix products, on_device(): sent = jnp.dot(theirs, w, preferred_element_type=jnp.float32)  11 us
  transfers between devices with their start and end apart: 5, of which 5 were waited for; matrix products, arithmetic and copies ran while one was open for 4% of the time, Pallas kernels for 0%

profile of v5, /device:TPU:0, one launch (start us, length us, event | category | flops | bytes accessed | tf_op | source)
XLA Modules:
  0.0 295.2 jit_solution(2300344378349320066)
XLA Ops:
  7.2 0.7 broadcast_in_dim.4
  8.0 1.7 maximum_maximum_fusion.src_ref
  9.6 67.9 %shard_map.50 = bf16[16,144,512]{2,1,0:T(8,128)(2,1)} custom-call(bf16[144,512]{1,0:T(8,128)(2,1)} %maximum_maximum_fusion.src_ref), custom_call_target="tpu_custom_call" | custom-call | bytes 4718592 | tf_op jit(solution)/shard_map/pallas_call | solution.py:101
  77.5 1.8 slice.32
  79.3 0.7 slice_convert_fusion
  80.1 0.7 fusion.1
  80.7 2.2 copy.17
  82.9 0.6 copy.24
  83.5 6.5 %fusion.6 = f32[512,2048]{1,0:T(8,128)} fusion(bf16[1024,4096]{1,0:T(8,128)(2,1)} %param.5, bf16[1024,1024]{1,0:T(8,128)(2,1)S(1)} %bitcast.31, s32[]{:T(128)S(6)} %select_n.13), kind=kOutput, calls=%fused_computation.8 | convolution fusion | flops 2147483648 | bytes 9437188 | tf_op jit(solution)/shard_map/dot_general | solution.py:142
  90.0 7.5 %collective-permute-done = f32[512,2048]{1,0:T(8,128)} collective-permute-done((f32[512,2048]{1,0:T(8,128)}, f32[512,2048]{1,0:T(8,128)}, u32[]{:S(2)}, u32[]{:S(2)}) %collective-permute-start) | collective-permute-done | bytes 4194336 | tf_op jit(solution)/shard_map/ppermute | solution.py:144
  97.5 7.7 %fusion.10 = f32[512,2048]{1,0:T(8,128)} fusion(f32[512,2048]{1,0:T(8,128)} %collective-permute-done, bf16[1024,4096]{1,0:T(8,128)(2,1)} %param.5, bf16[1024,1024]{1,0:T(8,128)(2,1)S(1)} %bitcast.32, s32[]{:T(128)S(6)} %select_n.12), kind=kOutput, calls=%fused_computation.12 | convolution fusion | flops 2148532224 | bytes 13631492 | tf_op jit(solution)/shard_map/dot_general | solution.py:143
  105.3 4.5 %fusion.2 = f32[512,2048]{1,0:T(8,128)S(1)} fusion(bf16[1024,4096]{1,0:T(8,128)(2,1)} %param.5, bf16[1024,1024]{1,0:T(8,128)(2,1)S(1)} %bitcast.33, s32[]{:T(128)S(6)} %select_n.13), kind=kOutput, calls=%fused_computation.4 | convolution fusion | flops 2147483648 | bytes 9437188 | tf_op jit(solution)/shard_map/dot_general | solution.py:142
  109.8 0.4 collective-permute-start.1
  110.2 7.0 %collective-permute-done.1 = f32[512,2048]{1,0:T(8,128)S(1)} collective-permute-done((f32[512,2048]{1,0:T(8,128)S(1)}, f32[512,2048]{1,0:T(8,128)S(1)}, u32[]{:S(2)}, u32[]{:S(2)}) %collective-permute-start.1) | collective-permute-done | bytes 4194336 | tf_op jit(solution)/shard_map/ppermute | solution.py:144
  117.2 6.5 %fusion.13 = f32[512,2048]{1,0:T(8,128)} fusion(f32[512,2048]{1,0:T(8,128)S(1)} %collective-permute-done.1, bf16[1024,4096]{1,0:T(8,128)(2,1)} %param.5, bf16[1024,1024]{1,0:T(8,128)(2,1)S(1)} %bitcast.34, s32[]{:T(128)S(6)} %select_n.12), kind=kOutput, calls=%fused_computation.13 | convolution fusion | flops 2148532224 | bytes 13631492 | tf_op jit(solution)/shard_map/dot_general | solution.py:143
  124.4 0.6 dynamic-slice
  125.1 30.9 %all-reduce = f32[4,128]{1,0:T(4,128)S(1)} all-reduce(f32[4,128]{1,0:T(4,128)S(1)} %dynamic-slice_add_fusion), channel_id=5, replica_groups=mesh['pair'=2,'batch'=4,'vocab'=16] {'batch'}, use_global_device_ids=true, to_apply=%region_3.0.clone | all-reduce | flops 512 | bytes 4096
  155.9 0.7 rsqrt_bitcast_fusion
  156.6 54.7 %reduce-scatter.3.cloned.1.call-done = f32[128,2048]{1,0:T(8,128)} async-done(((f32[512,2048]{1,0:T(8,128)}), f32[128,2048]{1,0:T(8,128)}) %reduce-scatter.3.cloned.1.call-update) | async-done | bytes 1048592 | tf_op jit(solution)/shard_map/reduce_scatter | solution.py:145
  211.3 49.1 %reduce-scatter.5.cloned.1.call-done = f32[128,2048]{1,0:T(8,128)} async-done(((f32[512,2048]{1,0:T(8,128)}), f32[128,2048]{1,0:T(8,128)}) %reduce-scatter.5.cloned.1.call-update) | async-done | bytes 1048592 | tf_op jit(solution)/shard_map/reduce_scatter | solution.py:145
  260.4 1.8 maximum_multiply_fusion
  262.5 0.5 exponential_reduce_fusion.1
  263.1 23.5 %all-gather.1 = f32[16,4,64]{2,1,0:T(4,128)S(1)} all-gather(f32[1,4,64]{2,1,0:T(4,128)S(1)} %maximum_bitcast_fusion), channel_id=2, replica_groups=mesh['pair'=2,'batch'=4,'vocab'=16] {'vocab'}, dimensions={0}, use_global_device_ids=true | all-gather | bytes 17408 | tf_op jit(solution)/shard_map/all_gather | solution.py:156
  286.7 1.6 slice_subtract_fusion
  (23 shorter events, 1.3 us)
Async XLA Ops:
  7.2 204.2 %reduce-scatter.3.cloned.1.call-start = ((), (), s32[]{:S(2)}) async-start(), calls=%async_computation.2 | async-start | bytes 5242880 | tf_op jit(solution)/shard_map/reduce_scatter | solution.py:145
  90.0 7.5 %collective-permute-start = (f32[512,2048]{1,0:T(8,128)}, f32[512,2048]{1,0:T(8,128)}, u32[]{:S(2)}, u32[]{:S(2)}) collective-permute-start(f32[512,2048]{1,0:T(8,128)} %fusion.6), channel_id=1, source_target_pairs={{0,64},{64,0},{1,65},{65,1},{2,66},{66,2},{3,67},{67,3},{4,68},{68... | collective-permute-start | bytes 12582920 | tf_op jit(solution)/shard_map/ppermute | solution.py:144
  105.2 155.2 %reduce-scatter.5.cloned.1.call-start = ((), (), s32[]{:S(2)}) async-start(), calls=%async_computation.3 | async-start | bytes 5242880 | tf_op jit(solution)/shard_map/reduce_scatter | solution.py:145
  109.8 7.4 %collective-permute-start.1 = (f32[512,2048]{1,0:T(8,128)S(1)}, f32[512,2048]{1,0:T(8,128)S(1)}, u32[]{:S(2)}, u32[]{:S(2)}) collective-permute-start(f32[512,2048]{1,0:T(8,128)S(1)} %fusion.2), channel_id=1, source_target_pairs={{0,64},{64,0},{1,65},{65,1},{2,66},{66,2},{3,67},{67,3},{4,68},{68... | collective-permute-start | bytes 12582920 | tf_op jit(solution)/shard_map/ppermute | solution.py:144
  123.7 0.7 copy-start
  123.9 1.2 collective-permute-start.2
Sparse Core Ops, SparseCore 0:
  105.3 105.9 reduce-scatter.2
  213.8 46.5 reduce-scatter.4

commit v6 on v5

--- a/solution.py
+++ b/solution.py
@@ -12,7 +12,6 @@
 EPS = 1e-05
 GUIDE = 1.5
 CHUNKS = 2
-SPARE = 16
 
 
 def dispatch_kernel(npair, nb, nv, span, src_ref, out_ref, send_sems, recv_sems):
@@ -109,28 +108,76 @@
     )(block)
 
 
+def gather_kernel(nv, src_ref, out_ref, send_sems, recv_sems):
+    beta = lax.axis_index("pair")
+    b = lax.axis_index("batch")
+    v = lax.axis_index("vocab")
+    barrier = pltpu.get_barrier_semaphore()
+    for w in range(nv):
+        @pl.when(v != w)
+        def _():
+            pl.semaphore_signal(barrier, inc=1, device_id=(beta, b, w), device_id_type=MESH)
+    pl.semaphore_wait(barrier, nv - 1)
+
+    def remote(w, s):
+        return pltpu.make_async_remote_copy(
+            src_ref=src_ref,
+            dst_ref=out_ref.at[s],
+            send_sem=send_sems.at[w],
+            recv_sem=recv_sems.at[s],
+            device_id=(beta, b, w),
+            device_id_type=MESH,
+        )
+
+    for w in range(nv):
+        @pl.when(v != w)
+        def _():
+            remote(w, v).start()
+
+    pltpu.make_async_copy(src_ref, out_ref.at[v], recv_sems.at[v]).start()
+    for w in range(nv):
+        @pl.when(v != w)
+        def _():
+            remote(w, v).wait_send()
+    for s in range(nv):
+        @pl.when(v != s)
+        def _():
+            remote(s, s).wait_recv()
+    pltpu.make_async_copy(src_ref, out_ref.at[v], recv_sems.at[v]).wait()
+
+
+def vocab_gather(block, nv, cid):
+    size = block.size * block.dtype.itemsize
+    return pl.pallas_call(
+        functools.partial(gather_kernel, nv),
+        out_shape=jax.ShapeDtypeStruct((nv,) + block.shape, block.dtype),
+        in_specs=[pl.BlockSpec(memory_space=pltpu.VMEM)],
+        out_specs=pl.BlockSpec(memory_space=pltpu.VMEM),
+        scratch_shapes=[pltpu.SemaphoreType.DMA((nv,)), pltpu.SemaphoreType.DMA((nv,))],
+        compiler_params=pltpu.CompilerParams(collective_id=cid, has_side_effects=True),
+        cost_estimate=pl.CostEstimate(flops=0, transcendentals=0, bytes_accessed=2 * nv * size),
+    )(block)
+
+
 def on_device(npair, nb, nv, hidden, norm_gain, head_weight):
     groups = npair * nb
     span = nv // groups
     local_rows, width = hidden.shape[1], hidden.shape[2]
     total_d = width * nv
-    pad = jnp.zeros((SPARE - 1, width), hidden.dtype)
-    block = jnp.concatenate([hidden[0], norm_gain[None, :], pad], axis=0)
-    got = dispatch(block, npair, nb, nv)
+    wide = hidden[0].astype(jnp.float32)
+    part = jnp.sum(wide * wide, axis=1)
+    lanes = 128
+    part_block = jnp.zeros((8, local_rows), jnp.float32).at[0].set(part)
+    parts = vocab_gather(part_block, nv, 1)
+    meansq = jnp.sum(parts[:, 0, :], axis=0) / total_d
+    scaled = wide * lax.rsqrt(meansq + EPS)[:, None] * norm_gain.astype(jnp.float32)[None, :]
+    features = scaled.astype(jnp.bfloat16)
+    got = dispatch(features, npair, nb, nv)
     half = local_rows // 2
-    raw = got[:, :local_rows, :].reshape(npair, nb, span, 2, half, width)
-    raw = raw.transpose(1, 3, 0, 4, 2, 5)
-    gain = got[:span, local_rows, :].reshape(span, width)
-    wide = raw.astype(jnp.float32)
-    sq = jnp.sum(wide * wide, axis=(4, 5)).reshape(groups, npair * half)
-    feats = (wide * gain.astype(jnp.float32)).astype(jnp.bfloat16)
-    ordered = feats.reshape(groups * npair * half, span * width)
+    raw = got.reshape(npair, nb, span, 2, half, width).transpose(1, 3, 0, 4, 2, 5)
+    ordered = raw.reshape(groups * npair * half, span * width)
     out_rows = half
     me = lax.axis_index("pair")
-    sq_mine = lax.dynamic_slice_in_dim(sq, me * nb, nb, axis=0)
-    sq_theirs = lax.dynamic_slice_in_dim(sq, (1 - me) * nb, nb, axis=0)
-    sq_half = sq_mine + lax.ppermute(sq_theirs, "pair", [(0, 1), (1, 0)])
-    total_sq = lax.psum_scatter(sq_half, "batch", scatter_dimension=0, tiled=True).reshape(npair * half)
     half_rows = ordered.shape[0] // 2
     mine = lax.dynamic_slice_in_dim(ordered, me * half_rows, half_rows, axis=0)
     theirs = lax.dynamic_slice_in_dim(ordered, (1 - me) * half_rows, half_rows, axis=0)
@@ -143,8 +190,7 @@
         kept = jnp.dot(mine, w, preferred_element_type=jnp.float32)
         got_half = lax.ppermute(sent, "pair", [(0, 1), (1, 0)])
         pieces.append(lax.psum_scatter(kept + got_half, "batch", scatter_dimension=0, tiled=True))
-    scale = lax.rsqrt(total_sq / total_d + EPS)
-    logits = jnp.concatenate(pieces, axis=1) * scale[:, None]
+    logits = jnp.concatenate(pieces, axis=1)
     cond = logits[:out_rows]
     uncond = logits[out_rows:]
     guided = GUIDE * cond + (1.0 - GUIDE) * uncond
@@ -152,8 +198,9 @@
     peak_g = jnp.max(guided, axis=1)
     local_c = jnp.sum(jnp.exp(cond - peak_c[:, None]), axis=1)
     local_g = jnp.sum(jnp.exp(guided - peak_g[:, None]), axis=1)
-    stats = jnp.stack([peak_c, local_c, peak_g, local_g])
-    every = lax.all_gather(stats, "vocab", axis=0)
+    stats = jnp.zeros((8, lanes), jnp.float32).at[:4, :out_rows].set(
+        jnp.stack([peak_c, local_c, peak_g, local_g]))
+    every = vocab_gather(stats, nv, 2)[:, :4, :out_rows]
     top_c = jnp.max(every[:, 0], axis=0)
     top_g = jnp.max(every[:, 2], axis=0)
     total_c = jnp.sum(every[:, 1] * jnp.exp(every[:, 0] - top_c[None, :]), axis=0)

time: 296 us -> 278 us (0.939)
  blocking collectives: 54.4 us -> 0 us
  waiting for transfers between devices: 118 us -> 140 us
  Pallas kernels: 67.9 us -> 80.6 us
    unnamed x1 -> x0, blocking collectives: 30.9 us -> none
    all_gather x1 -> x0, blocking collectives: 23.5 us -> none  [on_device(): every = lax.all_gather(stats, 'vocab', axis=0)]
    pallas_call x0 -> x2, Pallas kernels: none -> 22.7 us  [vocab_gather(): pl.pallas_call(functools.partial(gather_kernel, nv), out_shape=jax.ShapeD...]
    reduce_scatter x2, waiting for transfers between devices: 104 us -> 126 us  [on_device(): lax.psum_scatter(kept + got_half, 'batch', scatter_dimension=0, tiled=True)]
    pallas_call x1, Pallas kernels: 67.9 us -> 57.9 us  [dispatch(): pl.pallas_call(functools.partial(dispatch_kernel, npair, nb, nv, span), o...]
    reshape x1, local copies, waits for them, and re-layouts: 0.08 us -> 3.75 us  [on_device(): got.reshape(npair, nb, span, 2, half, width).transpose(1, 3, 0, 4, 2, 5)]
  transfers between devices with their start and end apart: 5 -> 4, of which waited for: 5 -> 4; matrix products, arithmetic and copies ran while one was open for 4% -> 4% of each run, Pallas kernels for 0% -> 0%
where the time goes in v6:
time: 278 us; the launch traced here: 277 us
  waiting for transfers between devices  140 us (50%)
  Pallas kernels  80.6 us (29%)
  matrix products  25.2 us (9%)
  between operations  14.1 us (5%)
  local copies, waits for them, and re-layouts  8.52 us (3%)
  other arithmetic  7.37 us (3%)
    reduce_scatter x2, waiting for transfers between devices, on_device(): lax.psum_scatter(kept + got_half, 'batch', scatter_dimension=0, tiled=True)  126 us
    pallas_call x1, Pallas kernels, dispatch(): pl.pallas_call(functools.partial(dispatch_kernel, npair, nb, nv, span), o...  57.9 us
    pallas_call x2, Pallas kernels, vocab_gather(): pl.pallas_call(functools.partial(gather_kernel, nv), out_shape=jax.ShapeD...  22.7 us
    dot_general x2, matrix products, on_device(): kept = jnp.dot(mine, w, preferred_element_type=jnp.float32)  14.2 us
    ppermute x2, waiting for transfers between devices, on_device(): got_half = lax.ppermute(sent, 'pair', [(0, 1), (1, 0)])  13.9 us
    dot_general x2, matrix products, on_device(): sent = jnp.dot(theirs, w, preferred_element_type=jnp.float32)  11 us
  transfers between devices with their start and end apart: 4, of which 4 were waited for; matrix products, arithmetic and copies ran while one was open for 4% of the time, Pallas kernels for 0%

profile of v6, /device:TPU:0, one launch (start us, length us, event | category | flops | bytes accessed | tf_op | source)
XLA Modules:
  0.0 277.3 jit_solution(12297229634545620807)
XLA Ops:
  7.2 1.0 fusion.19
  8.2 0.6 scatter.6.src_ref
  8.8 11.9 %shard_map.50 = f32[16,8,128]{2,1,0:T(8,128)} custom-call(f32[8,128]{1,0:T(8,128)} %scatter.6.src_ref), custom_call_target="tpu_custom_call" | custom-call | bytes 131072 | tf_op jit(solution)/shard_map/pallas_call | solution.py:151
  20.7 0.9 slice_reduce_fusion.1
  21.6 0.7 convert_element_type.14
  22.3 1.7 fusion.21.src_ref
  23.9 57.9 %shard_map.51 = bf16[16,128,512]{2,1,0:T(8,128)(2,1)} custom-call(bf16[128,512]{1,0:T(8,128)(2,1)} %fusion.21.src_ref), custom_call_target="tpu_custom_call" | custom-call | bytes 4194304 | tf_op jit(solution)/shard_map/pallas_call | solution.py:100
  81.8 3.8 %copy.7 = bf16[2,4,2,2,64,512]{5,2,4,0,3,1:T(2,128)(2,1)S(1)} copy(bf16[2,4,2,2,64,512]{5,4,3,2,1,0:T(8,128)(2,1)} %bitcast.22) | data formatting | bytes 4194304 | tf_op jit(solution)/shard_map/reshape | solution.py:177
  86.2 6.5 %fusion.4 = f32[512,2048]{1,0:T(8,128)} fusion(bf16[1024,4096]{1,0:T(8,128)(2,1)} %param.9, bf16[1024,1024]{1,0:T(8,128)(2,1)S(1)} %bitcast.24, s32[]{:T(128)S(6)} %select_n.7), kind=kOutput, calls=%fused_computation.4 | convolution fusion | flops 2147483648 | bytes 9437188 | tf_op jit(solution)/shard_map/dot_general | solution.py:189
  92.6 0.6 collective-permute-start
  93.2 7.1 %collective-permute-done = f32[512,2048]{1,0:T(8,128)} collective-permute-done((f32[512,2048]{1,0:T(8,128)}, f32[512,2048]{1,0:T(8,128)}, u32[]{:S(2)}, u32[]{:S(2)}) %collective-permute-start) | collective-permute-done | bytes 4194336 | tf_op jit(solution)/shard_map/ppermute | solution.py:191
  100.3 7.7 %fusion.8 = f32[512,2048]{1,0:T(8,128)} fusion(f32[512,2048]{1,0:T(8,128)} %collective-permute-done, bf16[1024,4096]{1,0:T(8,128)(2,1)} %param.9, bf16[1024,1024]{1,0:T(8,128)(2,1)S(1)} %bitcast.25, s32[]{:T(128)S(6)} %select_n.6), kind=kOutput, calls=%fused_computation.8 | convolution fusion | flops 2148532224 | bytes 13631492 | tf_op jit(solution)/shard_map/dot_general | solution.py:190
  108.1 4.5 %fusion = f32[512,2048]{1,0:T(8,128)S(1)} fusion(bf16[1024,4096]{1,0:T(8,128)(2,1)} %param.9, bf16[1024,1024]{1,0:T(8,128)(2,1)S(1)} %bitcast.26, s32[]{:T(128)S(6)} %select_n.7), kind=kOutput, calls=%fused_computation | convolution fusion | flops 2147483648 | bytes 9437188 | tf_op jit(solution)/shard_map/dot_general | solution.py:189
  112.7 0.6 collective-permute-start.1
  113.3 6.8 %collective-permute-done.1 = f32[512,2048]{1,0:T(8,128)S(1)} collective-permute-done((f32[512,2048]{1,0:T(8,128)S(1)}, f32[512,2048]{1,0:T(8,128)S(1)}, u32[]{:S(2)}, u32[]{:S(2)}) %collective-permute-start.1) | collective-permute-done | bytes 4194336 | tf_op jit(solution)/shard_map/ppermute | solution.py:191
  120.1 6.5 %fusion.11 = f32[512,2048]{1,0:T(8,128)} fusion(f32[512,2048]{1,0:T(8,128)S(1)} %collective-permute-done.1, bf16[1024,4096]{1,0:T(8,128)(2,1)} %param.9, bf16[1024,1024]{1,0:T(8,128)(2,1)S(1)} %bitcast.27, s32[]{:T(128)S(6)} %select_n.6), kind=kOutput, calls=%fused_computation.9 | convolution fusion | flops 2148532224 | bytes 13631492 | tf_op jit(solution)/shard_map/dot_general | solution.py:190
  126.6 78.4 %reduce-scatter.3.cloned.1.call-done = f32[128,2048]{1,0:T(8,128)} async-done(((f32[512,2048]{1,0:T(8,128)}), f32[128,2048]{1,0:T(8,128)}) %reduce-scatter.3.cloned.1.call-update) | async-done | bytes 1048592 | tf_op jit(solution)/shard_map/reduce_scatter | solution.py:192
  205.1 1.3 constant_dynamic-update-slice_fusion.1
  206.4 47.8 %reduce-scatter.5.cloned.1.call-done = f32[128,2048]{1,0:T(8,128)} async-done(((f32[512,2048]{1,0:T(8,128)}), f32[128,2048]{1,0:T(8,128)}) %reduce-scatter.5.cloned.1.call-update) | async-done | bytes 1048592 | tf_op jit(solution)/shard_map/reduce_scatter | solution.py:192
  254.2 1.3 constant_dynamic-update-slice_fusion
  256.3 0.6 select_maximum_fusion.src_ref
  256.9 10.8 %shard_map.52 = f32[16,8,128]{2,1,0:T(8,128)} custom-call(f32[8,128]{1,0:T(8,128)} %select_maximum_fusion.src_ref), custom_call_target="tpu_custom_call" | custom-call | bytes 131072 | tf_op jit(solution)/shard_map/pallas_call | solution.py:151
  267.7 1.0 fusion.27
  268.8 1.6 slice_subtract_fusion
  (13 shorter events, 1.6 us)
Async XLA Ops:
  7.2 197.9 %reduce-scatter.3.cloned.1.call-start = ((), (), s32[]{:S(2)}) async-start(), calls=%async_computation.2 | async-start | bytes 5242880 | tf_op jit(solution)/shard_map/reduce_scatter | solution.py:192
  92.6 7.7 %collective-permute-start = (f32[512,2048]{1,0:T(8,128)}, f32[512,2048]{1,0:T(8,128)}, u32[]{:S(2)}, u32[]{:S(2)}) collective-permute-start(f32[512,2048]{1,0:T(8,128)} %fusion.4), channel_id=1, source_target_pairs={{0,64},{64,0},{1,65},{65,1},{2,66},{66,2},{3,67},{67,3},{4,68},{68... | collective-permute-start | bytes 12582920 | tf_op jit(solution)/shard_map/ppermute | solution.py:191
  108.1 146.1 %reduce-scatter.5.cloned.1.call-start = ((), (), s32[]{:S(2)}) async-start(), calls=%async_computation.3 | async-start | bytes 5242880 | tf_op jit(solution)/shard_map/reduce_scatter | solution.py:192
  112.7 7.4 %collective-permute-start.1 = (f32[512,2048]{1,0:T(8,128)S(1)}, f32[512,2048]{1,0:T(8,128)S(1)}, u32[]{:S(2)}, u32[]{:S(2)}) collective-permute-start(f32[512,2048]{1,0:T(8,128)S(1)} %fusion), channel_id=1, source_target_pairs={{0,64},{64,0},{1,65},{65,1},{2,66},{66,2},{3,67},{67,3},{4,68},{68... | collective-permute-start | bytes 12582920 | tf_op jit(solution)/shard_map/ppermute | solution.py:191
Sparse Core Ops, SparseCore 0:
  108.2 96.8 reduce-scatter.2
  207.6 46.5 reduce-scatter.4

commit v7 on v6

--- a/solution.py
+++ b/solution.py
@@ -46,33 +46,33 @@
             pl.semaphore_signal(barrier, inc=1, device_id=(bs, bbs, sv), device_id_type=MESH)
     pl.semaphore_wait(barrier, 2 * (nv - own))
 
-    def remote(w):
+    def remote(k):
         return pltpu.make_async_remote_copy(
             src_ref=src_ref,
             dst_ref=out_ref.at[slot],
-            send_sem=send_sems.at[w],
+            send_sem=send_sems.at[k],
             recv_sem=recv_sems.at[slot],
-            device_id=(tp, tb, w),
+            device_id=(tp, tb, (k + slot) % nv),
             device_id_type=MESH,
         )
 
-    for w in range(nv):
-        here = (tp == beta) & (tb == b) & (v == w)
+    for k in range(nv):
+        here = (tp == beta) & (tb == b) & (v == (k + slot) % nv)
 
         @pl.when(jnp.logical_not(here))
         def _():
-            remote(w).start()
+            remote(k).start()
 
         @pl.when(here)
         def _():
             pltpu.make_async_copy(src_ref, out_ref.at[slot], recv_sems.at[slot]).start()
 
-    for w in range(nv):
-        here = (tp == beta) & (tb == b) & (v == w)
+    for k in range(nv):
+        here = (tp == beta) & (tb == b) & (v == (k + slot) % nv)
 
         @pl.when(jnp.logical_not(here))
         def _():
-            remote(w).wait_send()
+            remote(k).wait_send()
 
     for s in range(nv):
         bs, bbs, sv = sources(s)

time: 278 us -> 252 us (0.906)
  waiting for transfers between devices: 140 us -> 105 us
  starting transfers between devices: 1.28 us -> 23.2 us
  Pallas kernels: 80.6 us -> 68.2 us
    reduce_scatter x2, waiting for transfers between devices: 126 us -> 90.7 us  [on_device(): lax.psum_scatter(kept + got_half, 'batch', scatter_dimension=0, tiled=True)]
    ppermute x2, starting transfers between devices: 1.2 us -> 23.2 us  [on_device(): got_half = lax.ppermute(sent, 'pair', [(0, 1), (1, 0)])]
    pallas_call x1, Pallas kernels: 57.9 us -> 45.6 us  [dispatch(): pl.pallas_call(functools.partial(dispatch_kernel, npair, nb, nv, span), o...]
  transfers between devices with their start and end apart: 4 -> 4, of which waited for: 4 -> 4; matrix products, arithmetic and copies ran while one was open for 4% -> 5% of each run, Pallas kernels for 0% -> 0%
where the time goes in v7:
time: 252 us; the launch traced here: 251 us
  waiting for transfers between devices  105 us (42%)
  Pallas kernels  68.2 us (27%)
  matrix products  25.2 us (10%)
  starting transfers between devices  23.2 us (9%)
  between operations  14.1 us (6%)
  local copies, waits for them, and re-layouts  8.52 us (3%)
  other arithmetic  7.37 us (3%)
    reduce_scatter x2, waiting for transfers between devices, on_device(): lax.psum_scatter(kept + got_half, 'batch', scatter_dimension=0, tiled=True)  90.7 us
    pallas_call x1, Pallas kernels, dispatch(): pl.pallas_call(functools.partial(dispatch_kernel, npair, nb, nv, span), o...  45.6 us
    ppermute x2, starting transfers between devices, on_device(): got_half = lax.ppermute(sent, 'pair', [(0, 1), (1, 0)])  23.2 us
    pallas_call x2, Pallas kernels, vocab_gather(): pl.pallas_call(functools.partial(gather_kernel, nv), out_shape=jax.ShapeD...  22.6 us
    dot_general x2, matrix products, on_device(): kept = jnp.dot(mine, w, preferred_element_type=jnp.float32)  14.2 us
    ppermute x2, waiting for transfers between devices, on_device(): got_half = lax.ppermute(sent, 'pair', [(0, 1), (1, 0)])  13.9 us
    dot_general x2, matrix products, on_device(): sent = jnp.dot(theirs, w, preferred_element_type=jnp.float32)  11 us
  transfers between devices with their start and end apart: 4, of which 4 were waited for; matrix products, arithmetic and copies ran while one was open for 5% of the time, Pallas kernels for 0%

profile of v7, /device:TPU:0, one launch (start us, length us, event | category | flops | bytes accessed | tf_op | source)
XLA Modules:
  0.0 251.3 jit_solution(17682156071586448099)
XLA Ops:
  7.2 1.0 fusion.19
  8.2 0.6 scatter.6.src_ref
  8.8 11.9 %shard_map.50 = f32[16,8,128]{2,1,0:T(8,128)} custom-call(f32[8,128]{1,0:T(8,128)} %scatter.6.src_ref), custom_call_target="tpu_custom_call" | custom-call | bytes 131072 | tf_op jit(solution)/shard_map/pallas_call | solution.py:151
  20.7 0.9 slice_reduce_fusion.1
  21.6 0.7 convert_element_type.14
  22.3 1.7 fusion.21.src_ref
  23.9 45.6 %shard_map.51 = bf16[16,128,512]{2,1,0:T(8,128)(2,1)} custom-call(bf16[128,512]{1,0:T(8,128)(2,1)} %fusion.21.src_ref), custom_call_target="tpu_custom_call" | custom-call | bytes 4194304 | tf_op jit(solution)/shard_map/pallas_call | solution.py:100
  69.5 3.8 %copy.7 = bf16[2,4,2,2,64,512]{5,2,4,0,3,1:T(2,128)(2,1)S(1)} copy(bf16[2,4,2,2,64,512]{5,4,3,2,1,0:T(8,128)(2,1)} %bitcast.22) | data formatting | bytes 4194304 | tf_op jit(solution)/shard_map/reshape | solution.py:177
  73.8 6.5 %fusion.4 = f32[512,2048]{1,0:T(8,128)} fusion(bf16[1024,4096]{1,0:T(8,128)(2,1)} %param.9, bf16[1024,1024]{1,0:T(8,128)(2,1)S(1)} %bitcast.24, s32[]{:T(128)S(6)} %select_n.7), kind=kOutput, calls=%fused_computation.4 | convolution fusion | flops 2147483648 | bytes 9437188 | tf_op jit(solution)/shard_map/dot_general | solution.py:189
  80.3 22.5 %collective-permute-start = (f32[512,2048]{1,0:T(8,128)}, f32[512,2048]{1,0:T(8,128)}, u32[]{:S(2)}, u32[]{:S(2)}) collective-permute-start(f32[512,2048]{1,0:T(8,128)} %fusion.4), channel_id=1, source_target_pairs={{0,64},{64,0},{1,65},{65,1},{2,66},{66,2},{3,67},{67,3},{4,68},{68... | collective-permute-start | bytes 12582920 | tf_op jit(solution)/shard_map/ppermute | solution.py:191
  102.8 7.1 %collective-permute-done = f32[512,2048]{1,0:T(8,128)} collective-permute-done((f32[512,2048]{1,0:T(8,128)}, f32[512,2048]{1,0:T(8,128)}, u32[]{:S(2)}, u32[]{:S(2)}) %collective-permute-start) | collective-permute-done | bytes 4194336 | tf_op jit(solution)/shard_map/ppermute | solution.py:191
  110.0 7.7 %fusion.8 = f32[512,2048]{1,0:T(8,128)} fusion(f32[512,2048]{1,0:T(8,128)} %collective-permute-done, bf16[1024,4096]{1,0:T(8,128)(2,1)} %param.9, bf16[1024,1024]{1,0:T(8,128)(2,1)S(1)} %bitcast.25, s32[]{:T(128)S(6)} %select_n.6), kind=kOutput, calls=%fused_computation.8 | convolution fusion | flops 2148532224 | bytes 13631492 | tf_op jit(solution)/shard_map/dot_general | solution.py:190
  117.8 4.5 %fusion = f32[512,2048]{1,0:T(8,128)S(1)} fusion(bf16[1024,4096]{1,0:T(8,128)(2,1)} %param.9, bf16[1024,1024]{1,0:T(8,128)(2,1)S(1)} %bitcast.26, s32[]{:T(128)S(6)} %select_n.7), kind=kOutput, calls=%fused_computation | convolution fusion | flops 2147483648 | bytes 9437188 | tf_op jit(solution)/shard_map/dot_general | solution.py:189
  122.3 0.6 collective-permute-start.1
  122.9 6.8 %collective-permute-done.1 = f32[512,2048]{1,0:T(8,128)S(1)} collective-permute-done((f32[512,2048]{1,0:T(8,128)S(1)}, f32[512,2048]{1,0:T(8,128)S(1)}, u32[]{:S(2)}, u32[]{:S(2)}) %collective-permute-start.1) | collective-permute-done | bytes 4194336 | tf_op jit(solution)/shard_map/ppermute | solution.py:191
  129.7 6.5 %fusion.11 = f32[512,2048]{1,0:T(8,128)} fusion(f32[512,2048]{1,0:T(8,128)S(1)} %collective-permute-done.1, bf16[1024,4096]{1,0:T(8,128)(2,1)} %param.9, bf16[1024,1024]{1,0:T(8,128)(2,1)S(1)} %bitcast.27, s32[]{:T(128)S(6)} %select_n.6), kind=kOutput, calls=%fused_computation.9 | convolution fusion | flops 2148532224 | bytes 13631492 | tf_op jit(solution)/shard_map/dot_general | solution.py:190
  136.2 42.9 %reduce-scatter.3.cloned.1.call-done = f32[128,2048]{1,0:T(8,128)} async-done(((f32[512,2048]{1,0:T(8,128)}), f32[128,2048]{1,0:T(8,128)}) %reduce-scatter.3.cloned.1.call-update) | async-done | bytes 1048592 | tf_op jit(solution)/shard_map/reduce_scatter | solution.py:192
  179.1 1.3 constant_dynamic-update-slice_fusion.1
  180.4 47.8 %reduce-scatter.5.cloned.1.call-done = f32[128,2048]{1,0:T(8,128)} async-done(((f32[512,2048]{1,0:T(8,128)}), f32[128,2048]{1,0:T(8,128)}) %reduce-scatter.5.cloned.1.call-update) | async-done | bytes 1048592 | tf_op jit(solution)/shard_map/reduce_scatter | solution.py:192
  228.2 1.3 constant_dynamic-update-slice_fusion
  230.3 0.6 select_maximum_fusion.src_ref
  230.9 10.8 %shard_map.52 = f32[16,8,128]{2,1,0:T(8,128)} custom-call(f32[8,128]{1,0:T(8,128)} %select_maximum_fusion.src_ref), custom_call_target="tpu_custom_call" | custom-call | bytes 131072 | tf_op jit(solution)/shard_map/pallas_call | solution.py:151
  241.7 1.0 fusion.27
  242.8 1.6 slice_subtract_fusion
  (13 shorter events, 1.6 us)
Async XLA Ops:
  7.2 172.0 %reduce-scatter.3.cloned.1.call-start = ((), (), s32[]{:S(2)}) async-start(), calls=%async_computation.2 | async-start | bytes 5242880 | tf_op jit(solution)/shard_map/reduce_scatter | solution.py:192
  80.3 29.6 %collective-permute-start = (f32[512,2048]{1,0:T(8,128)}, f32[512,2048]{1,0:T(8,128)}, u32[]{:S(2)}, u32[]{:S(2)}) collective-permute-start(f32[512,2048]{1,0:T(8,128)} %fusion.4), channel_id=1, source_target_pairs={{0,64},{64,0},{1,65},{65,1},{2,66},{66,2},{3,67},{67,3},{4,68},{68... | collective-permute-start | bytes 12582920 | tf_op jit(solution)/shard_map/ppermute | solution.py:191
  117.7 110.5 %reduce-scatter.5.cloned.1.call-start = ((), (), s32[]{:S(2)}) async-start(), calls=%async_computation.3 | async-start | bytes 5242880 | tf_op jit(solution)/shard_map/reduce_scatter | solution.py:192
  122.3 7.4 %collective-permute-start.1 = (f32[512,2048]{1,0:T(8,128)S(1)}, f32[512,2048]{1,0:T(8,128)S(1)}, u32[]{:S(2)}, u32[]{:S(2)}) collective-permute-start(f32[512,2048]{1,0:T(8,128)S(1)} %fusion), channel_id=1, source_target_pairs={{0,64},{64,0},{1,65},{65,1},{2,66},{66,2},{3,67},{67,3},{4,68},{68... | collective-permute-start | bytes 12582920 | tf_op jit(solution)/shard_map/ppermute | solution.py:191
Sparse Core Ops, SparseCore 0:
  117.8 61.2 reduce-scatter.2
  181.6 46.5 reduce-scatter.4

commit v8 on v7

--- a/solution.py
+++ b/solution.py
@@ -183,13 +183,17 @@
     theirs = lax.dynamic_slice_in_dim(ordered, (1 - me) * half_rows, half_rows, axis=0)
     cols = head_weight.shape[1]
     step = cols // CHUNKS
+    weights = [head_weight[:, j * step:(j + 1) * step] for j in range(CHUNKS)]
+    arriving = []
+    for j in range(CHUNKS):
+        sent = jnp.dot(theirs, weights[j], preferred_element_type=jnp.float32)
+        if j > 0:
+            arriving[-1], sent = lax.optimization_barrier((arriving[-1], sent))
+        arriving.append(lax.ppermute(sent, "pair", [(0, 1), (1, 0)]))
     pieces = []
     for j in range(CHUNKS):
-        w = head_weight[:, j * step:(j + 1) * step]
-        sent = jnp.dot(theirs, w, preferred_element_type=jnp.float32)
-        kept = jnp.dot(mine, w, preferred_element_type=jnp.float32)
-        got_half = lax.ppermute(sent, "pair", [(0, 1), (1, 0)])
-        pieces.append(lax.psum_scatter(kept + got_half, "batch", scatter_dimension=0, tiled=True))
+        kept = jnp.dot(mine, weights[j], preferred_element_type=jnp.float32)
+        pieces.append(lax.psum_scatter(kept + arriving[j], "batch", scatter_dimension=0, tiled=True))
     logits = jnp.concatenate(pieces, axis=1)
     cond = logits[:out_rows]
     uncond = logits[out_rows:]

time: 252 us -> 253 us (level)
  other arithmetic: 7.37 us -> 15 us
  matrix products: 25.2 us -> 22 us
  waiting for transfers between devices: 105 us -> 102 us
    ppermute x2, waiting for transfers between devices: 13.9 us -> 2.83 us  [on_device(): arriving.append(lax.ppermute(sent, 'pair', [(0, 1), (1, 0)]))]
    reduce_scatter x2, waiting for transfers between devices: 90.7 us -> 98.7 us  [on_device(): lax.psum_scatter(kept + arriving[j], 'batch', scatter_dimension=0, tiled=...]
    add x0 -> x2, other arithmetic: none -> 7.6 us  [on_device(): kept + arriving[j]]
    dot_general x4, matrix products: 25.2 us -> 22 us  [the longest x2 13 us: on_device(): sent = jnp.dot(theirs, weights[j], preferred_element_type=jnp.float32)]
  transfers between devices with their start and end apart: 4 -> 4, of which waited for: 4 -> 3; matrix products, arithmetic and copies ran while one was open for 5% -> 8% of each run, Pallas kernels for 0% -> 0%
where the time goes in v8:
time: 253 us; the launch traced here: 252 us
  waiting for transfers between devices  102 us (40%)
  Pallas kernels  68.2 us (27%)
  starting transfers between devices  22.9 us (9%)
  matrix products  22 us (9%)
  other arithmetic  15 us (6%)
  between operations  14.1 us (6%)
  local copies, waits for them, and re-layouts  8.52 us (3%)
    reduce_scatter x2, waiting for transfers between devices, on_device(): lax.psum_scatter(kept + arriving[j], 'batch', scatter_dimension=0, tiled=...  98.7 us
    pallas_call x1, Pallas kernels, dispatch(): pl.pallas_call(functools.partial(dispatch_kernel, npair, nb, nv, span), o...  45.6 us
    ppermute x2, starting transfers between devices, on_device(): arriving.append(lax.ppermute(sent, 'pair', [(0, 1), (1, 0)]))  22.8 us
    pallas_call x2, Pallas kernels, vocab_gather(): pl.pallas_call(functools.partial(gather_kernel, nv), out_shape=jax.ShapeD...  22.6 us
    dot_general x2, matrix products, on_device(): sent = jnp.dot(theirs, weights[j], preferred_element_type=jnp.float32)  13 us
    dot_general x2, matrix products, on_device(): kept = jnp.dot(mine, weights[j], preferred_element_type=jnp.float32)  9.05 us
    add x2, other arithmetic, on_device(): kept + arriving[j]  7.6 us
  transfers between devices with their start and end apart: 4, of which 3 were waited for; matrix products, arithmetic and copies ran while one was open for 8% of the time, Pallas kernels for 0%

profile of v8, /device:TPU:0, one launch (start us, length us, event | category | flops | bytes accessed | tf_op | source)
XLA Modules:
  0.0 252.3 jit_solution(11614563510447783660)
XLA Ops:
  7.2 1.0 fusion.13
  8.2 0.6 scatter.6.src_ref
  8.8 11.9 %shard_map.50 = f32[16,8,128]{2,1,0:T(8,128)} custom-call(f32[8,128]{1,0:T(8,128)} %scatter.6.src_ref), custom_call_target="tpu_custom_call" | custom-call | bytes 131072 | tf_op jit(solution)/shard_map/pallas_call | solution.py:151
  20.7 0.9 slice_reduce_fusion.1
  21.6 0.7 convert_element_type.14
  22.3 1.7 fusion.15.src_ref
  23.9 45.6 %shard_map.51 = bf16[16,128,512]{2,1,0:T(8,128)(2,1)} custom-call(bf16[128,512]{1,0:T(8,128)(2,1)} %fusion.15.src_ref), custom_call_target="tpu_custom_call" | custom-call | bytes 4194304 | tf_op jit(solution)/shard_map/pallas_call | solution.py:100
  69.5 3.8 %copy.7 = bf16[2,4,2,2,64,512]{5,2,4,0,3,1:T(2,128)(2,1)S(1)} copy(bf16[2,4,2,2,64,512]{5,4,3,2,1,0:T(8,128)(2,1)} %bitcast.22) | data formatting | bytes 4194304 | tf_op jit(solution)/shard_map/reshape | solution.py:177
  73.8 6.5 %fusion.4 = f32[512,2048]{1,0:T(8,128)} fusion(bf16[1024,4096]{1,0:T(8,128)(2,1)} %param.9, bf16[1024,1024]{1,0:T(8,128)(2,1)S(1)} %bitcast.24, s32[]{:T(128)S(6)} %select_n.7), kind=kOutput, calls=%fused_computation.4 | convolution fusion | flops 2147483648 | bytes 9437188 | tf_op jit(solution)/shard_map/dot_general | solution.py:189
  80.3 22.5 %collective-permute-start = (f32[512,2048]{1,0:T(8,128)}, f32[512,2048]{1,0:T(8,128)}, u32[]{:S(2)}, u32[]{:S(2)}) collective-permute-start(f32[512,2048]{1,0:T(8,128)} %fusion.4), channel_id=1, source_target_pairs={{0,64},{64,0},{1,65},{65,1},{2,66},{66,2},{3,67},{67,3},{4,68},{68... | collective-permute-start | bytes 12582920 | tf_op jit(solution)/shard_map/ppermute | solution.py:192
  102.8 6.5 %fusion.2 = f32[512,2048]{1,0:T(8,128)} fusion(bf16[1024,4096]{1,0:T(8,128)(2,1)} %param.9, bf16[1024,1024]{1,0:T(8,128)(2,1)S(1)} %bitcast.25, s32[]{:T(128)S(6)} %select_n.7), kind=kOutput, calls=%fused_computation.2 | convolution fusion | flops 2147483648 | bytes 9437188 | tf_op jit(solution)/shard_map/dot_general | solution.py:189
  109.3 4.5 %fusion.6 = f32[512,2048]{1,0:T(8,128)S(1)} fusion(bf16[1024,4096]{1,0:T(8,128)(2,1)} %param.9, bf16[1024,1024]{1,0:T(8,128)(2,1)S(1)} %bitcast.26, s32[]{:T(128)S(6)} %select_n.6), kind=kOutput, calls=%fused_computation.6 | convolution fusion | flops 2147483648 | bytes 9437188 | tf_op jit(solution)/shard_map/dot_general | solution.py:195
  113.9 4.9 %add.55 = f32[512,2048]{1,0:T(8,128)} add(f32[512,2048]{1,0:T(8,128)S(1)} %fusion.6, f32[512,2048]{1,0:T(8,128)} %collective-permute-done) | non-fusion elementwise | flops 1048576 | bytes 12582912 | tf_op jit(solution)/shard_map/add | solution.py:196
  119.1 4.5 %fusion = f32[512,2048]{1,0:T(8,128)S(1)} fusion(bf16[1024,4096]{1,0:T(8,128)(2,1)} %param.9, bf16[1024,1024]{1,0:T(8,128)(2,1)S(1)} %bitcast.27, s32[]{:T(128)S(6)} %select_n.6), kind=kOutput, calls=%fused_computation | convolution fusion | flops 2147483648 | bytes 9437188 | tf_op jit(solution)/shard_map/dot_general | solution.py:195
  123.6 2.8 %collective-permute-done.1 = f32[512,2048]{1,0:T(8,128)S(1)} collective-permute-done((f32[512,2048]{1,0:T(8,128)}, f32[512,2048]{1,0:T(8,128)S(1)}, u32[]{:S(2)}, u32[]{:S(2)}) %collective-permute-start.1) | collective-permute-done | bytes 4194336 | tf_op jit(solution)/shard_map/ppermute | solution.py:192
  126.4 2.7 %add.56 = f32[512,2048]{1,0:T(8,128)} add(f32[512,2048]{1,0:T(8,128)S(1)} %fusion, f32[512,2048]{1,0:T(8,128)S(1)} %collective-permute-done.1) | non-fusion elementwise | flops 1048576 | bytes 12582912 | tf_op jit(solution)/shard_map/add | solution.py:196
  129.2 50.9 %reduce-scatter.3.cloned.1.call-done = f32[128,2048]{1,0:T(8,128)} async-done(((f32[512,2048]{1,0:T(8,128)}), f32[128,2048]{1,0:T(8,128)}) %reduce-scatter.3.cloned.1.call-update) | async-done | bytes 1048592 | tf_op jit(solution)/shard_map/reduce_scatter | solution.py:196
  180.1 1.3 constant_dynamic-update-slice_fusion.1
  181.4 47.8 %reduce-scatter.5.cloned.1.call-done = f32[128,2048]{1,0:T(8,128)} async-done(((f32[512,2048]{1,0:T(8,128)}), f32[128,2048]{1,0:T(8,128)}) %reduce-scatter.5.cloned.1.call-update) | async-done | bytes 1048592 | tf_op jit(solution)/shard_map/reduce_scatter | solution.py:196
  229.2 1.3 constant_dynamic-update-slice_fusion
  231.3 0.6 select_maximum_fusion.src_ref
  232.0 10.8 %shard_map.52 = f32[16,8,128]{2,1,0:T(8,128)} custom-call(f32[8,128]{1,0:T(8,128)} %select_maximum_fusion.src_ref), custom_call_target="tpu_custom_call" | custom-call | bytes 131072 | tf_op jit(solution)/shard_map/pallas_call | solution.py:151
  242.7 1.0 fusion.21
  243.9 1.6 slice_subtract_fusion
  (15 shorter events, 1.9 us)
Async XLA Ops:
  7.2 172.9 %reduce-scatter.3.cloned.1.call-start = ((), (), s32[]{:S(2)}) async-start(), calls=%async_computation.2 | async-start | bytes 5242880 | tf_op jit(solution)/shard_map/reduce_scatter | solution.py:196
  80.3 33.5 %collective-permute-start = (f32[512,2048]{1,0:T(8,128)}, f32[512,2048]{1,0:T(8,128)}, u32[]{:S(2)}, u32[]{:S(2)}) collective-permute-start(f32[512,2048]{1,0:T(8,128)} %fusion.4), channel_id=1, source_target_pairs={{0,64},{64,0},{1,65},{65,1},{2,66},{66,2},{3,67},{67,3},{4,68},{68... | collective-permute-start | bytes 12582920 | tf_op jit(solution)/shard_map/ppermute | solution.py:192
  118.8 110.5 %reduce-scatter.5.cloned.1.call-start = ((), (), s32[]{:S(2)}) async-start(), calls=%async_computation.3 | async-start | bytes 5242880 | tf_op jit(solution)/shard_map/reduce_scatter | solution.py:196
  118.8 7.6 %collective-permute-start.1 = (f32[512,2048]{1,0:T(8,128)}, f32[512,2048]{1,0:T(8,128)S(1)}, u32[]{:S(2)}, u32[]{:S(2)}) collective-permute-start(f32[512,2048]{1,0:T(8,128)} %fusion.2), channel_id=1, source_target_pairs={{0,64},{64,0},{1,65},{65,1},{2,66},{66,2},{3,67},{67,3},{4,68},{68... | collective-permute-start | bytes 12582920 | tf_op jit(solution)/shard_map/ppermute | solution.py:192
Sparse Core Ops, SparseCore 0:
  118.9 61.1 reduce-scatter.2
  182.6 46.5 reduce-scatter.4

commit v9 on v7

--- a/solution.py
+++ b/solution.py
@@ -157,6 +157,57 @@
         compiler_params=pltpu.CompilerParams(collective_id=cid, has_side_effects=True),
         cost_estimate=pl.CostEstimate(flops=0, transcendentals=0, bytes_accessed=2 * nv * size),
     )(block)
+
+
+def exchange_kernel(nb, src_ref, out_ref, send_sems, recv_sems):
+    beta = lax.axis_index("pair")
+    b = lax.axis_index("batch")
+    v = lax.axis_index("vocab")
+    barrier = pltpu.get_barrier_semaphore()
+    for w in range(nb):
+        @pl.when(b != w)
+        def _():
+            pl.semaphore_signal(barrier, inc=1, device_id=(beta, w, v), device_id_type=MESH)
+    pl.semaphore_wait(barrier, nb - 1)
+
+    def remote(k, s):
+        target = (b + k) % nb
+        return pltpu.make_async_remote_copy(
+            src_ref=src_ref.at[target],
+            dst_ref=out_ref.at[s],
+            send_sem=send_sems.at[k],
+            recv_sem=recv_sems.at[s],
+            device_id=(beta, target, v),
+            device_id_type=MESH,
+        )
+
+    for k in range(1, nb):
+        remote(k, b).start()
+    for k in range(1, nb):
+        remote(k, b).wait_send()
+    for k in range(1, nb):
+        s = (b + k) % nb
+        pltpu.make_async_remote_copy(
+            src_ref=src_ref.at[s],
+            dst_ref=out_ref.at[s],
+            send_sem=send_sems.at[0],
+            recv_sem=recv_sems.at[s],
+            device_id=(beta, s, v),
+            device_id_type=MESH,
+        ).wait_recv()
+
+
+def batch_exchange(blocks, nb):
+    size = blocks.size * blocks.dtype.itemsize
+    return pl.pallas_call(
+        functools.partial(exchange_kernel, nb),
+        out_shape=jax.ShapeDtypeStruct(blocks.shape, blocks.dtype),
+        in_specs=[pl.BlockSpec(memory_space=pl.ANY)],
+        out_specs=pl.BlockSpec(memory_space=pl.ANY),
+        scratch_shapes=[pltpu.SemaphoreType.DMA((nb,)), pltpu.SemaphoreType.DMA((nb,))],
+        compiler_params=pltpu.CompilerParams(collective_id=3, has_side_effects=True),
+        cost_estimate=pl.CostEstimate(flops=0, transcendentals=0, bytes_accessed=2 * size),
+    )(blocks)
 
 
 def on_device(npair, nb, nv, hidden, norm_gain, head_weight):
@@ -189,8 +240,13 @@
         sent = jnp.dot(theirs, w, preferred_element_type=jnp.float32)
         kept = jnp.dot(mine, w, preferred_element_type=jnp.float32)
         got_half = lax.ppermute(sent, "pair", [(0, 1), (1, 0)])
-        pieces.append(lax.psum_scatter(kept + got_half, "batch", scatter_dimension=0, tiled=True))
-    logits = jnp.concatenate(pieces, axis=1)
+        pieces.append(kept + got_half)
+    summed = jnp.concatenate(pieces, axis=1).reshape(nb, half_rows // nb, cols)
+    arrived = batch_exchange(summed, nb)
+    mb = lax.axis_index("batch")
+    own = lax.dynamic_index_in_dim(summed, mb, axis=0, keepdims=False)
+    slots = lax.broadcasted_iota(jnp.int32, (nb, 1, 1), 0)
+    logits = own + jnp.sum(jnp.where(slots == mb, 0.0, arrived), axis=0)
     cond = logits[:out_rows]
     uncond = logits[out_rows:]
     guided = GUIDE * cond + (1.0 - GUIDE) * uncond

time: 252 us -> 252 us (level)
  Pallas kernels: 68.2 us -> 180 us
  waiting for transfers between devices: 105 us -> 1.35 us
  between operations: 14.1 us -> 0.74 us
  other arithmetic: 7.37 us -> 17.6 us
  local copies, waits for them, and re-layouts: 8.52 us -> 5.94 us
    pallas_call x0 -> x1, Pallas kernels: none -> 107 us  [batch_exchange(): pl.pallas_call(functools.partial(exchange_kernel, nb), out_shape=jax.Shap...]
    reduce_scatter x2 -> x0, waiting for transfers between devices: 90.7 us -> none  [on_device(): lax.psum_scatter(kept + got_half, 'batch', scatter_dimension=0, tiled=True)]
    ppermute x2, waiting for transfers between devices: 13.9 us -> 1.35 us  [on_device(): got_half = lax.ppermute(sent, 'pair', [(0, 1), (1, 0)])]
    pallas_call x2, Pallas kernels: 22.6 us -> 27.7 us  [vocab_gather(): pl.pallas_call(functools.partial(gather_kernel, nv), out_shape=jax.ShapeD...]
    reduce_sum x0 -> x1, other arithmetic: none -> 4.63 us  [on_device(): logits = own + jnp.sum(jnp.where(slots == mb, 0.0, arrived), axis=0)]
    concatenate x0 -> x1, other arithmetic: none -> 3.76 us  [on_device(): summed = jnp.concatenate(pieces, axis=1).reshape(nb, half_rows // nb, cols)]
    dot_general x2, matrix products: 14.2 us -> 10.6 us  [on_device(): kept = jnp.dot(mine, w, preferred_element_type=jnp.float32)]
  transfers between devices with their start and end apart: 4 -> 2, of which waited for: 4 -> 2; matrix products, arithmetic and copies ran while one was open for 5% -> 5% of each run, Pallas kernels for 0% -> 0%
where the time goes in v9:
time: 252 us
  Pallas kernels  180 us (71%)
  matrix products  23.6 us (9%)
  starting transfers between devices  22.5 us (9%)
  other arithmetic  17.6 us (7%)
  local copies, waits for them, and re-layouts  5.94 us (2%)
    pallas_call x1, Pallas kernels, batch_exchange(): pl.pallas_call(functools.partial(exchange_kernel, nb), out_shape=jax.Shap...  107 us
    pallas_call x1, Pallas kernels, dispatch(): pl.pallas_call(functools.partial(dispatch_kernel, npair, nb, nv, span), o...  45.6 us
    pallas_call x2, Pallas kernels, vocab_gather(): pl.pallas_call(functools.partial(gather_kernel, nv), out_shape=jax.ShapeD...  27.7 us
    ppermute x2, starting transfers between devices, on_device(): got_half = lax.ppermute(sent, 'pair', [(0, 1), (1, 0)])  22.5 us
    dot_general x2, matrix products, on_device(): sent = jnp.dot(theirs, w, preferred_element_type=jnp.float32)  13 us
    dot_general x2, matrix products, on_device(): kept = jnp.dot(mine, w, preferred_element_type=jnp.float32)  10.6 us
  transfers between devices with their start and end apart: 2, of which 2 were waited for; matrix products, arithmetic and copies ran while one was open for 5% of the time, Pallas kernels for 0%

profile of v9, /device:TPU:0, one launch (start us, length us, event | category | flops | bytes accessed | tf_op | source)
XLA Modules:
  0.0 251.6 jit_solution(6411644174594853194)
XLA Ops:
  0.6 1.0 fusion.19
  1.7 0.7 convert_element_type.14
  2.3 0.6 scatter.6.src_ref
  2.9 11.9 %shard_map.50 = f32[16,8,128]{2,1,0:T(8,128)} custom-call(f32[8,128]{1,0:T(8,128)} %scatter.6.src_ref), custom_call_target="tpu_custom_call" | custom-call | bytes 131072 | tf_op jit(solution)/shard_map/pallas_call | solution.py:151
  14.8 0.9 slice_reduce_fusion.1
  15.7 1.7 fusion.21.src_ref
  17.4 45.6 %shard_map.51 = bf16[16,128,512]{2,1,0:T(8,128)(2,1)} custom-call(bf16[128,512]{1,0:T(8,128)(2,1)} %fusion.21.src_ref), custom_call_target="tpu_custom_call" | custom-call | bytes 4194304 | tf_op jit(solution)/shard_map/pallas_call | solution.py:100
  62.9 3.8 %copy.7 = bf16[2,4,2,2,64,512]{5,2,4,0,3,1:T(2,128)(2,1)S(1)} copy(bf16[2,4,2,2,64,512]{5,4,3,2,1,0:T(8,128)(2,1)} %bitcast.27) | data formatting | bytes 4194304 | tf_op jit(solution)/shard_map/reshape | solution.py:228
  66.7 0.6 copy.12
  67.3 6.5 %fusion.4 = f32[512,2048]{1,0:T(8,128)} fusion(bf16[1024,4096]{1,0:T(8,128)(2,1)} %param.9, bf16[1024,1024]{1,0:T(8,128)(2,1)S(1)} %bitcast.29, s32[]{:T(128)S(6)} %select_n.15), kind=kOutput, calls=%fused_computation.6 | convolution fusion | flops 2147483648 | bytes 9437188 | tf_op jit(solution)/shard_map/dot_general | solution.py:240
  73.8 22.5 %collective-permute-start = (f32[512,2048]{1,0:T(8,128)}, f32[512,2048]{1,0:T(8,128)}, u32[]{:S(2)}, u32[]{:S(2)}) collective-permute-start(f32[512,2048]{1,0:T(8,128)} %fusion.4), channel_id=1, source_target_pairs={{0,64},{64,0},{1,65},{65,1},{2,66},{66,2},{3,67},{67,3},{4,68},{68... | collective-permute-start | bytes 12582920 | tf_op jit(solution)/shard_map/ppermute | solution.py:242
  96.3 6.4 %fusion = f32[512,2048]{1,0:T(8,128)} fusion(bf16[1024,4096]{1,0:T(8,128)(2,1)} %param.9, bf16[1024,1024]{1,0:T(8,128)(2,1)S(1)} %bitcast.30, s32[]{:T(128)S(6)} %select_n.15), kind=kOutput, calls=%fused_computation.2 | convolution fusion | flops 2147483648 | bytes 9437188 | tf_op jit(solution)/shard_map/dot_general | solution.py:240
  102.8 0.7 collective-permute-done
  103.4 6.1 %fusion.8 = f32[512,2048]{1,0:T(8,128)S(1)} fusion(f32[512,2048]{1,0:T(8,128)} %collective-permute-done, bf16[1024,4096]{1,0:T(8,128)(2,1)} %param.9, bf16[1024,1024]{1,0:T(8,128)(2,1)S(1)} %bitcast.31, s32[]{:T(128)S(6)} %select_n.14), kind=kOutput, calls=%fused_computation.10 | convolution fusion | flops 2148532224 | bytes 13631492 | tf_op jit(solution)/shard_map/dot_general | solution.py:241
  109.5 0.7 collective-permute-done.1
  110.3 4.5 %fusion.11 = f32[512,2048]{1,0:T(8,128)S(1)} fusion(f32[512,2048]{1,0:T(8,128)} %collective-permute-done.1, bf16[1024,4096]{1,0:T(8,128)(2,1)S(1)} %bitcast.45, bf16[1024,1024]{1,0:T(8,128)(2,1)S(1)} %bitcast.32, s32[]{:T(128)S(6)} %select_n.14), kind=kOutput, calls=%fused_computation.11 | convolution fusion | flops 2148532224 | bytes 13631492 | tf_op jit(solution)/shard_map/dot_general | solution.py:241
  114.8 3.8 %pad_maximum_fusion = f32[512,4096]{1,0:T(8,128)} fusion(f32[512,2048]{1,0:T(8,128)S(1)} %fusion.11, f32[512,2048]{1,0:T(8,128)S(1)} %fusion.8), kind=kLoop, calls=%fused_computation | loop fusion | flops 2097152 | bytes 16777216 | tf_op jit(solution)/shard_map/concatenate | solution.py:244
  118.5 106.6 %shard_map.52 = f32[4,128,4096]{2,1,0:T(8,128)} custom-call(f32[4,128,4096]{2,1,0:T(8,128)} %bitcast.25), custom_call_target="tpu_custom_call" | custom-call | bytes 16777216 | tf_op jit(solution)/shard_map/pallas_call | solution.py:202
  225.1 4.6 %select_reduce_fusion = f32[128,4096]{1,0:T(8,128)S(1)} fusion(f32[4,128,4096]{2,1,0:T(8,128)} %shard_map.52, pred[4]{0:T(512)(128)(4,1)S(1)} %iota_compare_fusion.2), kind=kLoop, calls=%fused_computation.1 | loop fusion | flops 3670016 | bytes 10485764 | tf_op jit(solution)/shard_map/reduce_sum | solution.py:249
  229.7 1.8 bitcast_add_fusion
  232.4 0.6 select_maximum_fusion.src_ref
  233.0 15.8 %shard_map.53 = f32[16,8,128]{2,1,0:T(8,128)} custom-call(f32[8,128]{1,0:T(8,128)} %select_maximum_fusion.src_ref), custom_call_target="tpu_custom_call" | custom-call | bytes 131072 | tf_op jit(solution)/shard_map/pallas_call | solution.py:151
  248.8 1.0 fusion.27
  250.0 1.6 slice_subtract_fusion
  (15 shorter events, 0.9 us)
Async XLA Ops:
  73.8 29.6 %collective-permute-start = (f32[512,2048]{1,0:T(8,128)}, f32[512,2048]{1,0:T(8,128)}, u32[]{:S(2)}, u32[]{:S(2)}) collective-permute-start(f32[512,2048]{1,0:T(8,128)} %fusion.4), channel_id=1, source_target_pairs={{0,64},{64,0},{1,65},{65,1},{2,66},{66,2},{3,67},{67,3},{4,68},{68... | collective-permute-start | bytes 12582920 | tf_op jit(solution)/shard_map/ppermute | solution.py:242
  102.7 7.5 %collective-permute-start.1 = (f32[512,2048]{1,0:T(8,128)}, f32[512,2048]{1,0:T(8,128)}, u32[]{:S(2)}, u32[]{:S(2)}) collective-permute-start(f32[512,2048]{1,0:T(8,128)} %fusion), channel_id=1, source_target_pairs={{0,64},{64,0},{1,65},{65,1},{2,66},{66,2},{3,67},{67,3},{4,68},{68... | collective-permute-start | bytes 12582920 | tf_op jit(solution)/shard_map/ppermute | solution.py:242
  102.7 7.5 %slice-start = ((s8[8388608]{0:T(1024)(128)(4,1)}), s8[4194304]{0:T(1024)(128)(4,1)S(1)}, s32[]{:S(2)}) async-start(s8[8388608]{0:T(1024)(128)(4,1)} %bitcast.44), calls=%async_computation | async-start | bytes 8388608
  102.8 7.5 %slice-start.1 = ((s8[8388608]{0:T(1024)(128)(4,1)}), s8[4194304]{0:T(1024)(128)(4,1)S(1)}, s32[]{:S(2)}) async-start(s8[8388608]{0:T(1024)(128)(4,1)} %bitcast.44), calls=%async_computation.1 | async-start | bytes 8388608

commit v10 on v7

--- a/solution.py
+++ b/solution.py
@@ -11,7 +11,7 @@
 
 EPS = 1e-05
 GUIDE = 1.5
-CHUNKS = 2
+CHUNKS = 4
 
 
 def dispatch_kernel(npair, nb, nv, span, src_ref, out_ref, send_sems, recv_sems):

time: 252 us -> 273 us (1.083)
  waiting for transfers between devices: 105 us -> 118 us
  matrix products: 25.2 us -> 30.3 us
    reduce_scatter x2 -> x4, waiting for transfers between devices: 90.7 us -> 102 us  [on_device(): lax.psum_scatter(kept + got_half, 'batch', scatter_dimension=0, tiled=True)]
    dot_general x2 -> x4, matrix products: 14.2 us -> 17.4 us  [on_device(): kept = jnp.dot(mine, w, preferred_element_type=jnp.float32)]
    dot_general x2 -> x4, matrix products: 11 us -> 12.9 us  [on_device(): sent = jnp.dot(theirs, w, preferred_element_type=jnp.float32)]
    ppermute x2 -> x4, waiting for transfers between devices: 13.9 us -> 15.6 us  [on_device(): got_half = lax.ppermute(sent, 'pair', [(0, 1), (1, 0)])]
    ppermute x2 -> x4, starting transfers between devices: 23.2 us -> 23.8 us  [on_device(): got_half = lax.ppermute(sent, 'pair', [(0, 1), (1, 0)])]
  transfers between devices with their start and end apart: 4 -> 8, of which waited for: 4 -> 8; matrix products, arithmetic and copies ran while one was open for 5% -> 9% of each run, Pallas kernels for 0% -> 0%
where the time goes in v10:
time: 273 us; the launch traced here: 272 us
  waiting for transfers between devices  118 us (43%)
  Pallas kernels  68.2 us (25%)
  matrix products  30.3 us (11%)
  starting transfers between devices  24.1 us (9%)
  between operations  13.9 us (5%)
  local copies, waits for them, and re-layouts  10.2 us (4%)
  other arithmetic  7.37 us (3%)
    reduce_scatter x4, waiting for transfers between devices, on_device(): lax.psum_scatter(kept + got_half, 'batch', scatter_dimension=0, tiled=True)  102 us
    pallas_call x1, Pallas kernels, dispatch(): pl.pallas_call(functools.partial(dispatch_kernel, npair, nb, nv, span), o...  45.6 us
    ppermute x4, starting transfers between devices, on_device(): got_half = lax.ppermute(sent, 'pair', [(0, 1), (1, 0)])  23.8 us
    pallas_call x2, Pallas kernels, vocab_gather(): pl.pallas_call(functools.partial(gather_kernel, nv), out_shape=jax.ShapeD...  22.6 us
    dot_general x4, matrix products, on_device(): kept = jnp.dot(mine, w, preferred_element_type=jnp.float32)  17.4 us
    ppermute x4, waiting for transfers between devices, on_device(): got_half = lax.ppermute(sent, 'pair', [(0, 1), (1, 0)])  15.6 us
    dot_general x4, matrix products, on_device(): sent = jnp.dot(theirs, w, preferred_element_type=jnp.float32)  12.9 us
  transfers between devices with their start and end apart: 8, of which 8 were waited for; matrix products, arithmetic and copies ran while one was open for 9% of the time, Pallas kernels for 0%

profile of v10, /device:TPU:0, one launch (start us, length us, event | category | flops | bytes accessed | tf_op | source)
XLA Modules:
  0.0 272.0 jit_solution(17348713743233483511)
XLA Ops:
  8.8 11.9 %shard_map.50 = f32[16,8,128]{2,1,0:T(8,128)} custom-call(f32[8,128]{1,0:T(8,128)} %scatter.6.src_ref), custom_call_target="tpu_custom_call" | custom-call | bytes 131072 | tf_op jit(solution)/shard_map/pallas_call | solution.py:151
  22.3 1.7 fusion.39.src_ref
  23.9 45.6 %shard_map.51 = bf16[16,128,512]{2,1,0:T(8,128)(2,1)} custom-call(bf16[128,512]{1,0:T(8,128)(2,1)} %fusion.39.src_ref), custom_call_target="tpu_custom_call" | custom-call | bytes 4194304 | tf_op jit(solution)/shard_map/pallas_call | solution.py:100
  69.5 3.8 %copy.7 = bf16[2,4,2,2,64,512]{5,2,4,0,3,1:T(2,128)(2,1)S(1)} copy(bf16[2,4,2,2,64,512]{5,4,3,2,1,0:T(8,128)(2,1)} %bitcast.22) | data formatting | bytes 4194304 | tf_op jit(solution)/shard_map/reshape | solution.py:177
  73.8 4.2 %fusion.12 = f32[512,1024]{1,0:T(8,128)} fusion(bf16[1024,4096]{1,0:T(8,128)(2,1)} %param.9, bf16[1024,1024]{1,0:T(8,128)(2,1)S(1)} %bitcast.24, s32[]{:T(128)S(6)} %select_n.7), kind=kOutput, calls=%fused_computation.12 | convolution fusion | flops 1073741824 | bytes 5242884 | tf_op jit(solution)/shard_map/dot_general | solution.py:189
  78.0 22.5 %collective-permute-start = (f32[512,1024]{1,0:T(8,128)}, f32[512,1024]{1,0:T(8,128)}, u32[]{:S(2)}, u32[]{:S(2)}) collective-permute-start(f32[512,1024]{1,0:T(8,128)} %fusion.12), channel_id=1, source_target_pairs={{0,64},{64,0},{1,65},{65,1},{2,66},{66,2},{3,67},{67,3},{4,68},{68... | collective-permute-start | bytes 6291464 | tf_op jit(solution)/shard_map/ppermute | solution.py:191
  100.6 4.1 %collective-permute-done = f32[512,1024]{1,0:T(8,128)} collective-permute-done((f32[512,1024]{1,0:T(8,128)}, f32[512,1024]{1,0:T(8,128)}, u32[]{:S(2)}, u32[]{:S(2)}) %collective-permute-start) | collective-permute-done | bytes 2097184 | tf_op jit(solution)/shard_map/ppermute | solution.py:191
  104.7 4.8 %fusion.16 = f32[512,1024]{1,0:T(8,128)} fusion(f32[512,1024]{1,0:T(8,128)} %collective-permute-done, bf16[1024,4096]{1,0:T(8,128)(2,1)} %param.9, bf16[1024,1024]{1,0:T(8,128)(2,1)S(1)} %bitcast.25, s32[]{:T(128)S(6)} %select_n.6), kind=kOutput, calls=%fused_computation.16 | convolution fusion | flops 1074266112 | bytes 7340036 | tf_op jit(solution)/shard_map/dot_general | solution.py:190
  109.6 2.8 %fusion.8 = f32[512,1024]{1,0:T(8,128)S(1)} fusion(bf16[1024,4096]{1,0:T(8,128)(2,1)} %param.9, bf16[1024,1024]{1,0:T(8,128)(2,1)S(1)} %bitcast.26, s32[]{:T(128)S(6)} %select_n.7), kind=kOutput, calls=%fused_computation.8 | convolution fusion | flops 1073741824 | bytes 5242884 | tf_op jit(solution)/shard_map/dot_general | solution.py:189
  112.9 3.8 %collective-permute-done.1 = f32[512,1024]{1,0:T(8,128)S(1)} collective-permute-done((f32[512,1024]{1,0:T(8,128)S(1)}, f32[512,1024]{1,0:T(8,128)S(1)}, u32[]{:S(2)}, u32[]{:S(2)}) %collective-permute-start.1) | collective-permute-done | bytes 2097184 | tf_op jit(solution)/shard_map/ppermute | solution.py:191
  116.7 4.2 %fusion.19 = f32[512,1024]{1,0:T(8,128)} fusion(f32[512,1024]{1,0:T(8,128)S(1)} %collective-permute-done.1, bf16[1024,4096]{1,0:T(8,128)(2,1)} %param.9, bf16[1024,1024]{1,0:T(8,128)(2,1)S(1)} %bitcast.27, s32[]{:T(128)S(6)} %select_n.6), kind=kOutput, calls=%fused_computation.17 | convolution fusion | flops 1074266112 | bytes 7340036 | tf_op jit(solution)/shard_map/dot_general | solution.py:190
  120.9 2.8 %fusion.4 = f32[512,1024]{1,0:T(8,128)S(1)} fusion(bf16[1024,4096]{1,0:T(8,128)(2,1)} %param.9, bf16[1024,1024]{1,0:T(8,128)(2,1)S(1)} %bitcast.28, s32[]{:T(128)S(6)} %select_n.7), kind=kOutput, calls=%fused_computation.4 | convolution fusion | flops 1073741824 | bytes 5242884 | tf_op jit(solution)/shard_map/dot_general | solution.py:189
  124.2 3.8 %collective-permute-done.2 = f32[512,1024]{1,0:T(8,128)S(1)} collective-permute-done((f32[512,1024]{1,0:T(8,128)S(1)}, f32[512,1024]{1,0:T(8,128)S(1)}, u32[]{:S(2)}, u32[]{:S(2)}) %collective-permute-start.2) | collective-permute-done | bytes 2097184 | tf_op jit(solution)/shard_map/ppermute | solution.py:191
  128.0 4.2 %fusion.22 = f32[512,1024]{1,0:T(8,128)} fusion(f32[512,1024]{1,0:T(8,128)S(1)} %collective-permute-done.2, bf16[1024,4096]{1,0:T(8,128)(2,1)} %param.9, bf16[1024,1024]{1,0:T(8,128)(2,1)S(1)} %bitcast.29, s32[]{:T(128)S(6)} %select_n.6), kind=kOutput, calls=%fused_computation.18 | convolution fusion | flops 1074266112 | bytes 7340036 | tf_op jit(solution)/shard_map/dot_general | solution.py:190
  132.5 3.0 %fusion = f32[512,1024]{1,0:T(8,128)S(1)} fusion(bf16[1024,4096]{1,0:T(8,128)(2,1)} %param.9, bf16[1024,1024]{1,0:T(8,128)(2,1)S(1)} %bitcast.30, s32[]{:T(128)S(6)} %select_n.7), kind=kOutput, calls=%fused_computation | convolution fusion | flops 1073741824 | bytes 5242884 | tf_op jit(solution)/shard_map/dot_general | solution.py:189
  135.8 3.9 %collective-permute-done.3 = f32[512,1024]{1,0:T(8,128)S(1)} collective-permute-done((f32[512,1024]{1,0:T(8,128)S(1)}, f32[512,1024]{1,0:T(8,128)S(1)}, u32[]{:S(2)}, u32[]{:S(2)}) %collective-permute-start.3) | collective-permute-done | bytes 2097184 | tf_op jit(solution)/shard_map/ppermute | solution.py:191
  139.7 4.2 %fusion.25 = f32[512,1024]{1,0:T(8,128)} fusion(f32[512,1024]{1,0:T(8,128)S(1)} %collective-permute-done.3, bf16[1024,4096]{1,0:T(8,128)(2,1)} %param.9, bf16[1024,1024]{1,0:T(8,128)(2,1)S(1)} %bitcast.31, s32[]{:T(128)S(6)} %select_n.6), kind=kOutput, calls=%fused_computation.19 | convolution fusion | flops 1074266112 | bytes 7340036 | tf_op jit(solution)/shard_map/dot_general | solution.py:190
  144.0 9.8 %reduce-scatter.5.cloned.1.call-done = f32[128,1024]{1,0:T(8,128)} async-done(((f32[512,1024]{1,0:T(8,128)}), f32[128,1024]{1,0:T(8,128)}) %reduce-scatter.5.cloned.1.call-update) | async-done | bytes 524304 | tf_op jit(solution)/shard_map/reduce_scatter | solution.py:192
  154.9 30.9 %reduce-scatter.7.cloned.1.call-done = f32[128,1024]{1,0:T(8,128)} async-done(((f32[512,1024]{1,0:T(8,128)}), f32[128,1024]{1,0:T(8,128)}) %reduce-scatter.7.cloned.1.call-update) | async-done | bytes 524304 | tf_op jit(solution)/shard_map/reduce_scatter | solution.py:192
  186.9 30.7 %reduce-scatter.9.cloned.1.call-done = f32[128,1024]{1,0:T(8,128)} async-done(((f32[512,1024]{1,0:T(8,128)}), f32[128,1024]{1,0:T(8,128)}) %reduce-scatter.9.cloned.1.call-update) | async-done | bytes 524304 | tf_op jit(solution)/shard_map/reduce_scatter | solution.py:192
  217.6 1.1 constant_dynamic-update-slice_fusion.1
  218.7 30.7 %reduce-scatter.11.cloned.1.call-done = f32[128,1024]{1,0:T(8,128)} async-done(((f32[512,1024]{1,0:T(8,128)}), f32[128,1024]{1,0:T(8,128)}) %reduce-scatter.11.cloned.1.call-update) | async-done | bytes 524304 | tf_op jit(solution)/shard_map/reduce_scatter | solution.py:192
  252.0 10.8 %shard_map.52 = f32[16,8,128]{2,1,0:T(8,128)} custom-call(f32[8,128]{1,0:T(8,128)} %select_maximum_fusion.src_ref), custom_call_target="tpu_custom_call" | custom-call | bytes 131072 | tf_op jit(solution)/shard_map/pallas_call | solution.py:151
  263.9 1.6 slice_subtract_fusion
  (29 shorter events, 11.2 us)
Async XLA Ops:
  7.2 146.7 %reduce-scatter.5.cloned.1.call-start = ((), (), s32[]{:S(2)}) async-start(), calls=%async_computation.4 | async-start | bytes 2621440 | tf_op jit(solution)/shard_map/reduce_scatter | solution.py:192
  78.0 26.6 %collective-permute-start = (f32[512,1024]{1,0:T(8,128)}, f32[512,1024]{1,0:T(8,128)}, u32[]{:S(2)}, u32[]{:S(2)}) collective-permute-start(f32[512,1024]{1,0:T(8,128)} %fusion.12), channel_id=1, source_target_pairs={{0,64},{64,0},{1,65},{65,1},{2,66},{66,2},{3,67},{67,3},{4,68},{68... | collective-permute-start | bytes 6291464 | tf_op jit(solution)/shard_map/ppermute | solution.py:191
  109.6 76.2 %reduce-scatter.7.cloned.1.call-start = ((), (), s32[]{:S(2)}) async-start(), calls=%async_computation.5 | async-start | bytes 2621440 | tf_op jit(solution)/shard_map/reduce_scatter | solution.py:192
  112.5 4.2 %collective-permute-start.1 = (f32[512,1024]{1,0:T(8,128)S(1)}, f32[512,1024]{1,0:T(8,128)S(1)}, u32[]{:S(2)}, u32[]{:S(2)}) collective-permute-start(f32[512,1024]{1,0:T(8,128)S(1)} %fusion.8), channel_id=1, source_target_pairs={{0,64},{64,0},{1,65},{65,1},{2,66},{66,2},{3,67},{67,3},{4,68},{68... | collective-permute-start | bytes 6291464 | tf_op jit(solution)/shard_map/ppermute | solution.py:191
  120.9 96.7 %reduce-scatter.9.cloned.1.call-start = ((), (), s32[]{:S(2)}) async-start(), calls=%async_computation.6 | async-start | bytes 2621440 | tf_op jit(solution)/shard_map/reduce_scatter | solution.py:192
  123.8 4.2 %collective-permute-start.2 = (f32[512,1024]{1,0:T(8,128)S(1)}, f32[512,1024]{1,0:T(8,128)S(1)}, u32[]{:S(2)}, u32[]{:S(2)}) collective-permute-start(f32[512,1024]{1,0:T(8,128)S(1)} %fusion.4), channel_id=1, source_target_pairs={{0,64},{64,0},{1,65},{65,1},{2,66},{66,2},{3,67},{67,3},{4,68},{68... | collective-permute-start | bytes 6291464 | tf_op jit(solution)/shard_map/ppermute | solution.py:191
  132.2 117.2 %reduce-scatter.11.cloned.1.call-start = ((), (), s32[]{:S(2)}) async-start(), calls=%async_computation.7 | async-start | bytes 2621440 | tf_op jit(solution)/shard_map/reduce_scatter | solution.py:192
  135.5 4.2 %collective-permute-start.3 = (f32[512,1024]{1,0:T(8,128)S(1)}, f32[512,1024]{1,0:T(8,128)S(1)}, u32[]{:S(2)}, u32[]{:S(2)}) collective-permute-start(f32[512,1024]{1,0:T(8,128)S(1)} %fusion), channel_id=1, source_target_pairs={{0,64},{64,0},{1,65},{65,1},{2,66},{66,2},{3,67},{67,3},{4,68},{68... | collective-permute-start | bytes 6291464 | tf_op jit(solution)/shard_map/ppermute | solution.py:191
Sparse Core Ops, SparseCore 0:
  109.7 44.0 reduce-scatter.4
  156.3 29.4 reduce-scatter.6
  188.2 29.3 reduce-scatter.8
  220.0 29.3 reduce-scatter.10

commit v11 on v10

--- a/solution.py
+++ b/solution.py
@@ -11,7 +11,7 @@
 
 EPS = 1e-05
 GUIDE = 1.5
-CHUNKS = 4
+CHUNKS = 1
 
 
 def dispatch_kernel(npair, nb, nv, span, src_ref, out_ref, send_sems, recv_sems):

time: 273 us -> 253 us (0.927)
  waiting for transfers between devices: 118 us -> 108 us
  matrix products: 30.3 us -> 21.4 us
  other arithmetic: 7.37 us -> 12 us
  local copies, waits for them, and re-layouts: 10.2 us -> 5.92 us
    reduce_scatter x4 -> x1, waiting for transfers between devices: 102 us -> 95.1 us  [on_device(): lax.psum_scatter(kept + got_half, 'batch', scatter_dimension=0, tiled=True)]
    dot_general x4 -> x1, matrix products: 17.4 us -> 11.4 us  [on_device(): kept = jnp.dot(mine, w, preferred_element_type=jnp.float32)]
    unnamed x4 -> x1, local copies, waits for them, and re-layouts: 3.79 us -> 0.56 us
    dot_general x4 -> x1, matrix products: 12.9 us -> 10 us  [on_device(): sent = jnp.dot(theirs, w, preferred_element_type=jnp.float32)]
    ppermute x4 -> x1, waiting for transfers between devices: 15.6 us -> 13.1 us  [on_device(): got_half = lax.ppermute(sent, 'pair', [(0, 1), (1, 0)])]
    ppermute x4 -> x1, starting transfers between devices: 23.8 us -> 22.5 us  [on_device(): got_half = lax.ppermute(sent, 'pair', [(0, 1), (1, 0)])]
  transfers between devices with their start and end apart: 8 -> 2, of which waited for: 8 -> 2; matrix products, arithmetic and copies ran while one was open for 9% -> 0% of each run, Pallas kernels for 0% -> 0%
where the time goes in v11:
time: 253 us; the launch traced here: 252 us
  waiting for transfers between devices  108 us (43%)
  Pallas kernels  68.2 us (27%)
  starting transfers between devices  22.6 us (9%)
  matrix products  21.4 us (8%)
  between operations  14.1 us (6%)
  other arithmetic  12 us (5%)
  local copies, waits for them, and re-layouts  5.92 us (2%)
    reduce_scatter x1, waiting for transfers between devices, on_device(): lax.psum_scatter(kept + got_half, 'batch', scatter_dimension=0, tiled=True)  95.1 us
    pallas_call x1, Pallas kernels, dispatch(): pl.pallas_call(functools.partial(dispatch_kernel, npair, nb, nv, span), o...  45.6 us
    pallas_call x2, Pallas kernels, vocab_gather(): pl.pallas_call(functools.partial(gather_kernel, nv), out_shape=jax.ShapeD...  22.6 us
    ppermute x1, starting transfers between devices, on_device(): got_half = lax.ppermute(sent, 'pair', [(0, 1), (1, 0)])  22.5 us
    ppermute x1, waiting for transfers between devices, on_device(): got_half = lax.ppermute(sent, 'pair', [(0, 1), (1, 0)])  13.1 us
    dot_general x1, matrix products, on_device(): kept = jnp.dot(mine, w, preferred_element_type=jnp.float32)  11.4 us
    dot_general x1, matrix products, on_device(): sent = jnp.dot(theirs, w, preferred_element_type=jnp.float32)  10 us
  transfers between devices with their start and end apart: 2, of which 2 were waited for; matrix products, arithmetic and copies ran while one was open for 0% of the time, Pallas kernels for 0%

profile of v11, /device:TPU:0, one launch (start us, length us, event | category | flops | bytes accessed | tf_op | source)
XLA Modules:
  0.0 252.4 jit_solution(18344993017364669892)
XLA Ops:
  7.2 0.0 reduce-scatter.2.cloned.1.call-start
  7.2 1.0 fusion.4
  8.2 0.7 convert_element_type.14
  8.9 0.6 scatter.6.src_ref
  9.5 11.9 %shard_map.50 = f32[16,8,128]{2,1,0:T(8,128)} custom-call(f32[8,128]{1,0:T(8,128)} %scatter.6.src_ref), custom_call_target="tpu_custom_call" | custom-call | bytes 131072 | tf_op jit(solution)/shard_map/pallas_call | solution.py:151
  21.4 0.9 slice_reduce_fusion.1
  22.3 1.7 fusion.6.src_ref
  23.9 45.6 %shard_map.51 = bf16[16,128,512]{2,1,0:T(8,128)(2,1)} custom-call(bf16[128,512]{1,0:T(8,128)(2,1)} %fusion.6.src_ref), custom_call_target="tpu_custom_call" | custom-call | bytes 4194304 | tf_op jit(solution)/shard_map/pallas_call | solution.py:100
  69.5 3.8 %copy.7 = bf16[2,4,2,2,64,512]{5,2,4,0,3,1:T(2,128)(2,1)S(1)} copy(bf16[2,4,2,2,64,512]{5,4,3,2,1,0:T(8,128)(2,1)} %bitcast.24) | data formatting | bytes 4194304 | tf_op jit(solution)/shard_map/reshape | solution.py:177
  73.3 0.6 copy.12
  73.8 10.0 %fusion.1 = f32[512,4096]{1,0:T(8,128)} fusion(bf16[1024,4096]{1,0:T(8,128)(2,1)} %param.9, bf16[1024,1024]{1,0:T(8,128)(2,1)S(1)} %bitcast.26, s32[]{:T(128)S(6)} %select_n.7), kind=kOutput, calls=%fused_computation.5 | convolution fusion | flops 4294967296 | bytes 17825796 | tf_op jit(solution)/shard_map/dot_general | solution.py:189
  83.9 22.5 %collective-permute-start = (f32[512,4096]{1,0:T(8,128)}, f32[512,4096]{1,0:T(8,128)}, u32[]{:S(2)}, u32[]{:S(2)}) collective-permute-start(f32[512,4096]{1,0:T(8,128)} %fusion.1), channel_id=1, source_target_pairs={{0,64},{64,0},{1,65},{65,1},{2,66},{66,2},{3,67},{67,3},{4,68},{68... | collective-permute-start | bytes 25165832 | tf_op jit(solution)/shard_map/ppermute | solution.py:191
  106.4 13.1 %collective-permute-done = f32[512,4096]{1,0:T(8,128)} collective-permute-done((f32[512,4096]{1,0:T(8,128)}, f32[512,4096]{1,0:T(8,128)}, u32[]{:S(2)}, u32[]{:S(2)}) %collective-permute-start) | collective-permute-done | bytes 8388640 | tf_op jit(solution)/shard_map/ppermute | solution.py:191
  119.5 11.4 %convolution_add_fusion = f32[512,4096]{1,0:T(8,128)} fusion(f32[512,4096]{1,0:T(8,128)} %collective-permute-done, bf16[1024,4096]{1,0:T(8,128)(2,1)} %param.9, bf16[1024,1024]{1,0:T(8,128)(2,1)S(1)} %bitcast.27, s32[]{:T(128)S(6)} %select_n.6), kind=kOutput, calls=%fused_computation | convolution fusion | flops 4297064448 | bytes 26214404 | tf_op jit(solution)/shard_map/dot_general | solution.py:190
  130.9 0.0 reduce-scatter.2.cloned.1.call-update
  130.9 95.1 %reduce-scatter.2.cloned.1.call-done = f32[128,4096]{1,0:T(8,128)} async-done(((f32[512,4096]{1,0:T(8,128)}), f32[128,4096]{1,0:T(8,128)}) %reduce-scatter.2.cloned.1.call-update) | async-done | bytes 2097168 | tf_op jit(solution)/shard_map/reduce_scatter | solution.py:192
  226.0 1.8 slice_reduce_fusion
  227.8 2.1 exponential_reduce_fusion.1
  229.9 0.6 select_maximum_fusion.src_ref
  230.5 10.8 %shard_map.52 = f32[16,8,128]{2,1,0:T(8,128)} custom-call(f32[8,128]{1,0:T(8,128)} %select_maximum_fusion.src_ref), custom_call_target="tpu_custom_call" | custom-call | bytes 131072 | tf_op jit(solution)/shard_map/pallas_call | solution.py:151
  241.3 1.0 fusion.10
  242.4 3.1 %slice_subtract_fusion = (f32[64,4096]{1,0:T(8,128)}, f32[64,4096]{1,0:T(8,128)}) fusion(f32[128,4096]{1,0:T(8,128)} %reduce-scatter.2.cloned.1.call-done, f32[64]{0:T(128)S(1)} %get-tuple-element.36, f32[64]{0:T(128)S(1)} %get-tuple-element.37), kind=kLoop, calls=%fused_computation.8 | loop fusion | flops 1310720 | bytes 4194816 | tf_op jit(solution)/shard_map/sub | solution.py:208
  (6 shorter events, 0.1 us)
Async XLA Ops:
  7.2 218.9 %reduce-scatter.2.cloned.1.call-start = ((), (), s32[]{:S(2)}) async-start(), calls=%async_computation.1 | async-start | bytes 10485760 | tf_op jit(solution)/shard_map/reduce_scatter | solution.py:192
  83.9 35.6 %collective-permute-start = (f32[512,4096]{1,0:T(8,128)}, f32[512,4096]{1,0:T(8,128)}, u32[]{:S(2)}, u32[]{:S(2)}) collective-permute-start(f32[512,4096]{1,0:T(8,128)} %fusion.1), channel_id=1, source_target_pairs={{0,64},{64,0},{1,65},{65,1},{2,66},{66,2},{3,67},{67,3},{4,68},{68... | collective-permute-start | bytes 25165832 | tf_op jit(solution)/shard_map/ppermute | solution.py:191
Sparse Core Ops, SparseCore 0:
  131.1 94.9 reduce-scatter.1

commit v12 on v7

--- a/solution.py
+++ b/solution.py
@@ -159,24 +159,95 @@
     )(block)
 
 
+def scatter_kernel(npair, nb, src_ref, out_ref, send_sems, recv_sems):
+    beta = lax.axis_index("pair")
+    b = lax.axis_index("batch")
+    v = lax.axis_index("vocab")
+    groups = npair * nb
+    me = beta * nb + b
+    rows = out_ref.shape[3]
+    depth = out_ref.shape[4]
+    barrier = pltpu.get_barrier_semaphore()
+    for k in range(1, groups):
+        t = (me + k) % groups
+        pl.semaphore_signal(barrier, inc=1, device_id=(t // nb, t % nb, v), device_id_type=MESH)
+    pl.semaphore_wait(barrier, groups - 1)
+
+    def piece(t, h):
+        return src_ref.at[pl.ds(h * rows, rows), pl.ds(pl.multiple_of(t * depth, depth), depth)]
+
+    def remote(k, h):
+        t = (me + k) % groups
+        return pltpu.make_async_remote_copy(
+            src_ref=piece(t, h),
+            dst_ref=out_ref.at[b, h, beta],
+            send_sem=send_sems.at[k * 2 + h],
+            recv_sem=recv_sems.at[(b * 2 + h) * npair + beta],
+            device_id=(t // nb, t % nb, v),
+            device_id_type=MESH,
+        )
+
+    def local(h):
+        return pltpu.make_async_copy(
+            piece(me, h), out_ref.at[b, h, beta], recv_sems.at[(b * 2 + h) * npair + beta])
+
+    for k in range(1, groups):
+        for h in range(2):
+            remote(k, h).start()
+    for h in range(2):
+        local(h).start()
+    for k in range(1, groups):
+        for h in range(2):
+            remote(k, h).wait_send()
+    for k in range(1, groups):
+        s = (me + k) % groups
+        sp, sb = s // nb, s % nb
+        for h in range(2):
+            pltpu.make_async_remote_copy(
+                src_ref=piece(me, h),
+                dst_ref=out_ref.at[sb, h, sp],
+                send_sem=send_sems.at[0],
+                recv_sem=recv_sems.at[(sb * 2 + h) * npair + sp],
+                device_id=(sp, sb, v),
+                device_id_type=MESH,
+            ).wait_recv()
+    for h in range(2):
+        local(h).wait()
+
+
+def kblock_scatter(feats, npair, nb):
+    groups = npair * nb
+    rows = feats.shape[0] // 2
+    depth = feats.shape[1] // groups
+    size = feats.size * feats.dtype.itemsize
+    return pl.pallas_call(
+        functools.partial(scatter_kernel, npair, nb),
+        out_shape=jax.ShapeDtypeStruct((nb, 2, npair, rows, depth), feats.dtype),
+        in_specs=[pl.BlockSpec(memory_space=pltpu.VMEM)],
+        out_specs=pl.BlockSpec(memory_space=pltpu.VMEM),
+        scratch_shapes=[pltpu.SemaphoreType.DMA((2 * groups,)), pltpu.SemaphoreType.DMA((2 * groups,))],
+        compiler_params=pltpu.CompilerParams(collective_id=0, has_side_effects=True),
+        cost_estimate=pl.CostEstimate(flops=0, transcendentals=0, bytes_accessed=2 * size),
+    )(feats)
+
+
 def on_device(npair, nb, nv, hidden, norm_gain, head_weight):
     groups = npair * nb
     span = nv // groups
     local_rows, width = hidden.shape[1], hidden.shape[2]
     total_d = width * nv
-    wide = hidden[0].astype(jnp.float32)
-    part = jnp.sum(wide * wide, axis=1)
+    pad = jnp.zeros((15, width), hidden.dtype)
+    block = jnp.concatenate([hidden[0], norm_gain[None, :], pad], axis=0)
+    got = vocab_gather(block, nv, 1)
+    wide = got[:, :local_rows, :].transpose(1, 0, 2).reshape(local_rows, total_d).astype(jnp.float32)
+    gain = got[:, local_rows, :].reshape(total_d)
+    meansq = jnp.sum(wide * wide, axis=1) / total_d
+    scaled = wide * lax.rsqrt(meansq + EPS)[:, None] * gain.astype(jnp.float32)[None, :]
+    features = scaled.astype(jnp.bfloat16)
+    ordered = kblock_scatter(features, npair, nb).reshape(groups * local_rows, total_d // groups)
+    half = local_rows // 2
+    out_rows = half
     lanes = 128
-    part_block = jnp.zeros((8, local_rows), jnp.float32).at[0].set(part)
-    parts = vocab_gather(part_block, nv, 1)
-    meansq = jnp.sum(parts[:, 0, :], axis=0) / total_d
-    scaled = wide * lax.rsqrt(meansq + EPS)[:, None] * norm_gain.astype(jnp.float32)[None, :]
-    features = scaled.astype(jnp.bfloat16)
-    got = dispatch(features, npair, nb, nv)
-    half = local_rows // 2
-    raw = got.reshape(npair, nb, span, 2, half, width).transpose(1, 3, 0, 4, 2, 5)
-    ordered = raw.reshape(groups * npair * half, span * width)
-    out_rows = half
     me = lax.axis_index("pair")
     half_rows = ordered.shape[0] // 2
     mine = lax.dynamic_slice_in_dim(ordered, me * half_rows, half_rows, axis=0)

time: 252 us -> 243 us (0.964)
  starting transfers between devices: 23.2 us -> 0.3 us
  Pallas kernels: 68.2 us -> 86.9 us
  waiting for transfers between devices: 105 us -> 96.4 us
  other arithmetic: 7.37 us -> 11.4 us
    pallas_call x2, Pallas kernels: 22.6 us -> 55.7 us  [vocab_gather(): pl.pallas_call(functools.partial(gather_kernel, nv), out_shape=jax.ShapeD...]
    ppermute x2, starting transfers between devices: 23.2 us -> 0.22 us  [on_device(): got_half = lax.ppermute(sent, 'pair', [(0, 1), (1, 0)])]
    pallas_call x1, Pallas kernels: 45.6 us -> 31.2 us  [kblock_scatter(): pl.pallas_call(functools.partial(scatter_kernel, npair, nb), out_shape=ja...]
    reduce_scatter x2, waiting for transfers between devices: 90.7 us -> 81.9 us  [on_device(): lax.psum_scatter(kept + got_half, 'batch', scatter_dimension=0, tiled=True)]
    unnamed x0 -> x1, other arithmetic: none -> 4.24 us
    reshape x1 -> x0, local copies, waits for them, and re-layouts: 3.75 us -> none  [on_device(): got.reshape(npair, nb, span, 2, half, width).transpose(1, 3, 0, 4, 2, 5)]
    convert_element_type x0 -> x1, local copies, waits for them, and re-layouts: none -> 2.82 us  [on_device(): got[:, :local_rows, :].transpose(1, 0, 2).reshape(local_rows, total_d)]
where the time goes in v12:
time: 243 us; the launch traced here: 242 us
  waiting for transfers between devices  96.4 us (40%)
  Pallas kernels  86.9 us (36%)
  matrix products  25.7 us (11%)
  between operations  14.1 us (6%)
  other arithmetic  11.4 us (5%)
  local copies, waits for them, and re-layouts  7.19 us (3%)
    reduce_scatter x2, waiting for transfers between devices, on_device(): lax.psum_scatter(kept + got_half, 'batch', scatter_dimension=0, tiled=True)  81.9 us
    pallas_call x2, Pallas kernels, vocab_gather(): pl.pallas_call(functools.partial(gather_kernel, nv), out_shape=jax.ShapeD...  55.7 us
    pallas_call x1, Pallas kernels, kblock_scatter(): pl.pallas_call(functools.partial(scatter_kernel, npair, nb), out_shape=ja...  31.2 us
    ppermute x2, waiting for transfers between devices, on_device(): got_half = lax.ppermute(sent, 'pair', [(0, 1), (1, 0)])  14.5 us
    dot_general x2, matrix products, on_device(): kept = jnp.dot(mine, w, preferred_element_type=jnp.float32)  14.2 us
    dot_general x2, matrix products, on_device(): sent = jnp.dot(theirs, w, preferred_element_type=jnp.float32)  11.4 us
  transfers between devices with their start and end apart: 4, of which 4 were waited for; matrix products, arithmetic and copies ran while one was open for 5% of the time, Pallas kernels for 0%

profile of v12, /device:TPU:0, one launch (start us, length us, event | category | flops | bytes accessed | tf_op | source)
XLA Modules:
  0.0 242.0 jit_solution(17546249153105617894)
XLA Ops:
  7.2 0.7 broadcast_in_dim.4
  8.0 1.7 maximum_maximum_fusion.src_ref
  9.6 44.9 %shard_map.50 = bf16[16,144,512]{2,1,0:T(8,128)(2,1)} custom-call(bf16[144,512]{1,0:T(8,128)(2,1)} %maximum_maximum_fusion.src_ref), custom_call_target="tpu_custom_call" | custom-call | bytes 4718592 | tf_op jit(solution)/shard_map/pallas_call | solution.py:151
  54.5 4.2 %convert_bitcast_fusion = f32[16,16,8,512]{3,2,1,0:T(8,128)} fusion(bf16[16,144,512]{2,1,0:T(8,128)(2,1)} %shard_map.50), kind=kLoop, calls=%fused_computation.1 | loop fusion | flops 1048576 | bytes 6291456
  58.8 0.5 fusion
  59.3 2.8 %copy.10 = f32[16,16,8,512]{3,2,0,1:T(8,128)S(1)} copy(f32[16,16,8,512]{3,2,1,0:T(8,128)} %convert_bitcast_fusion) | data formatting | bytes 8388608 | tf_op jit(solution)/shard_map/convert_element_type | solution.py:242
  62.1 1.9 multiply_convert_fusion.src_ref
  64.0 31.2 %shard_map.51 = bf16[4,2,2,64,1024]{4,3,2,1,0:T(8,128)(2,1)} custom-call(bf16[128,8192]{1,0:T(8,128)(2,1)} %multiply_convert_fusion.src_ref), custom_call_target="tpu_custom_call" | custom-call | bytes 4194304 | tf_op jit(solution)/shard_map/pallas_call | solution.py:223
  95.2 6.9 %fusion.5 = f32[512,2048]{1,0:T(8,128)} fusion(bf16[1024,4096]{1,0:T(8,128)(2,1)} %param.7, bf16[1024,1024]{1,0:T(8,128)(2,1)} %bitcast.20, s32[]{:T(128)S(6)} %select_n.7), kind=kOutput, calls=%fused_computation.8 | convolution fusion | flops 2147483648 | bytes 9437188 | tf_op jit(solution)/shard_map/dot_general | solution.py:260
  102.1 7.5 %collective-permute-done = f32[512,2048]{1,0:T(8,128)} collective-permute-done((f32[512,2048]{1,0:T(8,128)}, f32[512,2048]{1,0:T(8,128)}, u32[]{:S(2)}, u32[]{:S(2)}) %collective-permute-start) | collective-permute-done | bytes 4194336 | tf_op jit(solution)/shard_map/ppermute | solution.py:262
  109.6 7.7 %fusion.9 = f32[512,2048]{1,0:T(8,128)} fusion(f32[512,2048]{1,0:T(8,128)} %collective-permute-done, bf16[1024,4096]{1,0:T(8,128)(2,1)} %param.7, bf16[1024,1024]{1,0:T(8,128)(2,1)S(1)} %bitcast.21, s32[]{:T(128)S(6)} %select_n.6), kind=kOutput, calls=%fused_computation.12 | convolution fusion | flops 2148532224 | bytes 13631492 | tf_op jit(solution)/shard_map/dot_general | solution.py:261
  117.5 4.5 %fusion.1 = f32[512,2048]{1,0:T(8,128)S(1)} fusion(bf16[1024,4096]{1,0:T(8,128)(2,1)} %param.7, bf16[1024,1024]{1,0:T(8,128)(2,1)S(1)} %bitcast.22, s32[]{:T(128)S(6)} %select_n.7), kind=kOutput, calls=%fused_computation.4 | convolution fusion | flops 2147483648 | bytes 9437188 | tf_op jit(solution)/shard_map/dot_general | solution.py:260
  122.2 7.0 %collective-permute-done.1 = f32[512,2048]{1,0:T(8,128)S(1)} collective-permute-done((f32[512,2048]{1,0:T(8,128)S(1)}, f32[512,2048]{1,0:T(8,128)S(1)}, u32[]{:S(2)}, u32[]{:S(2)}) %collective-permute-start.1) | collective-permute-done | bytes 4194336 | tf_op jit(solution)/shard_map/ppermute | solution.py:262
  129.2 6.5 %fusion.12 = f32[512,2048]{1,0:T(8,128)} fusion(f32[512,2048]{1,0:T(8,128)S(1)} %collective-permute-done.1, bf16[1024,4096]{1,0:T(8,128)(2,1)} %param.7, bf16[1024,1024]{1,0:T(8,128)(2,1)S(1)} %bitcast.23, s32[]{:T(128)S(6)} %select_n.6), kind=kOutput, calls=%fused_computation.13 | convolution fusion | flops 2148532224 | bytes 13631492 | tf_op jit(solution)/shard_map/dot_general | solution.py:261
  135.7 34.1 %reduce-scatter.3.cloned.1.call-done = f32[128,2048]{1,0:T(8,128)} async-done(((f32[512,2048]{1,0:T(8,128)}), f32[128,2048]{1,0:T(8,128)}) %reduce-scatter.3.cloned.1.call-update) | async-done | bytes 1048592 | tf_op jit(solution)/shard_map/reduce_scatter | solution.py:263
  169.9 1.3 constant_dynamic-update-slice_fusion.1
  171.2 47.8 %reduce-scatter.5.cloned.1.call-done = f32[128,2048]{1,0:T(8,128)} async-done(((f32[512,2048]{1,0:T(8,128)}), f32[128,2048]{1,0:T(8,128)}) %reduce-scatter.5.cloned.1.call-update) | async-done | bytes 1048592 | tf_op jit(solution)/shard_map/reduce_scatter | solution.py:263
  218.9 1.3 constant_dynamic-update-slice_fusion
  220.2 0.3 slice_reduce_fusion
  220.5 0.5 exponential_reduce_fusion.1
  221.1 0.6 select_maximum_fusion.src_ref
  221.7 10.8 %shard_map.52 = f32[16,8,128]{2,1,0:T(8,128)} custom-call(f32[8,128]{1,0:T(8,128)} %select_maximum_fusion.src_ref), custom_call_target="tpu_custom_call" | custom-call | bytes 131072 | tf_op jit(solution)/shard_map/pallas_call | solution.py:151
  232.5 1.0 fusion.25
  233.6 1.6 slice_subtract_fusion
  (19 shorter events, 0.5 us)
Async XLA Ops:
  7.2 162.7 %reduce-scatter.3.cloned.1.call-start = ((), (), s32[]{:S(2)}) async-start(), calls=%async_computation.2 | async-start | bytes 5242880 | tf_op jit(solution)/shard_map/reduce_scatter | solution.py:263
  54.5 4.3 %copy-start = (bf16[16,144,512]{2,1,0:T(8,128)(2,1)S(1)}, bf16[16,144,512]{2,1,0:T(8,128)(2,1)}, u32[]{:S(2)}) copy-start(bf16[16,144,512]{2,1,0:T(8,128)(2,1)} %shard_map.50) | copy-start | bytes 7077892
  95.2 14.4 %copy-start.1 = (bf16[4,2,2,64,1024]{4,3,2,1,0:T(8,128)(2,1)S(1)}, bf16[4,2,2,64,1024]{4,3,2,1,0:T(8,128)(2,1)}, u32[]{:S(2)}) copy-start(bf16[4,2,2,64,1024]{4,3,2,1,0:T(8,128)(2,1)} %shard_map.51) | copy-start | bytes 6291460
  102.1 7.5 %collective-permute-start = (f32[512,2048]{1,0:T(8,128)}, f32[512,2048]{1,0:T(8,128)}, u32[]{:S(2)}, u32[]{:S(2)}) collective-permute-start(f32[512,2048]{1,0:T(8,128)} %fusion.5), channel_id=1, source_target_pairs={{0,64},{64,0},{1,65},{65,1},{2,66},{66,2},{3,67},{67,3},{4,68},{68... | collective-permute-start | bytes 12582920 | tf_op jit(solution)/shard_map/ppermute | solution.py:262
  117.4 101.5 %reduce-scatter.5.cloned.1.call-start = ((), (), s32[]{:S(2)}) async-start(), calls=%async_computation.3 | async-start | bytes 5242880 | tf_op jit(solution)/shard_map/reduce_scatter | solution.py:263
  122.0 7.2 %collective-permute-start.1 = (f32[512,2048]{1,0:T(8,128)S(1)}, f32[512,2048]{1,0:T(8,128)S(1)}, u32[]{:S(2)}, u32[]{:S(2)}) collective-permute-start(f32[512,2048]{1,0:T(8,128)S(1)} %fusion.1), channel_id=1, source_target_pairs={{0,64},{64,0},{1,65},{65,1},{2,66},{66,2},{3,67},{67,3},{4,68},{68... | collective-permute-start | bytes 12582920 | tf_op jit(solution)/shard_map/ppermute | solution.py:262
Sparse Core Ops, SparseCore 0:
  117.5 52.2 reduce-scatter.2
  172.4 46.5 reduce-scatter.4

commit v13 on v12

--- a/solution.py
+++ b/solution.py
@@ -113,10 +113,8 @@
     b = lax.axis_index("batch")
     v = lax.axis_index("vocab")
     barrier = pltpu.get_barrier_semaphore()
-    for w in range(nv):
-        @pl.when(v != w)
-        def _():
-            pl.semaphore_signal(barrier, inc=1, device_id=(beta, b, w), device_id_type=MESH)
+    for k in range(1, nv):
+        pl.semaphore_signal(barrier, inc=1, device_id=(beta, b, (v + k) % nv), device_id_type=MESH)
     pl.semaphore_wait(barrier, nv - 1)
 
     def remote(w, s):
@@ -129,20 +127,15 @@
             device_id_type=MESH,
         )
 
-    for w in range(nv):
-        @pl.when(v != w)
-        def _():
-            remote(w, v).start()
+    for k in range(1, nv):
+        remote((v + k) % nv, v).start()
 
     pltpu.make_async_copy(src_ref, out_ref.at[v], recv_sems.at[v]).start()
-    for w in range(nv):
-        @pl.when(v != w)
-        def _():
-            remote(w, v).wait_send()
-    for s in range(nv):
-        @pl.when(v != s)
-        def _():
-            remote(s, s).wait_recv()
+    for k in range(1, nv):
+        remote((v + k) % nv, v).wait_send()
+    for k in range(1, nv):
+        s = (v + k) % nv
+        remote(s, s).wait_recv()
     pltpu.make_async_copy(src_ref, out_ref.at[v], recv_sems.at[v]).wait()
 
 

time: 243 us -> 242 us (level)
  no operation moved by 1% of the time
where the time goes in v13:
time: 242 us
  waiting for transfers between devices  96.1 us (40%)
  Pallas kernels  87 us (36%)
  matrix products  25.7 us (11%)
  between operations  14.1 us (6%)
  other arithmetic  11.4 us (5%)
  local copies, waits for them, and re-layouts  7.19 us (3%)
    reduce_scatter x2, waiting for transfers between devices, on_device(): lax.psum_scatter(kept + got_half, 'batch', scatter_dimension=0, tiled=True)  81.5 us
    pallas_call x2, Pallas kernels, vocab_gather(): pl.pallas_call(functools.partial(gather_kernel, nv), out_shape=jax.ShapeD...  55.7 us
    pallas_call x1, Pallas kernels, kblock_scatter(): pl.pallas_call(functools.partial(scatter_kernel, npair, nb), out_shape=ja...  31.2 us
    ppermute x2, waiting for transfers between devices, on_device(): got_half = lax.ppermute(sent, 'pair', [(0, 1), (1, 0)])  14.5 us
    dot_general x2, matrix products, on_device(): kept = jnp.dot(mine, w, preferred_element_type=jnp.float32)  14.3 us
    dot_general x2, matrix products, on_device(): sent = jnp.dot(theirs, w, preferred_element_type=jnp.float32)  11.4 us
  transfers between devices with their start and end apart: 4, of which 4 were waited for; matrix products, arithmetic and copies ran while one was open for 5% of the time, Pallas kernels for 0%

profile of v13, /device:TPU:0, one launch (start us, length us, event | category | flops | bytes accessed | tf_op | source)
XLA Modules:
  0.0 242.0 jit_solution(13562090747252462023)
XLA Ops:
  7.2 0.7 broadcast_in_dim.4
  8.0 1.7 maximum_maximum_fusion.src_ref
  9.6 44.9 %shard_map.50 = bf16[16,144,512]{2,1,0:T(8,128)(2,1)} custom-call(bf16[144,512]{1,0:T(8,128)(2,1)} %maximum_maximum_fusion.src_ref), custom_call_target="tpu_custom_call" | custom-call | bytes 4718592 | tf_op jit(solution)/shard_map/pallas_call | solution.py:144
  54.6 4.2 %convert_bitcast_fusion = f32[16,16,8,512]{3,2,1,0:T(8,128)} fusion(bf16[16,144,512]{2,1,0:T(8,128)(2,1)} %shard_map.50), kind=kLoop, calls=%fused_computation.1 | loop fusion | flops 1048576 | bytes 6291456
  58.9 0.5 fusion
  59.4 2.8 %copy.10 = f32[16,16,8,512]{3,2,0,1:T(8,128)S(1)} copy(f32[16,16,8,512]{3,2,1,0:T(8,128)} %convert_bitcast_fusion) | data formatting | bytes 8388608 | tf_op jit(solution)/shard_map/convert_element_type | solution.py:235
  62.2 1.9 multiply_convert_fusion.src_ref
  64.0 31.2 %shard_map.51 = bf16[4,2,2,64,1024]{4,3,2,1,0:T(8,128)(2,1)} custom-call(bf16[128,8192]{1,0:T(8,128)(2,1)} %multiply_convert_fusion.src_ref), custom_call_target="tpu_custom_call" | custom-call | bytes 4194304 | tf_op jit(solution)/shard_map/pallas_call | solution.py:216
  95.3 6.9 %fusion.5 = f32[512,2048]{1,0:T(8,128)} fusion(bf16[1024,4096]{1,0:T(8,128)(2,1)} %param.7, bf16[1024,1024]{1,0:T(8,128)(2,1)} %bitcast.20, s32[]{:T(128)S(6)} %select_n.7), kind=kOutput, calls=%fused_computation.8 | convolution fusion | flops 2147483648 | bytes 9437188 | tf_op jit(solution)/shard_map/dot_general | solution.py:253
  102.2 7.5 %collective-permute-done = f32[512,2048]{1,0:T(8,128)} collective-permute-done((f32[512,2048]{1,0:T(8,128)}, f32[512,2048]{1,0:T(8,128)}, u32[]{:S(2)}, u32[]{:S(2)}) %collective-permute-start) | collective-permute-done | bytes 4194336 | tf_op jit(solution)/shard_map/ppermute | solution.py:255
  109.7 7.7 %fusion.9 = f32[512,2048]{1,0:T(8,128)} fusion(f32[512,2048]{1,0:T(8,128)} %collective-permute-done, bf16[1024,4096]{1,0:T(8,128)(2,1)} %param.7, bf16[1024,1024]{1,0:T(8,128)(2,1)S(1)} %bitcast.21, s32[]{:T(128)S(6)} %select_n.6), kind=kOutput, calls=%fused_computation.12 | convolution fusion | flops 2148532224 | bytes 13631492 | tf_op jit(solution)/shard_map/dot_general | solution.py:254
  117.5 4.5 %fusion.1 = f32[512,2048]{1,0:T(8,128)S(1)} fusion(bf16[1024,4096]{1,0:T(8,128)(2,1)} %param.7, bf16[1024,1024]{1,0:T(8,128)(2,1)S(1)} %bitcast.22, s32[]{:T(128)S(6)} %select_n.7), kind=kOutput, calls=%fused_computation.4 | convolution fusion | flops 2147483648 | bytes 9437188 | tf_op jit(solution)/shard_map/dot_general | solution.py:253
  122.1 0.4 collective-permute-start.1
  122.5 7.0 %collective-permute-done.1 = f32[512,2048]{1,0:T(8,128)S(1)} collective-permute-done((f32[512,2048]{1,0:T(8,128)S(1)}, f32[512,2048]{1,0:T(8,128)S(1)}, u32[]{:S(2)}, u32[]{:S(2)}) %collective-permute-start.1) | collective-permute-done | bytes 4194336 | tf_op jit(solution)/shard_map/ppermute | solution.py:255
  129.5 6.6 %fusion.12 = f32[512,2048]{1,0:T(8,128)} fusion(f32[512,2048]{1,0:T(8,128)S(1)} %collective-permute-done.1, bf16[1024,4096]{1,0:T(8,128)(2,1)} %param.7, bf16[1024,1024]{1,0:T(8,128)(2,1)S(1)} %bitcast.23, s32[]{:T(128)S(6)} %select_n.6), kind=kOutput, calls=%fused_computation.13 | convolution fusion | flops 2148532224 | bytes 13631492 | tf_op jit(solution)/shard_map/dot_general | solution.py:254
  136.1 33.7 %reduce-scatter.3.cloned.1.call-done = f32[128,2048]{1,0:T(8,128)} async-done(((f32[512,2048]{1,0:T(8,128)}), f32[128,2048]{1,0:T(8,128)}) %reduce-scatter.3.cloned.1.call-update) | async-done | bytes 1048592 | tf_op jit(solution)/shard_map/reduce_scatter | solution.py:256
  169.8 1.3 constant_dynamic-update-slice_fusion.1
  171.1 47.8 %reduce-scatter.5.cloned.1.call-done = f32[128,2048]{1,0:T(8,128)} async-done(((f32[512,2048]{1,0:T(8,128)}), f32[128,2048]{1,0:T(8,128)}) %reduce-scatter.5.cloned.1.call-update) | async-done | bytes 1048592 | tf_op jit(solution)/shard_map/reduce_scatter | solution.py:256
  218.9 1.3 constant_dynamic-update-slice_fusion
  220.5 0.5 exponential_reduce_fusion.1
  221.0 0.6 select_maximum_fusion.src_ref
  221.6 10.8 %shard_map.52 = f32[16,8,128]{2,1,0:T(8,128)} custom-call(f32[8,128]{1,0:T(8,128)} %select_maximum_fusion.src_ref), custom_call_target="tpu_custom_call" | custom-call | bytes 131072 | tf_op jit(solution)/shard_map/pallas_call | solution.py:144
  232.4 1.0 fusion.25
  233.5 1.6 slice_subtract_fusion
  (19 shorter events, 0.6 us)
Async XLA Ops:
  7.2 162.6 %reduce-scatter.3.cloned.1.call-start = ((), (), s32[]{:S(2)}) async-start(), calls=%async_computation.2 | async-start | bytes 5242880 | tf_op jit(solution)/shard_map/reduce_scatter | solution.py:256
  54.6 4.3 %copy-start = (bf16[16,144,512]{2,1,0:T(8,128)(2,1)S(1)}, bf16[16,144,512]{2,1,0:T(8,128)(2,1)}, u32[]{:S(2)}) copy-start(bf16[16,144,512]{2,1,0:T(8,128)(2,1)} %shard_map.50) | copy-start | bytes 7077892
  95.3 14.4 %copy-start.1 = (bf16[4,2,2,64,1024]{4,3,2,1,0:T(8,128)(2,1)S(1)}, bf16[4,2,2,64,1024]{4,3,2,1,0:T(8,128)(2,1)}, u32[]{:S(2)}) copy-start(bf16[4,2,2,64,1024]{4,3,2,1,0:T(8,128)(2,1)} %shard_map.51) | copy-start | bytes 6291460
  102.2 7.5 %collective-permute-start = (f32[512,2048]{1,0:T(8,128)}, f32[512,2048]{1,0:T(8,128)}, u32[]{:S(2)}, u32[]{:S(2)}) collective-permute-start(f32[512,2048]{1,0:T(8,128)} %fusion.5), channel_id=1, source_target_pairs={{0,64},{64,0},{1,65},{65,1},{2,66},{66,2},{3,67},{67,3},{4,68},{68... | collective-permute-start | bytes 12582920 | tf_op jit(solution)/shard_map/ppermute | solution.py:255
  117.5 101.4 %reduce-scatter.5.cloned.1.call-start = ((), (), s32[]{:S(2)}) async-start(), calls=%async_computation.3 | async-start | bytes 5242880 | tf_op jit(solution)/shard_map/reduce_scatter | solution.py:256
  122.1 7.4 %collective-permute-start.1 = (f32[512,2048]{1,0:T(8,128)S(1)}, f32[512,2048]{1,0:T(8,128)S(1)}, u32[]{:S(2)}, u32[]{:S(2)}) collective-permute-start(f32[512,2048]{1,0:T(8,128)S(1)} %fusion.1), channel_id=1, source_target_pairs={{0,64},{64,0},{1,65},{65,1},{2,66},{66,2},{3,67},{67,3},{4,68},{68... | collective-permute-start | bytes 12582920 | tf_op jit(solution)/shard_map/ppermute | solution.py:255
Sparse Core Ops, SparseCore 0:
  117.6 52.1 reduce-scatter.2
  172.3 46.5 reduce-scatter.4

commit v14 on v13

--- a/solution.py
+++ b/solution.py
@@ -11,7 +11,6 @@
 
 EPS = 1e-05
 GUIDE = 1.5
-CHUNKS = 2
 
 
 def dispatch_kernel(npair, nb, nv, span, src_ref, out_ref, send_sems, recv_sems):
@@ -246,10 +245,10 @@
     mine = lax.dynamic_slice_in_dim(ordered, me * half_rows, half_rows, axis=0)
     theirs = lax.dynamic_slice_in_dim(ordered, (1 - me) * half_rows, half_rows, axis=0)
     cols = head_weight.shape[1]
-    step = cols // CHUNKS
+    edges = [0, cols // 4, cols]
     pieces = []
-    for j in range(CHUNKS):
-        w = head_weight[:, j * step:(j + 1) * step]
+    for j in range(len(edges) - 1):
+        w = head_weight[:, edges[j]:edges[j + 1]]
         sent = jnp.dot(theirs, w, preferred_element_type=jnp.float32)
         kept = jnp.dot(mine, w, preferred_element_type=jnp.float32)
         got_half = lax.ppermute(sent, "pair", [(0, 1), (1, 0)])

time: 242 us -> 248 us (1.025)
  waiting for transfers between devices: 96.1 us -> 100 us
    reduce_scatter x2, waiting for transfers between devices: 81.5 us -> 91.2 us  [on_device(): lax.psum_scatter(kept + got_half, 'batch', scatter_dimension=0, tiled=True)]
    ppermute x2, waiting for transfers between devices: 14.5 us -> 8.79 us  [on_device(): got_half = lax.ppermute(sent, 'pair', [(0, 1), (1, 0)])]
  transfers between devices with their start and end apart: 4 -> 4, of which waited for: 4 -> 3; matrix products, arithmetic and copies ran while one was open for 5% -> 8% of each run, Pallas kernels for 0% -> 0%
where the time goes in v14:
time: 248 us
  waiting for transfers between devices  100 us (40%)
  Pallas kernels  86.9 us (35%)
  matrix products  27.4 us (11%)
  between operations  14.1 us (6%)
  other arithmetic  11.4 us (5%)
  local copies, waits for them, and re-layouts  7.2 us (3%)
    reduce_scatter x2, waiting for transfers between devices, on_device(): lax.psum_scatter(kept + got_half, 'batch', scatter_dimension=0, tiled=True)  91.2 us
    pallas_call x2, Pallas kernels, vocab_gather(): pl.pallas_call(functools.partial(gather_kernel, nv), out_shape=jax.ShapeD...  55.7 us
    pallas_call x1, Pallas kernels, kblock_scatter(): pl.pallas_call(functools.partial(scatter_kernel, npair, nb), out_shape=ja...  31.2 us
    dot_general x2, matrix products, on_device(): kept = jnp.dot(mine, w, preferred_element_type=jnp.float32)  13.9 us
    dot_general x2, matrix products, on_device(): sent = jnp.dot(theirs, w, preferred_element_type=jnp.float32)  13.5 us
    ppermute x2, waiting for transfers between devices, on_device(): got_half = lax.ppermute(sent, 'pair', [(0, 1), (1, 0)])  8.79 us
  transfers between devices with their start and end apart: 4, of which 3 were waited for; matrix products, arithmetic and copies ran while one was open for 8% of the time, Pallas kernels for 0%

profile of v14, /device:TPU:0, one launch (start us, length us, event | category | flops | bytes accessed | tf_op | source)
XLA Modules:
  0.0 247.7 jit_solution(5775716423149255703)
XLA Ops:
  7.2 0.7 broadcast_in_dim.4
  8.0 1.7 maximum_maximum_fusion.src_ref
  9.6 44.9 %shard_map.50 = bf16[16,144,512]{2,1,0:T(8,128)(2,1)} custom-call(bf16[144,512]{1,0:T(8,128)(2,1)} %maximum_maximum_fusion.src_ref), custom_call_target="tpu_custom_call" | custom-call | bytes 4718592 | tf_op jit(solution)/shard_map/pallas_call | solution.py:143
  54.6 4.2 %convert_bitcast_fusion = f32[16,16,8,512]{3,2,1,0:T(8,128)} fusion(bf16[16,144,512]{2,1,0:T(8,128)(2,1)} %shard_map.50), kind=kLoop, calls=%fused_computation.5 | loop fusion | flops 1048576 | bytes 6291456
  58.9 0.5 fusion.7
  59.4 2.8 %copy.10 = f32[16,16,8,512]{3,2,0,1:T(8,128)S(1)} copy(f32[16,16,8,512]{3,2,1,0:T(8,128)} %convert_bitcast_fusion) | data formatting | bytes 8388608 | tf_op jit(solution)/shard_map/convert_element_type | solution.py:234
  62.2 1.9 multiply_convert_fusion.src_ref
  64.0 31.2 %shard_map.51 = bf16[4,2,2,64,1024]{4,3,2,1,0:T(8,128)(2,1)} custom-call(bf16[128,8192]{1,0:T(8,128)(2,1)} %multiply_convert_fusion.src_ref), custom_call_target="tpu_custom_call" | custom-call | bytes 4194304 | tf_op jit(solution)/shard_map/pallas_call | solution.py:215
  95.3 9.3 %fusion = f32[512,3072]{1,0:T(8,128)} fusion(bf16[1024,4096]{1,0:T(8,128)(2,1)} %param.7, bf16[1024,1024]{1,0:T(8,128)(2,1)} %bitcast.20, s32[]{:T(128)S(6)} %select_n.7), kind=kOutput, calls=%fused_computation | convolution fusion | flops 3221225472 | bytes 13631492 | tf_op jit(solution)/shard_map/dot_general | solution.py:252
  104.6 4.2 %fusion.8 = f32[512,1024]{1,0:T(8,128)} fusion(bf16[1024,4096]{1,0:T(8,128)(2,1)} %param.7, bf16[1024,1024]{1,0:T(8,128)(2,1)S(1)} %bitcast.21, s32[]{:T(128)S(6)} %select_n.7), kind=kOutput, calls=%fused_computation.9 | convolution fusion | flops 1073741824 | bytes 5242884 | tf_op jit(solution)/shard_map/dot_general | solution.py:252
  108.8 0.5 collective-permute-start
  109.3 8.8 %collective-permute-done = f32[512,1024]{1,0:T(8,128)} collective-permute-done((f32[512,1024]{1,0:T(8,128)}, f32[512,1024]{1,0:T(8,128)}, u32[]{:S(2)}, u32[]{:S(2)}) %collective-permute-start) | collective-permute-done | bytes 2097184 | tf_op jit(solution)/shard_map/ppermute | solution.py:254
  118.1 4.8 %fusion.12 = f32[512,1024]{1,0:T(8,128)} fusion(f32[512,1024]{1,0:T(8,128)} %collective-permute-done, bf16[1024,4096]{1,0:T(8,128)(2,1)} %param.7, bf16[1024,1024]{1,0:T(8,128)(2,1)S(1)} %bitcast.22, s32[]{:T(128)S(6)} %select_n.6), kind=kOutput, calls=%fused_computation.13 | convolution fusion | flops 1074266112 | bytes 7340036 | tf_op jit(solution)/shard_map/dot_general | solution.py:253
  123.0 9.0 %fusion.4 = f32[512,3072]{1,0:T(8,128)} fusion(f32[512,3072]{1,0:T(8,128)} %collective-permute-done.1, bf16[1024,4096]{1,0:T(8,128)(2,1)} %param.7, bf16[1024,1024]{1,0:T(8,128)(2,1)S(1)} %bitcast.23, s32[]{:T(128)S(6)} %select_n.6), kind=kOutput, calls=%fused_computation.6 | convolution fusion | flops 3222798336 | bytes 19922948 | tf_op jit(solution)/shard_map/dot_general | solution.py:253
  132.1 26.0 %reduce-scatter.3.cloned.1.call-done = f32[128,1024]{1,0:T(8,128)} async-done(((f32[512,1024]{1,0:T(8,128)}), f32[128,1024]{1,0:T(8,128)}) %reduce-scatter.3.cloned.1.call-update) | async-done | bytes 524304 | tf_op jit(solution)/shard_map/reduce_scatter | solution.py:255
  158.1 1.1 constant_dynamic-update-slice_fusion.1
  159.2 65.2 %reduce-scatter.5.cloned.1.call-done = f32[128,3072]{1,0:T(8,128)} async-done(((f32[512,3072]{1,0:T(8,128)}), f32[128,3072]{1,0:T(8,128)}) %reduce-scatter.5.cloned.1.call-update) | async-done | bytes 1572880 | tf_op jit(solution)/shard_map/reduce_scatter | solution.py:255
  224.4 1.5 constant_dynamic-update-slice_fusion
  225.9 0.3 slice_reduce_fusion
  226.2 0.5 exponential_reduce_fusion.1
  226.7 0.6 select_maximum_fusion.src_ref
  227.3 10.8 %shard_map.52 = f32[16,8,128]{2,1,0:T(8,128)} custom-call(f32[8,128]{1,0:T(8,128)} %select_maximum_fusion.src_ref), custom_call_target="tpu_custom_call" | custom-call | bytes 131072 | tf_op jit(solution)/shard_map/pallas_call | solution.py:143
  238.1 1.0 fusion.25
  239.2 1.6 slice_subtract_fusion
  (19 shorter events, 0.3 us)
Async XLA Ops:
  7.2 150.9 %reduce-scatter.3.cloned.1.call-start = ((), (), s32[]{:S(2)}) async-start(), calls=%async_computation.2 | async-start | bytes 2621440 | tf_op jit(solution)/shard_map/reduce_scatter | solution.py:255
  54.6 4.3 %copy-start = (bf16[16,144,512]{2,1,0:T(8,128)(2,1)S(1)}, bf16[16,144,512]{2,1,0:T(8,128)(2,1)}, u32[]{:S(2)}) copy-start(bf16[16,144,512]{2,1,0:T(8,128)(2,1)} %shard_map.50) | copy-start | bytes 7077892
  95.3 9.3 %copy-start.1 = (bf16[4,2,2,64,1024]{4,3,2,1,0:T(8,128)(2,1)S(1)}, bf16[4,2,2,64,1024]{4,3,2,1,0:T(8,128)(2,1)}, u32[]{:S(2)}) copy-start(bf16[4,2,2,64,1024]{4,3,2,1,0:T(8,128)(2,1)} %shard_map.51) | copy-start | bytes 6291460
  104.6 18.4 %collective-permute-start.1 = (f32[512,3072]{1,0:T(8,128)}, f32[512,3072]{1,0:T(8,128)}, u32[]{:S(2)}, u32[]{:S(2)}) collective-permute-start(f32[512,3072]{1,0:T(8,128)} %fusion), channel_id=1, source_target_pairs={{0,64},{64,0},{1,65},{65,1},{2,66},{66,2},{3,67},{67,3},{4,68},{68... | collective-permute-start | bytes 18874376 | tf_op jit(solution)/shard_map/ppermute | solution.py:254
  108.8 9.3 %collective-permute-start = (f32[512,1024]{1,0:T(8,128)}, f32[512,1024]{1,0:T(8,128)}, u32[]{:S(2)}, u32[]{:S(2)}) collective-permute-start(f32[512,1024]{1,0:T(8,128)} %fusion.8), channel_id=1, source_target_pairs={{0,64},{64,0},{1,65},{65,1},{2,66},{66,2},{3,67},{67,3},{4,68},{68... | collective-permute-start | bytes 6291464 | tf_op jit(solution)/shard_map/ppermute | solution.py:254
  123.0 101.4 %reduce-scatter.5.cloned.1.call-start = ((), (), s32[]{:S(2)}) async-start(), calls=%async_computation.3 | async-start | bytes 7864320 | tf_op jit(solution)/shard_map/reduce_scatter | solution.py:255
Sparse Core Ops, SparseCore 0:
  123.1 34.9 reduce-scatter.2
  160.6 63.6 reduce-scatter.4

commit v15 on v14

--- a/solution.py
+++ b/solution.py
@@ -247,12 +247,15 @@
     cols = head_weight.shape[1]
     edges = [0, cols // 4, cols]
     pieces = []
+    weight = head_weight
     for j in range(len(edges) - 1):
-        w = head_weight[:, edges[j]:edges[j + 1]]
+        w = weight[:, edges[j]:edges[j + 1]]
         sent = jnp.dot(theirs, w, preferred_element_type=jnp.float32)
         kept = jnp.dot(mine, w, preferred_element_type=jnp.float32)
         got_half = lax.ppermute(sent, "pair", [(0, 1), (1, 0)])
-        pieces.append(lax.psum_scatter(kept + got_half, "batch", scatter_dimension=0, tiled=True))
+        summed = kept + got_half
+        summed, weight, theirs, mine = lax.optimization_barrier((summed, weight, theirs, mine))
+        pieces.append(lax.psum_scatter(summed, "batch", scatter_dimension=0, tiled=True))
     logits = jnp.concatenate(pieces, axis=1)
     cond = logits[:out_rows]
     uncond = logits[out_rows:]

time: 248 us -> 240 us (0.968)
  waiting for transfers between devices: 100 us -> 95.5 us
  matrix products: 27.4 us -> 24.2 us
    reduce_scatter x2, waiting for transfers between devices: 91.2 us -> 81.1 us  [on_device(): lax.psum_scatter(summed, 'batch', scatter_dimension=0, tiled=True)]
    ppermute x2, waiting for transfers between devices: 8.79 us -> 14.4 us  [on_device(): got_half = lax.ppermute(sent, 'pair', [(0, 1), (1, 0)])]
    dot_general x2, matrix products: 13.5 us -> 10.9 us  [on_device(): sent = jnp.dot(theirs, w, preferred_element_type=jnp.float32)]
  transfers between devices with their start and end apart: 4 -> 4, of which waited for: 3 -> 4; matrix products, arithmetic and copies ran while one was open for 8% -> 4% of each run, Pallas kernels for 0% -> 0%
where the time goes in v15:
time: 240 us
  waiting for transfers between devices  95.5 us (40%)
  Pallas kernels  86.9 us (36%)
  matrix products  24.2 us (10%)
  between operations  14.1 us (6%)
  other arithmetic  11.8 us (5%)
  local copies, waits for them, and re-layouts  6.73 us (3%)
    reduce_scatter x2, waiting for transfers between devices, on_device(): lax.psum_scatter(summed, 'batch', scatter_dimension=0, tiled=True)  81.1 us
    pallas_call x2, Pallas kernels, vocab_gather(): pl.pallas_call(functools.partial(gather_kernel, nv), out_shape=jax.ShapeD...  55.7 us
    pallas_call x1, Pallas kernels, kblock_scatter(): pl.pallas_call(functools.partial(scatter_kernel, npair, nb), out_shape=ja...  31.1 us
    ppermute x2, waiting for transfers between devices, on_device(): got_half = lax.ppermute(sent, 'pair', [(0, 1), (1, 0)])  14.4 us
    dot_general x2, matrix products, on_device(): kept = jnp.dot(mine, w, preferred_element_type=jnp.float32)  13.3 us
    dot_general x2, matrix products, on_device(): sent = jnp.dot(theirs, w, preferred_element_type=jnp.float32)  10.9 us
  transfers between devices with their start and end apart: 4, of which 4 were waited for; matrix products, arithmetic and copies ran while one was open for 4% of the time, Pallas kernels for 0%

profile of v15, /device:TPU:0, one launch (start us, length us, event | category | flops | bytes accessed | tf_op | source)
XLA Modules:
  0.0 239.6 jit_solution(3456369122325325797)
XLA Ops:
  7.2 0.7 broadcast_in_dim.4
  8.0 1.7 maximum_maximum_fusion.src_ref
  9.6 44.9 %shard_map.50 = bf16[16,144,512]{2,1,0:T(8,128)(2,1)} custom-call(bf16[144,512]{1,0:T(8,128)(2,1)} %maximum_maximum_fusion.src_ref), custom_call_target="tpu_custom_call" | custom-call | bytes 4718592 | tf_op jit(solution)/shard_map/pallas_call | solution.py:143
  54.6 2.1 fusion.7
  56.7 0.9 slice_convert_fusion
  57.6 2.2 convert_bitcast_fusion
  59.8 0.6 copy.10
  60.4 1.9 multiply_convert_fusion.src_ref
  62.3 31.1 %shard_map.51 = bf16[4,2,2,64,1024]{4,3,2,1,0:T(8,128)(2,1)} custom-call(bf16[128,8192]{1,0:T(8,128)(2,1)} %multiply_convert_fusion.src_ref), custom_call_target="tpu_custom_call" | custom-call | bytes 4194304 | tf_op jit(solution)/shard_map/pallas_call | solution.py:215
  93.4 1.7 constant_dynamic-slice_fusion.1
  95.1 2.8 %fusion.8 = f32[512,1024]{1,0:T(8,128)S(1)} fusion(bf16[512,1024]{1,0:T(8,128)(2,1)S(1)} %get-tuple-element.22, bf16[1024,4096]{1,0:T(8,128)(2,1)} %param.7), kind=kOutput, calls=%fused_computation.9 | convolution fusion | flops 1073741824 | bytes 5242880 | tf_op jit(solution)/shard_map/dot_general | solution.py:253
  98.1 4.1 %collective-permute-done = f32[512,1024]{1,0:T(8,128)S(1)} collective-permute-done((f32[512,1024]{1,0:T(8,128)S(1)}, f32[512,1024]{1,0:T(8,128)S(1)}, u32[]{:S(2)}, u32[]{:S(2)}) %collective-permute-start) | collective-permute-done | bytes 2097184 | tf_op jit(solution)/shard_map/ppermute | solution.py:255
  102.2 4.2 %fusion.12 = f32[512,1024]{1,0:T(8,128)} fusion(f32[512,1024]{1,0:T(8,128)S(1)} %collective-permute-done, bf16[512,1024]{1,0:T(8,128)(2,1)S(1)} %get-tuple-element.20, bf16[1024,4096]{1,0:T(8,128)(2,1)} %param.7), kind=kOutput, calls=%fused_computation.13 | convolution fusion | flops 1074266112 | bytes 7340032 | tf_op jit(solution)/shard_map/dot_general | solution.py:254
  106.4 8.1 %fusion = f32[512,3072]{1,0:T(8,128)} fusion(bf16[512,1024]{1,0:T(8,128)(2,1)S(1)} %get-tuple-element.22, bf16[1024,4096]{1,0:T(8,128)(2,1)} %param.7), kind=kOutput, calls=%fused_computation | convolution fusion | flops 3221225472 | bytes 13631488 | tf_op jit(solution)/shard_map/dot_general | solution.py:253
  114.7 10.3 %collective-permute-done.1 = f32[512,3072]{1,0:T(8,128)} collective-permute-done((f32[512,3072]{1,0:T(8,128)}, f32[512,3072]{1,0:T(8,128)}, u32[]{:S(2)}, u32[]{:S(2)}) %collective-permute-start.1) | collective-permute-done | bytes 6291488 | tf_op jit(solution)/shard_map/ppermute | solution.py:255
  125.0 9.1 %fusion.4 = f32[512,3072]{1,0:T(8,128)} fusion(f32[512,3072]{1,0:T(8,128)} %collective-permute-done.1, bf16[512,1024]{1,0:T(8,128)(2,1)S(1)} %get-tuple-element.20, bf16[1024,4096]{1,0:T(8,128)(2,1)} %param.7), kind=kOutput, calls=%fused_computation.6 | convolution fusion | flops 3222798336 | bytes 19922944 | tf_op jit(solution)/shard_map/dot_general | solution.py:254
  134.1 15.9 %reduce-scatter.3.cloned.1.call-done = f32[128,1024]{1,0:T(8,128)} async-done(((f32[512,1024]{1,0:T(8,128)}), f32[128,1024]{1,0:T(8,128)}) %reduce-scatter.3.cloned.1.call-update) | async-done | bytes 524304 | tf_op jit(solution)/shard_map/reduce_scatter | solution.py:258
  150.0 1.1 constant_dynamic-update-slice_fusion.1
  151.1 65.2 %reduce-scatter.5.cloned.1.call-done = f32[128,3072]{1,0:T(8,128)} async-done(((f32[512,3072]{1,0:T(8,128)}), f32[128,3072]{1,0:T(8,128)}) %reduce-scatter.5.cloned.1.call-update) | async-done | bytes 1572880 | tf_op jit(solution)/shard_map/reduce_scatter | solution.py:258
  216.3 1.5 constant_dynamic-update-slice_fusion
  218.6 0.6 select_maximum_fusion.src_ref
  219.2 10.8 %shard_map.52 = f32[16,8,128]{2,1,0:T(8,128)} custom-call(f32[8,128]{1,0:T(8,128)} %select_maximum_fusion.src_ref), custom_call_target="tpu_custom_call" | custom-call | bytes 131072 | tf_op jit(solution)/shard_map/pallas_call | solution.py:143
  230.0 1.0 fusion.17
  231.2 1.6 slice_subtract_fusion
  (16 shorter events, 1.3 us)
Async XLA Ops:
  7.2 142.9 %reduce-scatter.3.cloned.1.call-start = ((), (), s32[]{:S(2)}) async-start(), calls=%async_computation.2 | async-start | bytes 2621440 | tf_op jit(solution)/shard_map/reduce_scatter | solution.py:258
  98.0 4.2 %collective-permute-start = (f32[512,1024]{1,0:T(8,128)S(1)}, f32[512,1024]{1,0:T(8,128)S(1)}, u32[]{:S(2)}, u32[]{:S(2)}) collective-permute-start(f32[512,1024]{1,0:T(8,128)S(1)} %fusion.8), channel_id=1, source_target_pairs={{0,64},{64,0},{1,65},{65,1},{2,66},{66,2},{3,67},{67,3},{4,68},{68... | collective-permute-start | bytes 6291464 | tf_op jit(solution)/shard_map/ppermute | solution.py:255
  114.5 10.5 %collective-permute-start.1 = (f32[512,3072]{1,0:T(8,128)}, f32[512,3072]{1,0:T(8,128)}, u32[]{:S(2)}, u32[]{:S(2)}) collective-permute-start(f32[512,3072]{1,0:T(8,128)} %fusion), channel_id=1, source_target_pairs={{0,64},{64,0},{1,65},{65,1},{2,66},{66,2},{3,67},{67,3},{4,68},{68... | collective-permute-start | bytes 18874376 | tf_op jit(solution)/shard_map/ppermute | solution.py:255
  114.7 101.6 %reduce-scatter.5.cloned.1.call-start = ((), (), s32[]{:S(2)}) async-start(), calls=%async_computation.3 | async-start | bytes 7864320 | tf_op jit(solution)/shard_map/reduce_scatter | solution.py:258
Sparse Core Ops, SparseCore 0:
  114.8 35.1 reduce-scatter.2
  152.6 63.6 reduce-scatter.4

commit v16 on v15

--- a/solution.py
+++ b/solution.py
@@ -245,7 +245,7 @@
     mine = lax.dynamic_slice_in_dim(ordered, me * half_rows, half_rows, axis=0)
     theirs = lax.dynamic_slice_in_dim(ordered, (1 - me) * half_rows, half_rows, axis=0)
     cols = head_weight.shape[1]
-    edges = [0, cols // 4, cols]
+    edges = [0, cols // 8, cols]
     pieces = []
     weight = head_weight
     for j in range(len(edges) - 1):

time: 240 us -> 238 us (level)
  transfers between devices with their start and end apart: 4 -> 4, of which waited for: 4 -> 4; matrix products, arithmetic and copies ran while one was open for 4% -> 5% of each run, Pallas kernels for 0% -> 0%
where the time goes in v16:
time: 238 us; the launch traced here: 237 us
  waiting for transfers between devices  95.2 us (40%)
  Pallas kernels  86.9 us (37%)
  matrix products  24.4 us (10%)
  between operations  14.2 us (6%)
  other arithmetic  9.47 us (4%)
  local copies, waits for them, and re-layouts  6.74 us (3%)
    reduce_scatter x2, waiting for transfers between devices, on_device(): lax.psum_scatter(summed, 'batch', scatter_dimension=0, tiled=True)  80.7 us
    pallas_call x2, Pallas kernels, vocab_gather(): pl.pallas_call(functools.partial(gather_kernel, nv), out_shape=jax.ShapeD...  55.7 us
    pallas_call x1, Pallas kernels, kblock_scatter(): pl.pallas_call(functools.partial(scatter_kernel, npair, nb), out_shape=ja...  31.1 us
    ppermute x2, waiting for transfers between devices, on_device(): got_half = lax.ppermute(sent, 'pair', [(0, 1), (1, 0)])  14.4 us
    dot_general x2, matrix products, on_device(): kept = jnp.dot(mine, w, preferred_element_type=jnp.float32)  13.4 us
    dot_general x2, matrix products, on_device(): sent = jnp.dot(theirs, w, preferred_element_type=jnp.float32)  11.1 us
  transfers between devices with their start and end apart: 4, of which 4 were waited for; matrix products, arithmetic and copies ran while one was open for 5% of the time, Pallas kernels for 0%

profile of v16, /device:TPU:0, one launch (start us, length us, event | category | flops | bytes accessed | tf_op | source)
XLA Modules:
  0.0 237.1 jit_solution(4316646517310553648)
XLA Ops:
  7.2 0.7 broadcast_in_dim.4
  8.0 1.7 maximum_maximum_fusion.src_ref
  9.6 44.9 %shard_map.50 = bf16[16,144,512]{2,1,0:T(8,128)(2,1)} custom-call(bf16[144,512]{1,0:T(8,128)(2,1)} %maximum_maximum_fusion.src_ref), custom_call_target="tpu_custom_call" | custom-call | bytes 4718592 | tf_op jit(solution)/shard_map/pallas_call | solution.py:143
  54.6 2.3 convert_bitcast_fusion
  56.9 0.5 fusion.7
  57.4 0.6 copy.10
  58.1 1.9 multiply_convert_fusion.src_ref
  59.9 31.1 %shard_map.51 = bf16[4,2,2,64,1024]{4,3,2,1,0:T(8,128)(2,1)} custom-call(bf16[128,8192]{1,0:T(8,128)(2,1)} %multiply_convert_fusion.src_ref), custom_call_target="tpu_custom_call" | custom-call | bytes 4194304 | tf_op jit(solution)/shard_map/pallas_call | solution.py:215
  91.1 1.7 constant_dynamic-slice_fusion.1
  92.8 1.9 fusion.9
  94.8 2.6 %collective-permute-done = f32[512,512]{1,0:T(8,128)S(1)} collective-permute-done((f32[512,512]{1,0:T(8,128)S(1)}, f32[512,512]{1,0:T(8,128)S(1)}, u32[]{:S(2)}, u32[]{:S(2)}) %collective-permute-start) | collective-permute-done | bytes 1048608 | tf_op jit(solution)/shard_map/ppermute | solution.py:255
  97.5 2.9 %convolution_add_fusion = f32[512,512]{1,0:T(8,128)} fusion(f32[512,512]{1,0:T(8,128)S(1)} %collective-permute-done, bf16[512,1024]{1,0:T(8,128)(2,1)S(1)} %get-tuple-element.20, bf16[1024,4096]{1,0:T(8,128)(2,1)} %param.7), kind=kOutput, calls=%fused_computation.9 | convolution fusion | flops 537133056 | bytes 4194304 | tf_op jit(solution)/shard_map/dot_general | solution.py:254
  100.4 9.1 %fusion = f32[512,3584]{1,0:T(8,128)} fusion(bf16[512,1024]{1,0:T(8,128)(2,1)S(1)} %get-tuple-element.22, bf16[1024,4096]{1,0:T(8,128)(2,1)} %param.7), kind=kOutput, calls=%fused_computation | convolution fusion | flops 3758096384 | bytes 15728640 | tf_op jit(solution)/shard_map/dot_general | solution.py:253
  109.7 11.8 %collective-permute-done.1 = f32[512,3584]{1,0:T(8,128)} collective-permute-done((f32[512,3584]{1,0:T(8,128)}, f32[512,3584]{1,0:T(8,128)}, u32[]{:S(2)}, u32[]{:S(2)}) %collective-permute-start.1) | collective-permute-done | bytes 7340064 | tf_op jit(solution)/shard_map/ppermute | solution.py:255
  121.5 10.5 %fusion.4 = f32[512,3584]{1,0:T(8,128)} fusion(f32[512,3584]{1,0:T(8,128)} %collective-permute-done.1, bf16[512,1024]{1,0:T(8,128)(2,1)S(1)} %get-tuple-element.20, bf16[1024,4096]{1,0:T(8,128)(2,1)} %param.7), kind=kOutput, calls=%fused_computation.4 | convolution fusion | flops 3759931392 | bytes 23068672 | tf_op jit(solution)/shard_map/dot_general | solution.py:254
  132.0 6.8 %reduce-scatter.3.cloned.1.call-done = f32[128,512]{1,0:T(8,128)} async-done(((f32[512,512]{1,0:T(8,128)}), f32[128,512]{1,0:T(8,128)}) %reduce-scatter.3.cloned.1.call-update) | async-done | bytes 262160 | tf_op jit(solution)/shard_map/reduce_scatter | solution.py:258
  138.8 1.0 constant_dynamic-update-slice_fusion.1
  139.8 73.9 %reduce-scatter.5.cloned.1.call-done = f32[128,3584]{1,0:T(8,128)} async-done(((f32[512,3584]{1,0:T(8,128)}), f32[128,3584]{1,0:T(8,128)}) %reduce-scatter.5.cloned.1.call-update) | async-done | bytes 1835024 | tf_op jit(solution)/shard_map/reduce_scatter | solution.py:258
  213.7 1.6 constant_dynamic-update-slice_fusion
  215.6 0.5 exponential_reduce_fusion.1
  216.2 0.6 select_maximum_fusion.src_ref
  216.8 10.8 %shard_map.52 = f32[16,8,128]{2,1,0:T(8,128)} custom-call(f32[8,128]{1,0:T(8,128)} %select_maximum_fusion.src_ref), custom_call_target="tpu_custom_call" | custom-call | bytes 131072 | tf_op jit(solution)/shard_map/pallas_call | solution.py:143
  227.6 1.0 fusion.13
  228.7 1.6 slice_subtract_fusion
  (18 shorter events, 0.8 us)
Async XLA Ops:
  7.2 131.7 %reduce-scatter.3.cloned.1.call-start = ((), (), s32[]{:S(2)}) async-start(), calls=%async_computation.2 | async-start | bytes 1310720 | tf_op jit(solution)/shard_map/reduce_scatter | solution.py:258
  54.6 2.3 copy-start
  94.7 2.7 %collective-permute-start = (f32[512,512]{1,0:T(8,128)S(1)}, f32[512,512]{1,0:T(8,128)S(1)}, u32[]{:S(2)}, u32[]{:S(2)}) collective-permute-start(f32[512,512]{1,0:T(8,128)S(1)} %fusion.9), channel_id=1, source_target_pairs={{0,64},{64,0},{1,65},{65,1},{2,66},{66,2},{3,67},{67,3},{4,68},{68... | collective-permute-start | bytes 3145736 | tf_op jit(solution)/shard_map/ppermute | solution.py:255
  109.5 12.0 %collective-permute-start.1 = (f32[512,3584]{1,0:T(8,128)}, f32[512,3584]{1,0:T(8,128)}, u32[]{:S(2)}, u32[]{:S(2)}) collective-permute-start(f32[512,3584]{1,0:T(8,128)} %fusion), channel_id=1, source_target_pairs={{0,64},{64,0},{1,65},{65,1},{2,66},{66,2},{3,67},{67,3},{4,68},{68... | collective-permute-start | bytes 22020104 | tf_op jit(solution)/shard_map/ppermute | solution.py:255
  109.7 104.0 %reduce-scatter.5.cloned.1.call-start = ((), (), s32[]{:S(2)}) async-start(), calls=%async_computation.3 | async-start | bytes 9175040 | tf_op jit(solution)/shard_map/reduce_scatter | solution.py:258
Sparse Core Ops, SparseCore 0:
  109.8 28.9 reduce-scatter.2
  141.4 72.2 reduce-scatter.4

commit v17 on v16

--- a/solution.py
+++ b/solution.py
@@ -149,6 +149,57 @@
         compiler_params=pltpu.CompilerParams(collective_id=cid, has_side_effects=True),
         cost_estimate=pl.CostEstimate(flops=0, transcendentals=0, bytes_accessed=2 * nv * size),
     )(block)
+
+
+def gather_pair_kernel(nv, h_ref, g_ref, ho_ref, go_ref, hs, hr, gs, gr):
+    beta = lax.axis_index("pair")
+    b = lax.axis_index("batch")
+    v = lax.axis_index("vocab")
+    barrier = pltpu.get_barrier_semaphore()
+    for k in range(1, nv):
+        pl.semaphore_signal(barrier, inc=1, device_id=(beta, b, (v + k) % nv), device_id_type=MESH)
+    pl.semaphore_wait(barrier, nv - 1)
+
+    def remote(src, dst, send, recv, w, s):
+        return pltpu.make_async_remote_copy(
+            src_ref=src,
+            dst_ref=dst.at[s],
+            send_sem=send.at[w],
+            recv_sem=recv.at[s],
+            device_id=(beta, b, w),
+            device_id_type=MESH,
+        )
+
+    pairs = ((h_ref, ho_ref, hs, hr), (g_ref, go_ref, gs, gr))
+    for k in range(1, nv):
+        for src, dst, send, recv in pairs:
+            remote(src, dst, send, recv, (v + k) % nv, v).start()
+    for src, dst, send, recv in pairs:
+        pltpu.make_async_copy(src, dst.at[v], recv.at[v]).start()
+    for k in range(1, nv):
+        for src, dst, send, recv in pairs:
+            remote(src, dst, send, recv, (v + k) % nv, v).wait_send()
+    for k in range(1, nv):
+        s = (v + k) % nv
+        for src, dst, send, recv in pairs:
+            remote(src, dst, send, recv, s, s).wait_recv()
+    for src, dst, send, recv in pairs:
+        pltpu.make_async_copy(src, dst.at[v], recv.at[v]).wait()
+
+
+def vocab_gather_pair(rows, gain, nv, cid):
+    size = rows.size * rows.dtype.itemsize + gain.size * gain.dtype.itemsize
+    sems = [pltpu.SemaphoreType.DMA((nv,))] * 4
+    return pl.pallas_call(
+        functools.partial(gather_pair_kernel, nv),
+        out_shape=(jax.ShapeDtypeStruct((nv,) + rows.shape, rows.dtype),
+                   jax.ShapeDtypeStruct((nv,) + gain.shape, gain.dtype)),
+        in_specs=[pl.BlockSpec(memory_space=pltpu.VMEM)] * 2,
+        out_specs=(pl.BlockSpec(memory_space=pltpu.VMEM), pl.BlockSpec(memory_space=pltpu.VMEM)),
+        scratch_shapes=sems,
+        compiler_params=pltpu.CompilerParams(collective_id=cid, has_side_effects=True),
+        cost_estimate=pl.CostEstimate(flops=0, transcendentals=0, bytes_accessed=2 * nv * size),
+    )(rows, gain)
 
 
 def scatter_kernel(npair, nb, src_ref, out_ref, send_sems, recv_sems):
@@ -228,11 +279,12 @@
     span = nv // groups
     local_rows, width = hidden.shape[1], hidden.shape[2]
     total_d = width * nv
-    pad = jnp.zeros((15, width), hidden.dtype)
-    block = jnp.concatenate([hidden[0], norm_gain[None, :], pad], axis=0)
-    got = vocab_gather(block, nv, 1)
-    wide = got[:, :local_rows, :].transpose(1, 0, 2).reshape(local_rows, total_d).astype(jnp.float32)
-    gain = got[:, local_rows, :].reshape(total_d)
+    lanes = 128
+    gain_rows = width // lanes
+    gain_block = jnp.zeros((16, lanes), norm_gain.dtype).at[:gain_rows].set(norm_gain.reshape(gain_rows, lanes))
+    got, got_gain = vocab_gather_pair(hidden[0], gain_block, nv, 1)
+    wide = got.transpose(1, 0, 2).reshape(local_rows, total_d).astype(jnp.float32)
+    gain = got_gain[:, :gain_rows, :].reshape(total_d)
     meansq = jnp.sum(wide * wide, axis=1) / total_d
     scaled = wide * lax.rsqrt(meansq + EPS)[:, None] * gain.astype(jnp.float32)[None, :]
     features = scaled.astype(jnp.bfloat16)

time: 238 us -> 234 us (0.983)
  Pallas kernels: 86.9 us -> 82.9 us
    pallas_call x2 -> x1, Pallas kernels: 55.7 us -> 10.8 us  [vocab_gather(): pl.pallas_call(functools.partial(gather_kernel, nv), out_shape=jax.ShapeD...]
    pallas_call x0 -> x1, Pallas kernels: none -> 40.9 us  [vocab_gather_pair(): pl.pallas_call(functools.partial(gather_pair_kernel, nv), out_shape=(jax....]
where the time goes in v17:
time: 234 us; the launch traced here: 233 us
  waiting for transfers between devices  95.5 us (41%)
  Pallas kernels  82.9 us (35%)
  matrix products  24.4 us (10%)
  between operations  14.1 us (6%)
  local copies, waits for them, and re-layouts  8.02 us (3%)
  other arithmetic  7.79 us (3%)
    reduce_scatter x2, waiting for transfers between devices, on_device(): lax.psum_scatter(summed, 'batch', scatter_dimension=0, tiled=True)  81 us
    pallas_call x1, Pallas kernels, vocab_gather_pair(): pl.pallas_call(functools.partial(gather_pair_kernel, nv), out_shape=(jax....  40.9 us
    pallas_call x1, Pallas kernels, kblock_scatter(): pl.pallas_call(functools.partial(scatter_kernel, npair, nb), out_shape=ja...  31.1 us
    ppermute x2, waiting for transfers between devices, on_device(): got_half = lax.ppermute(sent, 'pair', [(0, 1), (1, 0)])  14.4 us
    dot_general x2, matrix products, on_device(): kept = jnp.dot(mine, w, preferred_element_type=jnp.float32)  13.4 us
    dot_general x2, matrix products, on_device(): sent = jnp.dot(theirs, w, preferred_element_type=jnp.float32)  11.1 us
    pallas_call x1, Pallas kernels, vocab_gather(): pl.pallas_call(functools.partial(gather_kernel, nv), out_shape=jax.ShapeD...  10.8 us
  transfers between devices with their start and end apart: 4, of which 4 were waited for; matrix products, arithmetic and copies ran while one was open for 5% of the time, Pallas kernels for 0%

profile of v17, /device:TPU:0, one launch (start us, length us, event | category | flops | bytes accessed | tf_op | source)
XLA Modules:
  0.0 233.1 jit_solution(12647507349323095971)
XLA Ops:
  7.2 1.3 scatter.6.g_ref
  8.5 40.9 %shard_map.50 = (bf16[16,128,512]{2,1,0:T(8,128)(2,1)}, bf16[16,16,128]{2,1,0:T(8,128)(2,1)}) custom-call(bf16[128,512]{1,0:T(8,128)(2,1)} %bitcast.27, bf16[16,128]{1,0:T(8,128)(2,1)} %scatter.6.g_ref), custom_call_target="tpu_custom_call" | custom-call | bytes 4325376 | tf_op jit(solution)/shard_map/pallas_call | solution.py:193
  49.5 2.3 convert_bitcast_fusion
  51.8 0.5 fusion.7
  52.3 0.6 copy.10
  52.9 0.8 slice.70
  53.7 1.9 multiply_convert_fusion.src_ref
  55.5 31.1 %shard_map.51 = bf16[4,2,2,64,1024]{4,3,2,1,0:T(8,128)(2,1)} custom-call(bf16[128,8192]{1,0:T(8,128)(2,1)} %multiply_convert_fusion.src_ref), custom_call_target="tpu_custom_call" | custom-call | bytes 4194304 | tf_op jit(solution)/shard_map/pallas_call | solution.py:266
  86.7 1.7 constant_dynamic-slice_fusion.1
  88.4 1.9 fusion.9
  90.4 2.6 %collective-permute-done = f32[512,512]{1,0:T(8,128)S(1)} collective-permute-done((f32[512,512]{1,0:T(8,128)S(1)}, f32[512,512]{1,0:T(8,128)S(1)}, u32[]{:S(2)}, u32[]{:S(2)}) %collective-permute-start) | collective-permute-done | bytes 1048608 | tf_op jit(solution)/shard_map/ppermute | solution.py:307
  93.1 2.9 %convolution_add_fusion = f32[512,512]{1,0:T(8,128)} fusion(f32[512,512]{1,0:T(8,128)S(1)} %collective-permute-done, bf16[512,1024]{1,0:T(8,128)(2,1)S(1)} %get-tuple-element.36, bf16[1024,4096]{1,0:T(8,128)(2,1)} %param.9), kind=kOutput, calls=%fused_computation.9 | convolution fusion | flops 537133056 | bytes 4194304 | tf_op jit(solution)/shard_map/dot_general | solution.py:306
  96.0 9.1 %fusion = f32[512,3584]{1,0:T(8,128)} fusion(bf16[512,1024]{1,0:T(8,128)(2,1)S(1)} %get-tuple-element.38, bf16[1024,4096]{1,0:T(8,128)(2,1)} %param.9), kind=kOutput, calls=%fused_computation | convolution fusion | flops 3758096384 | bytes 15728640 | tf_op jit(solution)/shard_map/dot_general | solution.py:305
  105.3 11.8 %collective-permute-done.1 = f32[512,3584]{1,0:T(8,128)} collective-permute-done((f32[512,3584]{1,0:T(8,128)}, f32[512,3584]{1,0:T(8,128)}, u32[]{:S(2)}, u32[]{:S(2)}) %collective-permute-start.1) | collective-permute-done | bytes 7340064 | tf_op jit(solution)/shard_map/ppermute | solution.py:307
  117.1 10.5 %fusion.4 = f32[512,3584]{1,0:T(8,128)} fusion(f32[512,3584]{1,0:T(8,128)} %collective-permute-done.1, bf16[512,1024]{1,0:T(8,128)(2,1)S(1)} %get-tuple-element.36, bf16[1024,4096]{1,0:T(8,128)(2,1)} %param.9), kind=kOutput, calls=%fused_computation.4 | convolution fusion | flops 3759931392 | bytes 23068672 | tf_op jit(solution)/shard_map/dot_general | solution.py:306
  127.6 7.1 %reduce-scatter.3.cloned.1.call-done = f32[128,512]{1,0:T(8,128)} async-done(((f32[512,512]{1,0:T(8,128)}), f32[128,512]{1,0:T(8,128)}) %reduce-scatter.3.cloned.1.call-update) | async-done | bytes 262160 | tf_op jit(solution)/shard_map/reduce_scatter | solution.py:310
  134.8 1.0 constant_dynamic-update-slice_fusion.1
  135.7 73.9 %reduce-scatter.5.cloned.1.call-done = f32[128,3584]{1,0:T(8,128)} async-done(((f32[512,3584]{1,0:T(8,128)}), f32[128,3584]{1,0:T(8,128)}) %reduce-scatter.5.cloned.1.call-update) | async-done | bytes 1835024 | tf_op jit(solution)/shard_map/reduce_scatter | solution.py:310
  209.6 1.6 constant_dynamic-update-slice_fusion
  211.6 0.5 exponential_reduce_fusion.1
  212.1 0.6 select_maximum_fusion.src_ref
  212.7 10.8 %shard_map.52 = f32[16,8,128]{2,1,0:T(8,128)} custom-call(f32[8,128]{1,0:T(8,128)} %select_maximum_fusion.src_ref), custom_call_target="tpu_custom_call" | custom-call | bytes 131072 | tf_op jit(solution)/shard_map/pallas_call | solution.py:143
  223.5 1.0 fusion.13
  224.6 1.6 slice_subtract_fusion
  (16 shorter events, 0.7 us)
Async XLA Ops:
  7.2 127.6 %reduce-scatter.3.cloned.1.call-start = ((), (), s32[]{:S(2)}) async-start(), calls=%async_computation.2 | async-start | bytes 1310720 | tf_op jit(solution)/shard_map/reduce_scatter | solution.py:310
  49.4 2.3 copy-start
  90.4 2.7 %collective-permute-start = (f32[512,512]{1,0:T(8,128)S(1)}, f32[512,512]{1,0:T(8,128)S(1)}, u32[]{:S(2)}, u32[]{:S(2)}) collective-permute-start(f32[512,512]{1,0:T(8,128)S(1)} %fusion.9), channel_id=1, source_target_pairs={{0,64},{64,0},{1,65},{65,1},{2,66},{66,2},{3,67},{67,3},{4,68},{68... | collective-permute-start | bytes 3145736 | tf_op jit(solution)/shard_map/ppermute | solution.py:307
  105.1 12.0 %collective-permute-start.1 = (f32[512,3584]{1,0:T(8,128)}, f32[512,3584]{1,0:T(8,128)}, u32[]{:S(2)}, u32[]{:S(2)}) collective-permute-start(f32[512,3584]{1,0:T(8,128)} %fusion), channel_id=1, source_target_pairs={{0,64},{64,0},{1,65},{65,1},{2,66},{66,2},{3,67},{67,3},{4,68},{68... | collective-permute-start | bytes 22020104 | tf_op jit(solution)/shard_map/ppermute | solution.py:307
  105.3 104.3 %reduce-scatter.5.cloned.1.call-start = ((), (), s32[]{:S(2)}) async-start(), calls=%async_computation.3 | async-start | bytes 9175040 | tf_op jit(solution)/shard_map/reduce_scatter | solution.py:310
Sparse Core Ops, SparseCore 0:
  105.4 29.3 reduce-scatter.2
  137.3 72.2 reduce-scatter.4

commit v18 on v17

--- a/solution.py
+++ b/solution.py
@@ -297,7 +297,7 @@
     mine = lax.dynamic_slice_in_dim(ordered, me * half_rows, half_rows, axis=0)
     theirs = lax.dynamic_slice_in_dim(ordered, (1 - me) * half_rows, half_rows, axis=0)
     cols = head_weight.shape[1]
-    edges = [0, cols // 8, cols]
+    edges = [0, cols // 16, cols]
     pieces = []
     weight = head_weight
     for j in range(len(edges) - 1):

time: 234 us -> 234 us (level)
  no operation moved by 1% of the time
where the time goes in v18:
time: 234 us
  waiting for transfers between devices  96.4 us (41%)
  Pallas kernels  82.9 us (35%)
  matrix products  24.3 us (10%)
  between operations  14.1 us (6%)
  local copies, waits for them, and re-layouts  8.06 us (3%)
  other arithmetic  7.79 us (3%)
    reduce_scatter x2, waiting for transfers between devices, on_device(): lax.psum_scatter(summed, 'batch', scatter_dimension=0, tiled=True)  81.9 us
    pallas_call x1, Pallas kernels, vocab_gather_pair(): pl.pallas_call(functools.partial(gather_pair_kernel, nv), out_shape=(jax....  40.9 us
    pallas_call x1, Pallas kernels, kblock_scatter(): pl.pallas_call(functools.partial(scatter_kernel, npair, nb), out_shape=ja...  31.1 us
    ppermute x2, waiting for transfers between devices, on_device(): got_half = lax.ppermute(sent, 'pair', [(0, 1), (1, 0)])  14.4 us
    dot_general x2, matrix products, on_device(): kept = jnp.dot(mine, w, preferred_element_type=jnp.float32)  13.2 us
    dot_general x2, matrix products, on_device(): sent = jnp.dot(theirs, w, preferred_element_type=jnp.float32)  11.1 us
    pallas_call x1, Pallas kernels, vocab_gather(): pl.pallas_call(functools.partial(gather_kernel, nv), out_shape=jax.ShapeD...  10.8 us
  transfers between devices with their start and end apart: 4, of which 4 were waited for; matrix products, arithmetic and copies ran while one was open for 5% of the time, Pallas kernels for 0%

profile of v18, /device:TPU:0, one launch (start us, length us, event | category | flops | bytes accessed | tf_op | source)
XLA Modules:
  0.0 233.8 jit_solution(3488313105100554306)
XLA Ops:
  7.2 1.3 scatter.6.g_ref
  8.5 40.9 %shard_map.50 = (bf16[16,128,512]{2,1,0:T(8,128)(2,1)}, bf16[16,16,128]{2,1,0:T(8,128)(2,1)}) custom-call(bf16[128,512]{1,0:T(8,128)(2,1)} %bitcast.27, bf16[16,128]{1,0:T(8,128)(2,1)} %scatter.6.g_ref), custom_call_target="tpu_custom_call" | custom-call | bytes 4325376 | tf_op jit(solution)/shard_map/pallas_call | solution.py:193
  49.5 2.3 convert_bitcast_fusion
  51.8 0.5 fusion.7
  52.3 0.6 copy.10
  52.9 0.8 slice.70
  53.7 1.9 multiply_convert_fusion.src_ref
  55.5 31.1 %shard_map.51 = bf16[4,2,2,64,1024]{4,3,2,1,0:T(8,128)(2,1)} custom-call(bf16[128,8192]{1,0:T(8,128)(2,1)} %multiply_convert_fusion.src_ref), custom_call_target="tpu_custom_call" | custom-call | bytes 4194304 | tf_op jit(solution)/shard_map/pallas_call | solution.py:266
  86.7 1.7 constant_dynamic-slice_fusion.1
  88.4 1.5 fusion.9
  90.0 1.9 collective-permute-done
  91.9 2.3 convolution_add_fusion
  94.2 9.6 %fusion = f32[512,3840]{1,0:T(8,128)} fusion(bf16[512,1024]{1,0:T(8,128)(2,1)S(1)} %get-tuple-element.38, bf16[1024,4096]{1,0:T(8,128)(2,1)} %param.9), kind=kOutput, calls=%fused_computation | convolution fusion | flops 4026531840 | bytes 16777216 | tf_op jit(solution)/shard_map/dot_general | solution.py:305
  104.0 12.5 %collective-permute-done.1 = f32[512,3840]{1,0:T(8,128)} collective-permute-done((f32[512,3840]{1,0:T(8,128)}, f32[512,3840]{1,0:T(8,128)}, u32[]{:S(2)}, u32[]{:S(2)}) %collective-permute-start.1) | collective-permute-done | bytes 7864352 | tf_op jit(solution)/shard_map/ppermute | solution.py:307
  116.5 10.9 %fusion.4 = f32[512,3840]{1,0:T(8,128)} fusion(f32[512,3840]{1,0:T(8,128)} %collective-permute-done.1, bf16[512,1024]{1,0:T(8,128)(2,1)S(1)} %get-tuple-element.36, bf16[1024,4096]{1,0:T(8,128)(2,1)} %param.9), kind=kOutput, calls=%fused_computation.4 | convolution fusion | flops 4028497920 | bytes 24641536 | tf_op jit(solution)/shard_map/dot_general | solution.py:306
  127.5 3.9 %reduce-scatter.3.cloned.1.call-done = f32[128,256]{1,0:T(8,128)} async-done(((f32[512,256]{1,0:T(8,128)}), f32[128,256]{1,0:T(8,128)}) %reduce-scatter.3.cloned.1.call-update) | async-done | bytes 131088 | tf_op jit(solution)/shard_map/reduce_scatter | solution.py:310
  131.4 0.9 constant_dynamic-update-slice_fusion.1
  132.3 78.0 %reduce-scatter.5.cloned.1.call-done = f32[128,3840]{1,0:T(8,128)} async-done(((f32[512,3840]{1,0:T(8,128)}), f32[128,3840]{1,0:T(8,128)}) %reduce-scatter.5.cloned.1.call-update) | async-done | bytes 1966096 | tf_op jit(solution)/shard_map/reduce_scatter | solution.py:310
  210.3 1.7 constant_dynamic-update-slice_fusion
  212.3 0.5 exponential_reduce_fusion.1
  212.9 0.6 select_maximum_fusion.src_ref
  213.5 10.8 %shard_map.52 = f32[16,8,128]{2,1,0:T(8,128)} custom-call(f32[8,128]{1,0:T(8,128)} %select_maximum_fusion.src_ref), custom_call_target="tpu_custom_call" | custom-call | bytes 131072 | tf_op jit(solution)/shard_map/pallas_call | solution.py:143
  224.3 1.0 fusion.13
  225.4 1.6 slice_subtract_fusion
  (16 shorter events, 0.7 us)
Async XLA Ops:
  7.2 124.2 %reduce-scatter.3.cloned.1.call-start = ((), (), s32[]{:S(2)}) async-start(), calls=%async_computation.2 | async-start | bytes 655360 | tf_op jit(solution)/shard_map/reduce_scatter | solution.py:310
  49.4 2.3 copy-start
  89.9 2.0 collective-permute-start
  103.8 12.8 %collective-permute-start.1 = (f32[512,3840]{1,0:T(8,128)}, f32[512,3840]{1,0:T(8,128)}, u32[]{:S(2)}, u32[]{:S(2)}) collective-permute-start(f32[512,3840]{1,0:T(8,128)} %fusion), channel_id=1, source_target_pairs={{0,64},{64,0},{1,65},{65,1},{2,66},{66,2},{3,67},{67,3},{4,68},{68... | collective-permute-start | bytes 23592968 | tf_op jit(solution)/shard_map/ppermute | solution.py:307
  103.9 106.4 %reduce-scatter.5.cloned.1.call-start = ((), (), s32[]{:S(2)}) async-start(), calls=%async_computation.3 | async-start | bytes 9830400 | tf_op jit(solution)/shard_map/reduce_scatter | solution.py:310
Sparse Core Ops, SparseCore 0:
  104.1 27.2 reduce-scatter.2
  133.8 76.5 reduce-scatter.4

commit v19 on v17

--- a/solution.py
+++ b/solution.py
@@ -302,6 +302,11 @@
     weight = head_weight
     for j in range(len(edges) - 1):
         w = weight[:, edges[j]:edges[j + 1]]
+        if j == 0:
+            full = jnp.dot(ordered, w, preferred_element_type=jnp.float32)
+            full, weight, theirs, mine = lax.optimization_barrier((full, weight, theirs, mine))
+            pieces.append(lax.psum_scatter(full, ("pair", "batch"), scatter_dimension=0, tiled=True))
+            continue
         sent = jnp.dot(theirs, w, preferred_element_type=jnp.float32)
         kept = jnp.dot(mine, w, preferred_element_type=jnp.float32)
         got_half = lax.ppermute(sent, "pair", [(0, 1), (1, 0)])

time: 234 us -> 244 us (1.043)
  waiting for transfers between devices: 95.5 us -> 107 us
    reduce_scatter x0 -> x1, waiting for transfers between devices: none -> 20.9 us  [on_device(): lax.psum_scatter(full, ('pair', 'batch'), scatter_dimension=0, tiled=True)]
    reduce_scatter x2 -> x1, waiting for transfers between devices: 81 us -> 74.1 us  [on_device(): lax.psum_scatter(summed, 'batch', scatter_dimension=0, tiled=True)]
    dot_general x0 -> x1, matrix products: none -> 4.58 us  [on_device(): full = jnp.dot(ordered, w, preferred_element_type=jnp.float32)]
    dot_general x2 -> x1, matrix products: 13.4 us -> 10.4 us  [on_device(): kept = jnp.dot(mine, w, preferred_element_type=jnp.float32)]
    ppermute x2 -> x1, waiting for transfers between devices: 14.4 us -> 11.9 us  [on_device(): got_half = lax.ppermute(sent, 'pair', [(0, 1), (1, 0)])]
    dot_general x2 -> x1, matrix products: 11.1 us -> 9.08 us  [on_device(): sent = jnp.dot(theirs, w, preferred_element_type=jnp.float32)]
  transfers between devices with their start and end apart: 4 -> 3, of which waited for: 4 -> 3; matrix products, arithmetic and copies ran while one was open for 5% -> 5% of each run, Pallas kernels for 0% -> 0%
where the time goes in v19:
time: 244 us
  waiting for transfers between devices  107 us (44%)
  Pallas kernels  82.9 us (34%)
  matrix products  24 us (10%)
  between operations  14.1 us (6%)
  other arithmetic  9.17 us (4%)
  local copies, waits for them, and re-layouts  6.32 us (3%)
    reduce_scatter x1, waiting for transfers between devices, on_device(): lax.psum_scatter(summed, 'batch', scatter_dimension=0, tiled=True)  74.1 us
    pallas_call x1, Pallas kernels, vocab_gather_pair(): pl.pallas_call(functools.partial(gather_pair_kernel, nv), out_shape=(jax....  40.9 us
    pallas_call x1, Pallas kernels, kblock_scatter(): pl.pallas_call(functools.partial(scatter_kernel, npair, nb), out_shape=ja...  31.2 us
    reduce_scatter x1, waiting for transfers between devices, on_device(): lax.psum_scatter(full, ('pair', 'batch'), scatter_dimension=0, tiled=True)  20.9 us
    ppermute x1, waiting for transfers between devices, on_device(): got_half = lax.ppermute(sent, 'pair', [(0, 1), (1, 0)])  11.9 us
    pallas_call x1, Pallas kernels, vocab_gather(): pl.pallas_call(functools.partial(gather_kernel, nv), out_shape=jax.ShapeD...  10.8 us
    dot_general x1, matrix products, on_device(): kept = jnp.dot(mine, w, preferred_element_type=jnp.float32)  10.4 us
    dot_general x1, matrix products, on_device(): sent = jnp.dot(theirs, w, preferred_element_type=jnp.float32)  9.08 us
  transfers between devices with their start and end apart: 3, of which 3 were waited for; matrix products, arithmetic and copies ran while one was open for 5% of the time, Pallas kernels for 0%

profile of v19, /device:TPU:0, one launch (start us, length us, event | category | flops | bytes accessed | tf_op | source)
XLA Modules:
  0.0 243.6 jit_solution(16787383569995062495)
XLA Ops:
  7.2 1.3 scatter.6.g_ref
  8.5 40.9 %shard_map.50 = (bf16[16,128,512]{2,1,0:T(8,128)(2,1)}, bf16[16,16,128]{2,1,0:T(8,128)(2,1)}) custom-call(bf16[128,512]{1,0:T(8,128)(2,1)} %bitcast.27, bf16[16,128]{1,0:T(8,128)(2,1)} %scatter.6.g_ref), custom_call_target="tpu_custom_call" | custom-call | bytes 4325376 | tf_op jit(solution)/shard_map/pallas_call | solution.py:193
  49.4 2.1 fusion.7
  51.5 2.2 convert_bitcast_fusion
  53.7 0.8 slice.70
  54.5 0.5 copy.10
  55.0 1.8 multiply_convert_fusion.src_ref
  56.8 31.2 %shard_map.51 = bf16[4,2,2,64,1024]{4,3,2,1,0:T(8,128)(2,1)} custom-call(bf16[128,8192]{1,0:T(8,128)(2,1)} %multiply_convert_fusion.src_ref), custom_call_target="tpu_custom_call" | custom-call | bytes 4194304 | tf_op jit(solution)/shard_map/pallas_call | solution.py:266
  88.0 4.6 %fusion.9 = f32[1024,512]{1,0:T(8,128)} fusion(bf16[1024,1024]{1,0:T(8,128)(2,1)} %bitcast.25, bf16[1024,4096]{1,0:T(8,128)(2,1)} %param.9), kind=kOutput, calls=%fused_computation.13 | convolution fusion | flops 1073741824 | bytes 5242880 | tf_op jit(solution)/shard_map/dot_general | solution.py:306
  92.6 0.2 constant_dynamic-slice_fusion
  92.7 9.1 %fusion = f32[512,3584]{1,0:T(8,128)} fusion(bf16[512,1024]{1,0:T(8,128)(2,1)S(1)} %get-tuple-element.38, bf16[1024,4096]{1,0:T(8,128)(2,1)} %param.9), kind=kOutput, calls=%fused_computation | convolution fusion | flops 3758096384 | bytes 15728640 | tf_op jit(solution)/shard_map/dot_general | solution.py:310
  101.8 0.0 reduce-scatter.5.cloned.1.call-start
  101.9 11.9 %collective-permute-done = f32[512,3584]{1,0:T(8,128)} collective-permute-done((f32[512,3584]{1,0:T(8,128)}, f32[512,3584]{1,0:T(8,128)}, u32[]{:S(2)}, u32[]{:S(2)}) %collective-permute-start) | collective-permute-done | bytes 7340064 | tf_op jit(solution)/shard_map/ppermute | solution.py:312
  113.8 10.4 %fusion.4 = f32[512,3584]{1,0:T(8,128)} fusion(f32[512,3584]{1,0:T(8,128)} %collective-permute-done, bf16[512,1024]{1,0:T(8,128)(2,1)S(1)} %get-tuple-element.36, bf16[1024,4096]{1,0:T(8,128)(2,1)} %param.9), kind=kOutput, calls=%fused_computation.4 | convolution fusion | flops 3759931392 | bytes 23068672 | tf_op jit(solution)/shard_map/dot_general | solution.py:311
  124.2 20.9 %reduce-scatter.3.cloned.1.call-done = f32[128,512]{1,0:T(8,128)} async-done(((f32[1024,512]{1,0:T(8,128)}), f32[128,512]{1,0:T(8,128)}) %reduce-scatter.3.cloned.1.call-update) | async-done | bytes 262160 | tf_op jit(solution)/shard_map/reduce_scatter | solution.py:308
  145.1 1.0 constant_dynamic-update-slice_fusion.1
  146.1 74.1 %reduce-scatter.5.cloned.1.call-done = f32[128,3584]{1,0:T(8,128)} async-done(((f32[512,3584]{1,0:T(8,128)}), f32[128,3584]{1,0:T(8,128)}) %reduce-scatter.5.cloned.1.call-update) | async-done | bytes 1835024 | tf_op jit(solution)/shard_map/reduce_scatter | solution.py:315
  220.2 1.6 constant_dynamic-update-slice_fusion
  221.8 0.3 slice_reduce_fusion
  222.1 0.5 exponential_reduce_fusion.1
  222.7 0.6 select_maximum_fusion.src_ref
  223.3 10.8 %shard_map.52 = f32[16,8,128]{2,1,0:T(8,128)} custom-call(f32[8,128]{1,0:T(8,128)} %select_maximum_fusion.src_ref), custom_call_target="tpu_custom_call" | custom-call | bytes 131072 | tf_op jit(solution)/shard_map/pallas_call | solution.py:143
  234.1 1.0 fusion.12
  235.2 1.6 slice_subtract_fusion
  (13 shorter events, 0.2 us)
Async XLA Ops:
  7.2 137.9 %reduce-scatter.3.cloned.1.call-start = ((), (), s32[]{:S(2)}) async-start(), calls=%async_computation.2 | async-start | bytes 2359296 | tf_op jit(solution)/shard_map/reduce_scatter | solution.py:308
  88.0 4.6 %copy-start = (bf16[4,2,2,64,1024]{4,3,2,1,0:T(8,128)(2,1)S(1)}, bf16[4,2,2,64,1024]{4,3,2,1,0:T(8,128)(2,1)}, u32[]{:S(2)}) copy-start(bf16[4,2,2,64,1024]{4,3,2,1,0:T(8,128)(2,1)} %shard_map.51) | copy-start | bytes 6291460
  101.8 12.0 %collective-permute-start = (f32[512,3584]{1,0:T(8,128)}, f32[512,3584]{1,0:T(8,128)}, u32[]{:S(2)}, u32[]{:S(2)}) collective-permute-start(f32[512,3584]{1,0:T(8,128)} %fusion), channel_id=1, source_target_pairs={{0,64},{64,0},{1,65},{65,1},{2,66},{66,2},{3,67},{67,3},{4,68},{68... | collective-permute-start | bytes 22020104 | tf_op jit(solution)/shard_map/ppermute | solution.py:312
  101.8 118.4 %reduce-scatter.5.cloned.1.call-start = ((), (), s32[]{:S(2)}) async-start(), calls=%async_computation.3 | async-start | bytes 9175040 | tf_op jit(solution)/shard_map/reduce_scatter | solution.py:315
Sparse Core Ops, SparseCore 0:
  102.0 43.0 reduce-scatter.2
  147.5 72.6 reduce-scatter.4

commit v20 on v17

--- a/solution.py
+++ b/solution.py
@@ -11,6 +11,10 @@
 
 EPS = 1e-05
 GUIDE = 1.5
+
+
+def STEPS(nv):
+    return [(i + 1) // 2 if i % 2 else nv - i // 2 for i in range(1, nv)]
 
 
 def dispatch_kernel(npair, nb, nv, span, src_ref, out_ref, send_sems, recv_sems):
@@ -112,7 +116,7 @@
     b = lax.axis_index("batch")
     v = lax.axis_index("vocab")
     barrier = pltpu.get_barrier_semaphore()
-    for k in range(1, nv):
+    for k in STEPS(nv):
         pl.semaphore_signal(barrier, inc=1, device_id=(beta, b, (v + k) % nv), device_id_type=MESH)
     pl.semaphore_wait(barrier, nv - 1)
 
@@ -126,13 +130,13 @@
             device_id_type=MESH,
         )
 
-    for k in range(1, nv):
+    for k in STEPS(nv):
         remote((v + k) % nv, v).start()
 
     pltpu.make_async_copy(src_ref, out_ref.at[v], recv_sems.at[v]).start()
-    for k in range(1, nv):
+    for k in STEPS(nv):
         remote((v + k) % nv, v).wait_send()
-    for k in range(1, nv):
+    for k in STEPS(nv):
         s = (v + k) % nv
         remote(s, s).wait_recv()
     pltpu.make_async_copy(src_ref, out_ref.at[v], recv_sems.at[v]).wait()
@@ -156,7 +160,7 @@
     b = lax.axis_index("batch")
     v = lax.axis_index("vocab")
     barrier = pltpu.get_barrier_semaphore()
-    for k in range(1, nv):
+    for k in STEPS(nv):
         pl.semaphore_signal(barrier, inc=1, device_id=(beta, b, (v + k) % nv), device_id_type=MESH)
     pl.semaphore_wait(barrier, nv - 1)
 
@@ -171,15 +175,15 @@
         )
 
     pairs = ((h_ref, ho_ref, hs, hr), (g_ref, go_ref, gs, gr))
-    for k in range(1, nv):
+    for k in STEPS(nv):
         for src, dst, send, recv in pairs:
             remote(src, dst, send, recv, (v + k) % nv, v).start()
     for src, dst, send, recv in pairs:
         pltpu.make_async_copy(src, dst.at[v], recv.at[v]).start()
-    for k in range(1, nv):
+    for k in STEPS(nv):
         for src, dst, send, recv in pairs:
             remote(src, dst, send, recv, (v + k) % nv, v).wait_send()
-    for k in range(1, nv):
+    for k in STEPS(nv):
         s = (v + k) % nv
         for src, dst, send, recv in pairs:
             remote(src, dst, send, recv, s, s).wait_recv()

time: 234 us -> 225 us (0.962)
  waiting for transfers between devices: 95.5 us -> 87.4 us
    reduce_scatter x2, waiting for transfers between devices: 81 us -> 73 us  [on_device(): lax.psum_scatter(summed, 'batch', scatter_dimension=0, tiled=True)]
  transfers between devices with their start and end apart: 4 -> 4, of which waited for: 4 -> 3; matrix products, arithmetic and copies ran while one was open for 5% -> 5% of each run, Pallas kernels for 0% -> 0%
where the time goes in v20:
time: 225 us; the launch traced here: 224 us
  waiting for transfers between devices  87.4 us (39%)
  Pallas kernels  82 us (36%)
  matrix products  24.4 us (11%)
  between operations  14.2 us (6%)
  local copies, waits for them, and re-layouts  8.02 us (4%)
  other arithmetic  7.79 us (3%)
    reduce_scatter x2, waiting for transfers between devices, on_device(): lax.psum_scatter(summed, 'batch', scatter_dimension=0, tiled=True)  73 us
    pallas_call x1, Pallas kernels, vocab_gather_pair(): pl.pallas_call(functools.partial(gather_pair_kernel, nv), out_shape=(jax....  40.1 us
    pallas_call x1, Pallas kernels, kblock_scatter(): pl.pallas_call(functools.partial(scatter_kernel, npair, nb), out_shape=ja...  31.1 us
    ppermute x2, waiting for transfers between devices, on_device(): got_half = lax.ppermute(sent, 'pair', [(0, 1), (1, 0)])  14.4 us
    dot_general x2, matrix products, on_device(): kept = jnp.dot(mine, w, preferred_element_type=jnp.float32)  13.3 us
    dot_general x2, matrix products, on_device(): sent = jnp.dot(theirs, w, preferred_element_type=jnp.float32)  11.1 us
    pallas_call x1, Pallas kernels, vocab_gather(): pl.pallas_call(functools.partial(gather_kernel, nv), out_shape=jax.ShapeD...  10.8 us
  transfers between devices with their start and end apart: 4, of which 3 were waited for; matrix products, arithmetic and copies ran while one was open for 5% of the time, Pallas kernels for 0%

profile of v20, /device:TPU:0, one launch (start us, length us, event | category | flops | bytes accessed | tf_op | source)
XLA Modules:
  0.0 224.1 jit_solution(6446953736735901596)
XLA Ops:
  7.2 1.3 scatter.6.g_ref
  8.5 40.1 %shard_map.50 = (bf16[16,128,512]{2,1,0:T(8,128)(2,1)}, bf16[16,16,128]{2,1,0:T(8,128)(2,1)}) custom-call(bf16[128,512]{1,0:T(8,128)(2,1)} %bitcast.27, bf16[16,128]{1,0:T(8,128)(2,1)} %scatter.6.g_ref), custom_call_target="tpu_custom_call" | custom-call | bytes 4325376 | tf_op jit(solution)/shard_map/pallas_call | solution.py:197
  48.6 2.3 %convert_bitcast_fusion = f32[16,16,8,512]{3,2,1,0:T(8,128)S(1)} fusion(bf16[16,128,512]{2,1,0:T(8,128)(2,1)} %get-tuple-element.33), kind=kLoop, calls=%fused_computation.6 | loop fusion | flops 1048576 | bytes 6291456
  50.9 0.5 fusion.7
  51.4 0.6 copy.10
  52.0 0.8 slice.70
  52.8 1.9 multiply_convert_fusion.src_ref
  54.7 31.1 %shard_map.51 = bf16[4,2,2,64,1024]{4,3,2,1,0:T(8,128)(2,1)} custom-call(bf16[128,8192]{1,0:T(8,128)(2,1)} %multiply_convert_fusion.src_ref), custom_call_target="tpu_custom_call" | custom-call | bytes 4194304 | tf_op jit(solution)/shard_map/pallas_call | solution.py:270
  85.8 1.7 constant_dynamic-slice_fusion.1
  87.5 1.9 fusion.9
  89.6 2.6 %collective-permute-done = f32[512,512]{1,0:T(8,128)S(1)} collective-permute-done((f32[512,512]{1,0:T(8,128)S(1)}, f32[512,512]{1,0:T(8,128)S(1)}, u32[]{:S(2)}, u32[]{:S(2)}) %collective-permute-start) | collective-permute-done | bytes 1048608 | tf_op jit(solution)/shard_map/ppermute | solution.py:311
  92.2 2.9 %convolution_add_fusion = f32[512,512]{1,0:T(8,128)} fusion(f32[512,512]{1,0:T(8,128)S(1)} %collective-permute-done, bf16[512,1024]{1,0:T(8,128)(2,1)S(1)} %get-tuple-element.36, bf16[1024,4096]{1,0:T(8,128)(2,1)} %param.9), kind=kOutput, calls=%fused_computation.9 | convolution fusion | flops 537133056 | bytes 4194304 | tf_op jit(solution)/shard_map/dot_general | solution.py:310
  95.1 9.1 %fusion = f32[512,3584]{1,0:T(8,128)} fusion(bf16[512,1024]{1,0:T(8,128)(2,1)S(1)} %get-tuple-element.38, bf16[1024,4096]{1,0:T(8,128)(2,1)} %param.9), kind=kOutput, calls=%fused_computation | convolution fusion | flops 3758096384 | bytes 15728640 | tf_op jit(solution)/shard_map/dot_general | solution.py:309
  104.5 11.8 %collective-permute-done.1 = f32[512,3584]{1,0:T(8,128)} collective-permute-done((f32[512,3584]{1,0:T(8,128)}, f32[512,3584]{1,0:T(8,128)}, u32[]{:S(2)}, u32[]{:S(2)}) %collective-permute-start.1) | collective-permute-done | bytes 7340064 | tf_op jit(solution)/shard_map/ppermute | solution.py:311
  116.3 10.4 %fusion.4 = f32[512,3584]{1,0:T(8,128)} fusion(f32[512,3584]{1,0:T(8,128)} %collective-permute-done.1, bf16[512,1024]{1,0:T(8,128)(2,1)S(1)} %get-tuple-element.36, bf16[1024,4096]{1,0:T(8,128)(2,1)} %param.9), kind=kOutput, calls=%fused_computation.4 | convolution fusion | flops 3759931392 | bytes 23068672 | tf_op jit(solution)/shard_map/dot_general | solution.py:310
  126.7 1.0 constant_dynamic-update-slice_fusion.1
  127.7 73.0 %reduce-scatter.5.cloned.1.call-done = f32[128,3584]{1,0:T(8,128)} async-done(((f32[512,3584]{1,0:T(8,128)}), f32[128,3584]{1,0:T(8,128)}) %reduce-scatter.5.cloned.1.call-update) | async-done | bytes 1835024 | tf_op jit(solution)/shard_map/reduce_scatter | solution.py:314
  200.6 1.6 constant_dynamic-update-slice_fusion
  202.3 0.3 slice_reduce_fusion
  202.5 0.5 exponential_reduce_fusion.1
  203.1 0.6 select_maximum_fusion.src_ref
  203.7 10.8 %shard_map.52 = f32[16,8,128]{2,1,0:T(8,128)} custom-call(f32[8,128]{1,0:T(8,128)} %select_maximum_fusion.src_ref), custom_call_target="tpu_custom_call" | custom-call | bytes 131072 | tf_op jit(solution)/shard_map/pallas_call | solution.py:147
  214.5 1.0 fusion.13
  215.6 1.6 slice_subtract_fusion
  (16 shorter events, 0.5 us)
Async XLA Ops:
  7.2 119.5 %reduce-scatter.3.cloned.1.call-start = ((), (), s32[]{:S(2)}) async-start(), calls=%async_computation.2 | async-start | bytes 1310720 | tf_op jit(solution)/shard_map/reduce_scatter | solution.py:314
  48.6 2.3 %copy-start = (bf16[16,128,512]{2,1,0:T(8,128)(2,1)S(1)}, bf16[16,128,512]{2,1,0:T(8,128)(2,1)}, u32[]{:S(2)}) copy-start(bf16[16,128,512]{2,1,0:T(8,128)(2,1)} %get-tuple-element.33) | copy-start | bytes 6291460
  89.5 2.7 %collective-permute-start = (f32[512,512]{1,0:T(8,128)S(1)}, f32[512,512]{1,0:T(8,128)S(1)}, u32[]{:S(2)}, u32[]{:S(2)}) collective-permute-start(f32[512,512]{1,0:T(8,128)S(1)} %fusion.9), channel_id=1, source_target_pairs={{0,64},{64,0},{1,65},{65,1},{2,66},{66,2},{3,67},{67,3},{4,68},{68... | collective-permute-start | bytes 3145736 | tf_op jit(solution)/shard_map/ppermute | solution.py:311
  104.3 12.0 %collective-permute-start.1 = (f32[512,3584]{1,0:T(8,128)}, f32[512,3584]{1,0:T(8,128)}, u32[]{:S(2)}, u32[]{:S(2)}) collective-permute-start(f32[512,3584]{1,0:T(8,128)} %fusion), channel_id=1, source_target_pairs={{0,64},{64,0},{1,65},{65,1},{2,66},{66,2},{3,67},{67,3},{4,68},{68... | collective-permute-start | bytes 22020104 | tf_op jit(solution)/shard_map/ppermute | solution.py:311
  104.4 96.2 %reduce-scatter.5.cloned.1.call-start = ((), (), s32[]{:S(2)}) async-start(), calls=%async_computation.3 | async-start | bytes 9175040 | tf_op jit(solution)/shard_map/reduce_scatter | solution.py:314
Sparse Core Ops, SparseCore 0:
  104.5 21.1 reduce-scatter.2
  128.2 72.3 reduce-scatter.4

commit v21 on v20

--- a/solution.py
+++ b/solution.py
@@ -215,7 +215,7 @@
     rows = out_ref.shape[3]
     depth = out_ref.shape[4]
     barrier = pltpu.get_barrier_semaphore()
-    for k in range(1, groups):
+    for k in STEPS(groups):
         t = (me + k) % groups
         pl.semaphore_signal(barrier, inc=1, device_id=(t // nb, t % nb, v), device_id_type=MESH)
     pl.semaphore_wait(barrier, groups - 1)
@@ -238,15 +238,15 @@
         return pltpu.make_async_copy(
             piece(me, h), out_ref.at[b, h, beta], recv_sems.at[(b * 2 + h) * npair + beta])
 
-    for k in range(1, groups):
+    for k in STEPS(groups):
         for h in range(2):
             remote(k, h).start()
     for h in range(2):
         local(h).start()
-    for k in range(1, groups):
+    for k in STEPS(groups):
         for h in range(2):
             remote(k, h).wait_send()
-    for k in range(1, groups):
+    for k in STEPS(groups):
         s = (me + k) % groups
         sp, sb = s // nb, s % nb
         for h in range(2):

time: 225 us -> 224 us (level)
  no operation moved by 1% of the time
where the time goes in v21:
time: 224 us
  waiting for transfers between devices  87.6 us (39%)
  Pallas kernels  81.7 us (36%)
  matrix products  24.3 us (11%)
  between operations  14.2 us (6%)
  local copies, waits for them, and re-layouts  8.02 us (4%)
  other arithmetic  7.79 us (3%)
    reduce_scatter x2, waiting for transfers between devices, on_device(): lax.psum_scatter(summed, 'batch', scatter_dimension=0, tiled=True)  73.1 us
    pallas_call x1, Pallas kernels, vocab_gather_pair(): pl.pallas_call(functools.partial(gather_pair_kernel, nv), out_shape=(jax....  40.1 us
    pallas_call x1, Pallas kernels, kblock_scatter(): pl.pallas_call(functools.partial(scatter_kernel, npair, nb), out_shape=ja...  30.9 us
    ppermute x2, waiting for transfers between devices, on_device(): got_half = lax.ppermute(sent, 'pair', [(0, 1), (1, 0)])  14.4 us
    dot_general x2, matrix products, on_device(): kept = jnp.dot(mine, w, preferred_element_type=jnp.float32)  13.3 us
    dot_general x2, matrix products, on_device(): sent = jnp.dot(theirs, w, preferred_element_type=jnp.float32)  11.1 us
    pallas_call x1, Pallas kernels, vocab_gather(): pl.pallas_call(functools.partial(gather_kernel, nv), out_shape=jax.ShapeD...  10.8 us
  transfers between devices with their start and end apart: 4, of which 3 were waited for; matrix products, arithmetic and copies ran while one was open for 5% of the time, Pallas kernels for 0%

profile of v21, /device:TPU:0, one launch (start us, length us, event | category | flops | bytes accessed | tf_op | source)
XLA Modules:
  0.0 223.9 jit_solution(5314735001697237463)
XLA Ops:
  7.2 1.3 scatter.6.g_ref
  8.5 40.1 %shard_map.50 = (bf16[16,128,512]{2,1,0:T(8,128)(2,1)}, bf16[16,16,128]{2,1,0:T(8,128)(2,1)}) custom-call(bf16[128,512]{1,0:T(8,128)(2,1)} %bitcast.27, bf16[16,128]{1,0:T(8,128)(2,1)} %scatter.6.g_ref), custom_call_target="tpu_custom_call" | custom-call | bytes 4325376 | tf_op jit(solution)/shard_map/pallas_call | solution.py:197
  48.6 2.3 %convert_bitcast_fusion = f32[16,16,8,512]{3,2,1,0:T(8,128)S(1)} fusion(bf16[16,128,512]{2,1,0:T(8,128)(2,1)} %get-tuple-element.33), kind=kLoop, calls=%fused_computation.6 | loop fusion | flops 1048576 | bytes 6291456
  50.9 0.5 fusion.7
  51.4 0.6 copy.10
  52.0 0.8 slice.70
  52.8 1.9 multiply_convert_fusion.src_ref
  54.7 30.9 %shard_map.51 = bf16[4,2,2,64,1024]{4,3,2,1,0:T(8,128)(2,1)} custom-call(bf16[128,8192]{1,0:T(8,128)(2,1)} %multiply_convert_fusion.src_ref), custom_call_target="tpu_custom_call" | custom-call | bytes 4194304 | tf_op jit(solution)/shard_map/pallas_call | solution.py:270
  85.6 1.7 constant_dynamic-slice_fusion.1
  87.3 1.9 fusion.9
  89.3 2.6 %collective-permute-done = f32[512,512]{1,0:T(8,128)S(1)} collective-permute-done((f32[512,512]{1,0:T(8,128)S(1)}, f32[512,512]{1,0:T(8,128)S(1)}, u32[]{:S(2)}, u32[]{:S(2)}) %collective-permute-start) | collective-permute-done | bytes 1048608 | tf_op jit(solution)/shard_map/ppermute | solution.py:311
  92.0 2.9 %convolution_add_fusion = f32[512,512]{1,0:T(8,128)} fusion(f32[512,512]{1,0:T(8,128)S(1)} %collective-permute-done, bf16[512,1024]{1,0:T(8,128)(2,1)S(1)} %get-tuple-element.36, bf16[1024,4096]{1,0:T(8,128)(2,1)} %param.9), kind=kOutput, calls=%fused_computation.9 | convolution fusion | flops 537133056 | bytes 4194304 | tf_op jit(solution)/shard_map/dot_general | solution.py:310
  94.9 9.1 %fusion = f32[512,3584]{1,0:T(8,128)} fusion(bf16[512,1024]{1,0:T(8,128)(2,1)S(1)} %get-tuple-element.38, bf16[1024,4096]{1,0:T(8,128)(2,1)} %param.9), kind=kOutput, calls=%fused_computation | convolution fusion | flops 3758096384 | bytes 15728640 | tf_op jit(solution)/shard_map/dot_general | solution.py:309
  104.2 11.8 %collective-permute-done.1 = f32[512,3584]{1,0:T(8,128)} collective-permute-done((f32[512,3584]{1,0:T(8,128)}, f32[512,3584]{1,0:T(8,128)}, u32[]{:S(2)}, u32[]{:S(2)}) %collective-permute-start.1) | collective-permute-done | bytes 7340064 | tf_op jit(solution)/shard_map/ppermute | solution.py:311
  116.0 10.4 %fusion.4 = f32[512,3584]{1,0:T(8,128)} fusion(f32[512,3584]{1,0:T(8,128)} %collective-permute-done.1, bf16[512,1024]{1,0:T(8,128)(2,1)S(1)} %get-tuple-element.36, bf16[1024,4096]{1,0:T(8,128)(2,1)} %param.9), kind=kOutput, calls=%fused_computation.4 | convolution fusion | flops 3759931392 | bytes 23068672 | tf_op jit(solution)/shard_map/dot_general | solution.py:310
  126.4 1.0 constant_dynamic-update-slice_fusion.1
  127.4 73.1 %reduce-scatter.5.cloned.1.call-done = f32[128,3584]{1,0:T(8,128)} async-done(((f32[512,3584]{1,0:T(8,128)}), f32[128,3584]{1,0:T(8,128)}) %reduce-scatter.5.cloned.1.call-update) | async-done | bytes 1835024 | tf_op jit(solution)/shard_map/reduce_scatter | solution.py:314
  200.5 1.6 constant_dynamic-update-slice_fusion
  202.2 0.3 slice_reduce_fusion
  202.4 0.5 exponential_reduce_fusion.1
  203.0 0.6 select_maximum_fusion.src_ref
  203.6 10.8 %shard_map.52 = f32[16,8,128]{2,1,0:T(8,128)} custom-call(f32[8,128]{1,0:T(8,128)} %select_maximum_fusion.src_ref), custom_call_target="tpu_custom_call" | custom-call | bytes 131072 | tf_op jit(solution)/shard_map/pallas_call | solution.py:147
  214.4 1.0 fusion.13
  215.5 1.6 slice_subtract_fusion
  (16 shorter events, 0.5 us)
Async XLA Ops:
  7.2 119.3 %reduce-scatter.3.cloned.1.call-start = ((), (), s32[]{:S(2)}) async-start(), calls=%async_computation.2 | async-start | bytes 1310720 | tf_op jit(solution)/shard_map/reduce_scatter | solution.py:314
  48.6 2.3 %copy-start = (bf16[16,128,512]{2,1,0:T(8,128)(2,1)S(1)}, bf16[16,128,512]{2,1,0:T(8,128)(2,1)}, u32[]{:S(2)}) copy-start(bf16[16,128,512]{2,1,0:T(8,128)(2,1)} %get-tuple-element.33) | copy-start | bytes 6291460
  89.2 2.7 %collective-permute-start = (f32[512,512]{1,0:T(8,128)S(1)}, f32[512,512]{1,0:T(8,128)S(1)}, u32[]{:S(2)}, u32[]{:S(2)}) collective-permute-start(f32[512,512]{1,0:T(8,128)S(1)} %fusion.9), channel_id=1, source_target_pairs={{0,64},{64,0},{1,65},{65,1},{2,66},{66,2},{3,67},{67,3},{4,68},{68... | collective-permute-start | bytes 3145736 | tf_op jit(solution)/shard_map/ppermute | solution.py:311
  104.0 12.0 %collective-permute-start.1 = (f32[512,3584]{1,0:T(8,128)}, f32[512,3584]{1,0:T(8,128)}, u32[]{:S(2)}, u32[]{:S(2)}) collective-permute-start(f32[512,3584]{1,0:T(8,128)} %fusion), channel_id=1, source_target_pairs={{0,64},{64,0},{1,65},{65,1},{2,66},{66,2},{3,67},{67,3},{4,68},{68... | collective-permute-start | bytes 22020104 | tf_op jit(solution)/shard_map/ppermute | solution.py:311
  104.2 96.3 %reduce-scatter.5.cloned.1.call-start = ((), (), s32[]{:S(2)}) async-start(), calls=%async_computation.3 | async-start | bytes 9175040 | tf_op jit(solution)/shard_map/reduce_scatter | solution.py:314
Sparse Core Ops, SparseCore 0:
  104.3 21.3 reduce-scatter.2
  128.3 72.1 reduce-scatter.4
